TPU v7x, 256 devices: a whole 4x4x8 slice. The times are simulated.
256 devices in a mesh: wide: 32 (over z_hi, y, core), narrow: 8 (over z_lo, x).
Axes of the slice: x: 4, y: 4, z: 8 (z_hi: 4, z_lo: 2; z = z_hi * 2 + z_lo), core: 2. Of those that a mesh axis runs over, the one named last changes fastest.
Arguments:
- valence: float32 [8, 32768], P(None, ('wide', 'narrow')), may hold values from -6 to 6
- conduction: float32 [256, 32768], P(('wide', 'narrow')), may hold values from -6 to 6
- eps_val: float32 [8], replicated, may hold values from -12 to -2
- eps_cond: float32 [256], replicated, may hold values from 0.5 to 20
- omega: float32 [6], replicated, may hold values from 0.3 to 30
- gmap: int32 [8192], replicated, may hold values from 0 to 32767, as said below
Outputs:
- chi: float32 [6, 8192, 8192], P(None, 'wide', 'narrow')
Inputs may be any that keep to these rules, and one draw needn't show every extreme that they name: `gmap`: distinct grid indices: the 8192 grid points of smallest squared wave vector (frequencies folded to -16 .. 15), equal lengths in random order, listed by rising length.
All inputs are finite; a program needn't handle non-finite values.
Results may differ from a plain program's by a relative error of at most 0.0042.
Values may be sent and summed in bfloat16 or wider, within the bound.
No kernel may reach another device: no remote copies, remote signals or barrier semaphores. Data moves between devices by JAX's collectives and lax.ppermute only.
A program may use at most 128 MiB of HBM per device.

v0:
```python
import functools

import jax
import jax.numpy as jnp
import ml_dtypes
import numpy as np
from jax import lax
from jax.experimental import pallas as pl
from jax.experimental.pallas import tpu as pltpu
from jax.sharding import Mesh
from jax.sharding import PartitionSpec as P

GRID = 32
AXES = ("zh", "y", "co", "zl", "x")
WIDE = ("zh", "y", "co")
NARROW = ("zl", "x")
NPW = 8192
DISC = 256
NKX = 26
CAN = 640
BF = jnp.bfloat16
F32 = jnp.float32


def split_bf16(value):
    high = value.astype(BF)
    return high, (value - high.astype(value.dtype)).astype(BF)


def tables():
    k = np.arange(GRID)
    fold = np.where(k < GRID // 2, k, k - GRID)
    length = fold[:, None, None] ** 2 + fold[None, :, None] ** 2 + fold[None, None, :] ** 2
    ordered = np.sort(length.ravel())[:NPW]
    limit = ordered[-1]
    disc = []
    for ky in range(-15, 16):
        for kz in range(0, 16):
            if ky * ky + kz * kz <= limit and (kz > 0 or ky >= 0):
                disc.append((ky, kz))
    assert len(disc) <= DISC
    points = np.arange(GRID)
    wave = np.zeros((GRID, GRID, 2 * DISC))
    key = np.full((DISC, 1), -9000, np.int32)
    for m, (ky, kz) in enumerate(disc):
        angle = 2 * np.pi * ((ky * points[:, None] + kz * points[None, :]) % GRID) / GRID
        wave[:, :, m] = np.cos(angle)
        wave[:, :, DISC + m] = -np.sin(angle)
        key[m, 0] = ky * 64 + kz
    kx = np.arange(NKX) - 12
    assert limit < 13 * 13
    angle = 2 * np.pi * (kx[:, None] * points[None, :] % GRID) / GRID
    eye = np.eye(8)
    along = np.concatenate([np.kron(np.cos(angle), eye), np.kron(np.sin(angle), eye)])
    blocks = 8
    col_key = np.full((blocks, 1, CAN), -8000, np.int32)
    col_kx = np.zeros((blocks, 1, CAN), np.int32)
    col_id = np.full((blocks, 1, CAN), -(1 << 20), np.int32)
    size = NPW // blocks
    for j in range(blocks):
        low, high = ordered[j * size], ordered[(j + 1) * size - 1]
        n = 0
        for ky, kz in disc:
            for x in range(-12, 13):
                if (ky, kz) == (0, 0) and x < 0:
                    continue
                if low <= x * x + ky * ky + kz * kz <= high:
                    col_key[j, 0, n] = ky * 64 + kz
                    col_kx[j, 0, n] = x + 12
                    col_id[j, 0, n] = (x * 64 + ky) * 64 + kz
                    n += 1
        assert n <= CAN
    wave = wave.reshape(GRID * GRID, 2 * DISC).astype(np.float32)
    along = along.astype(np.float32)
    return split_np(wave) + split_np(along) + (key, col_key, col_kx, col_id)


def split_np(value):


    high = value.astype(ml_dtypes.bfloat16)
    low = (value - high.astype(np.float32)).astype(ml_dtypes.bfloat16)
    return high, low


def folded(index):
    def fold(k):
        return jnp.where(k < GRID // 2, k, k - GRID)

    return (
        fold(lax.shift_right_logical(index, 10)),
        fold(lax.shift_right_logical(index, 5) & 31),
        fold(index & 31),
    )


def dot(a, b):
    return jnp.dot(a, b, preferred_element_type=F32)


def fetch(sources, targets, sems):
    copies = [pltpu.make_async_copy(s, t, sems.at[i]) for i, (s, t) in enumerate(zip(sources, targets))]
    for copy in copies:
        copy.start()
    return copies


def picked(spectrum, count, key, wanted, kx, store):
    half = NKX * 8
    hot = jnp.where(key[...] == wanted, jnp.float32(1), jnp.float32(0)).astype(BF)
    found = dot(spectrum[: 2 * count * half, :], hot)
    masks = [jnp.broadcast_to(kx == i, (8, wanted.shape[1])) for i in range(NKX - 1)]
    for s in range(count):
        parts = []
        for part in range(2):
            base = (2 * s + part) * half
            value = found[base : base + 8]
            for i in range(1, NKX - 1):
                value = jnp.where(masks[i], found[base + i * 8 : base + i * 8 + 8], value)
            parts.append(value)
        store(s, *parts)


def waves(pos, own, other, bands, wave_hi, wave_lo, along_hi, along_lo, ready, a_hi, a_lo, spectrum, first):
    zh, y, co = pos[0], pos[1], pos[2]
    count = len(bands)

    def product(q, carry):
        szh = (zh - q // 4) & 3
        sy = (y - q % 4) & 3
        start = pl.multiple_of(q * 16, 16)
        rows_of = [band[pl.ds(start, 16), :] for band in bands]
        for n in range(8):
            mine = own[sy, szh, n]
            theirs = other[sy, szh, n]
            lower = jnp.where(co == 0, mine, theirs)
            upper = jnp.where(co == 0, theirs, mine)
            for s in range(count):
                pair = [lower * rows_of[s][n : n + 1, :], upper * rows_of[s][8 + n : 9 + n, :]]
                high, low = split_bf16(jnp.concatenate(pair, axis=0))
                at = pl.ds(pl.multiple_of(s * 256 + start, 16), 16)
                a_hi[at, n * 128 : (n + 1) * 128] = high
                a_lo[at, n * 128 : (n + 1) * 128] = low
        return carry

    lax.fori_loop(0, 16, product, 0)
    ready()
    field = dot(a_hi[...], wave_hi[...]) + (dot(a_lo[...], wave_hi[...]) + dot(a_hi[...], wave_lo[...]))
    half = NKX * 8
    norm = jnp.float32(1.0) / jnp.sqrt(jnp.float32(GRID**3))
    for s in range(count):
        f_hi, f_lo = split_bf16(field[s * 256 : s * 256 + 256])
        full = dot(along_hi[...], f_hi) + (dot(along_lo[...], f_hi) + dot(along_hi[...], f_lo))
        real = full[:half, :DISC] + full[half:, DISC:]
        imag = full[:half, DISC:] - full[half:, :DISC]
        at = 2 * (first + s) * half
        spectrum[at : at + half, :] = (real * norm).astype(BF)
        spectrum[at + half : at + 2 * half, :] = (imag * norm).astype(BF)


def row_kernel(pos, *refs):
    sources, rows, spectrum, targets = refs[:9], refs[9], refs[10], refs[11:20]
    a_hi, a_lo, sems = refs[20:]
    own, other, band, wave_hi, wave_lo, along_hi, along_lo, key, gmap = targets
    copies = fetch(sources, targets, sems)
    for copy in copies[:3]:
        copy.wait()

    def ready():
        for copy in copies[3:]:
            copy.wait()

    waves(pos, own, other, [band], wave_hi, wave_lo, along_hi, along_lo, ready, a_hi, a_lo, spectrum, 0)

    def row_blocks(r, carry):
        kx, ky, kz = folded(gmap[r])
        flip = jnp.where((kz < 0) | ((kz == 0) & (ky < 0)), -1, 1)
        sign = flip.astype(F32)

        def store(s, real, imag):
            both = jnp.concatenate([real, imag * sign], axis=0).astype(BF)
            for t in range(4):
                rows[4 * r + t] = both[:, t * 256 : (t + 1) * 256]

        picked(spectrum, 1, key, flip * (ky * 64 + kz), flip * kx + 12, store)
        return carry

    lax.fori_loop(0, 8, row_blocks, 0)


def column_kernel(pos, *refs):
    sources, cols, targets = refs[:13], refs[13], refs[14:27]
    spectrum, a_hi, a_lo, sems = refs[27:]
    first, own, other, band1, band2, band3, wave_hi, wave_lo, along_hi, along_lo, key, col_key, col_kx = targets
    zl, x = pos[3], pos[4]
    copies = fetch(sources, targets, sems)
    for copy in copies[:6]:
        copy.wait()

    def ready():
        for copy in copies[6:]:
            copy.wait()

    spectrum[: 2 * NKX * 8, :] = first[...]
    bands = [band1, band2, band3]
    waves(pos, own, other, bands, wave_hi, wave_lo, along_hi, along_lo, ready, a_hi, a_lo, spectrum, 1)

    def columns(part, carry):
        j = (zl ^ part) * 4 + x

        def store(s, real, imag):
            cols[part, (x - s) & 3] = jnp.concatenate([real, imag], axis=0).astype(BF)

        picked(spectrum, 4, key, col_key[j], col_kx[j], store)
        return carry

    lax.fori_loop(0, 2, columns, 0)


def whole(shape):
    return pl.BlockSpec(shape, lambda *_: (0,) * len(shape), pipeline_mode=pl.Buffered(1))


def resident():
    return pl.BlockSpec(memory_space=pltpu.VMEM)


def transform_call(kernel, pos, operands, outs, scratch, flops, name):
    return pl.pallas_call(
        kernel,
        grid_spec=pltpu.PrefetchScalarGridSpec(
            num_scalar_prefetch=1,
            grid=(1,),
            in_specs=[pl.BlockSpec(memory_space=pl.ANY)] * len(operands),
            out_specs=[whole(v.shape) for v in outs],
            scratch_shapes=[pltpu.VMEM(v.shape, v.dtype) for v in operands]
            + scratch
            + [pltpu.SemaphoreType.DMA((len(operands),))],
        ),
        out_shape=outs,
        compiler_params=pltpu.CompilerParams(vmem_limit_bytes=60 << 20),
        cost_estimate=pl.CostEstimate(flops=flops, transcendentals=0, bytes_accessed=6 * 2**20),
        name=name,
    )(pos, *operands)


def row_pairs(pos, own, other, band, gmap):
    consts = [jnp.asarray(t) for t in tables()[:5]]
    outs = [jax.ShapeDtypeStruct((32, 16, 256), BF), jax.ShapeDtypeStruct((2 * NKX * 8, DISC), BF)]
    scratch = [pltpu.VMEM((256, 1024), BF)] * 2
    operands = [own, other, band, *consts, gmap.reshape(8, 1, 1024)]
    return transform_call(row_kernel, pos, operands, outs, scratch, 4 * 10**9, "row_pairs")


def column_pairs(pos, first, own, other, bands):
    consts = [jnp.asarray(t) for t in tables()[:7]]
    outs = [jax.ShapeDtypeStruct((2, 4, 16, CAN), BF)]
    scratch = [pltpu.VMEM((8 * NKX * 8, DISC), BF)] + [pltpu.VMEM((768, 1024), BF)] * 2
    operands = [first, own, other, *bands, *consts]
    return transform_call(column_kernel, pos, operands, outs, scratch, 8 * 10**9, "column_pairs")[0]


def prepare_kernel(pos, omega, r0, r1, r2, r3, gap, gmap, ident, scaled, hot, sign, row_k):
    zh, co, zl, x = pos[0], pos[2], pos[3], pos[4]

    @pl.when(pl.program_id(0) == 0)
    def _():
        kx, ky, kz = folded(gmap[0])
        flip = jnp.where((kz < 0) | ((kz == 0) & ((ky < 0) | ((ky == 0) & (kx < 0)))), -1, 1)
        wanted = (flip * ((kx * 64 + ky) * 64 + kz)).astype(F32)
        names = jnp.broadcast_to(ident[0].astype(F32), (128, CAN)).T
        signs = jnp.concatenate([jnp.ones((8, 1024), F32), jnp.broadcast_to(flip.astype(F32), (8, 1024))], axis=0)
        for t in range(8):
            at = slice(t * 128, (t + 1) * 128)
            here = slice(t % 2 * 128, t % 2 * 128 + 128)
            hot[t // 2, :, here] = jnp.where(names == wanted[:, at], jnp.float32(1), jnp.float32(0)).astype(BF)
            sign[t // 2, :, here] = signs[:, at]

    for side in range(2):
        co_at = co if side == 0 else 1 - co
        energies = []
        for s in range(4):
            zh_at = (zh - s) & 3
            energies.append(gap[zh_at, 0, co_at])
            for sx, ref in enumerate((r0, r1, r2, r3)):
                for szl in range(2):
                    n = (zl ^ szl) * 4 + ((x - sx) & 3)
                    to = pl.multiple_of(side * 512 + s * 128 + n * 16, 16)
                    row_k[pl.ds(to, 16), :] = ref[szl, zh_at, 0, co_at]
        energy = jnp.concatenate(energies, axis=1)
        total = row_k[side * 512 : side * 512 + 512, :].astype(F32).T
        for w in range(6):
            weight = -2.0 * energy / (energy * energy + omega[w] * omega[w])
            weight = weight / jnp.sqrt(jnp.float32(2048))
            at = slice(side * 512, side * 512 + 512)
            scaled[pl.program_id(0), w * 256 : (w + 1) * 256, at] = (total * weight).astype(BF)


def prepare(pos, omega, rows, gap, gmap, ident):
    rows = [pltpu.with_memory_space_constraint(r, pltpu.HBM) for r in rows]
    gmap, ident = (pltpu.with_memory_space_constraint(v, pltpu.HBM) for v in (gmap.reshape(8, 1, 1024), ident))
    row_spec = pl.BlockSpec((2, 4, 1, 2, 16, 256), lambda s, pos, om: (0, 0, (pos[1] - s) & 3, 0, 0, 0))
    return pl.pallas_call(
        prepare_kernel,
        grid_spec=pltpu.PrefetchScalarGridSpec(
            num_scalar_prefetch=2,
            grid=(4,),
            in_specs=[row_spec] * 4
            + [
                pl.BlockSpec((4, 1, 2, 1, 128), lambda s, pos, om: (0, (pos[1] - s) & 3, 0, 0, 0)),
                pl.BlockSpec((1, 1, 1024), lambda s, pos, om: (pos[3] * 4 + pos[4], 0, 0)),
                pl.BlockSpec((1, 1, CAN), lambda s, pos, om: (pos[3] * 4 + pos[4], 0, 0)),
            ],
            out_specs=[resident(), resident(), resident()],
            scratch_shapes=[pltpu.VMEM((1024, 256), BF)],
        ),
        out_shape=[pltpu.VMEM((4, 1536, 1024), BF), pltpu.VMEM((4, CAN, 256), BF), pltpu.VMEM((4, 16, 256), F32)],
        compiler_params=pltpu.CompilerParams(vmem_limit_bytes=20 << 20),
        cost_estimate=pl.CostEstimate(flops=10**9, transcendentals=0, bytes_accessed=20 * 2**20),
        name="scaled_rows",
    )(pos, omega, *rows, gap, gmap, ident)


def product_step(sy, mine, theirs, scaled, hot, sign, total, last):
    def kernel(mine, theirs, scaled, hot, sign, *refs):
        out, cols = refs[-2:]
        add = None if total is None else refs[0]

        def quarter(n):
            for side, ref in enumerate((mine, theirs)):
                full = dot(ref[...].reshape(512, CAN), hot[n]).reshape(32, 16, 256) * sign[n][None]
                cols[n, side * 512 : side * 512 + 512, :] = full.reshape(512, 256).astype(BF)
            part = dot(scaled[sy], cols[n]).reshape(6, 256, 256)
            at = pl.ds(pl.multiple_of(n * 256, 256), 256)
            part = part if add is None else add[:, :, at] + part
            if last:
                out[...] = part
            else:
                out[:, :, at] = part

        if last:
            quarter(pl.program_id(0))
        else:
            pl.loop(0, 4)(quarter)

    operands = [mine, theirs, scaled, hot, sign] + ([] if total is None else [total])
    aliases = {} if total is None or last else {5: 0}
    return pl.pallas_call(
        kernel,
        grid=(4 if last else 1,),
        in_specs=[resident()] * len(operands),
        out_specs=pl.BlockSpec((6, 256, 256), lambda n: (0, 0, n)) if last else resident(),
        scratch_shapes=[pltpu.VMEM((4, 1024, 256), BF)],
        out_shape=(jax.ShapeDtypeStruct if last else pltpu.VMEM)((6, 256, 1024), F32),
        input_output_aliases=aliases,
        compiler_params=pltpu.CompilerParams(vmem_limit_bytes=20 << 20),
        cost_estimate=pl.CostEstimate(flops=46 * 10**8, transcendentals=0, bytes_accessed=10 * 2**20),
        name="response_product",
    )(*operands)


def shifted(value, axis, shift):
    size = lax.axis_size(axis)
    return lax.ppermute(value, axis, [(i, (i + shift) % size) for i in range(size)])


def around(value, axis):
    return [value] + [shifted(value, axis, s) for s in range(1, lax.axis_size(axis))]


def neighbours(value, axis):
    return shifted(value, axis, 1), shifted(value, axis, 3)


def opposite(behind, ahead, axis):
    half = behind.shape[0] // 2
    return shifted(ahead[:half], axis, 3), shifted(behind[half:], axis, 1)


def body(valence, conduction, eps_val, eps_cond, omega, gmap):
    pos = jnp.stack([lax.axis_index(a) for a in AXES]).astype(jnp.int32)
    bands = around(conduction.reshape(256, 128), "x")
    own = lax.all_to_all(jnp.broadcast_to(valence, (8, *valence.shape)), NARROW, 0, 0, tiled=True)
    own, bands = lax.optimization_barrier((own, bands))
    own = jnp.stack(around(own, "zh"))
    gap = jnp.broadcast_to((eps_cond[:, None] - eps_val)[:, None, :], (256, 2, 8)).reshape(4, 4, 2, 1, 128)
    own, gap = lax.optimization_barrier((own, gap))
    own = jnp.stack(around(own, "y"))
    other = shifted(own, "co", 1)

    rows, spectrum = row_pairs(pos, own, other, bands[0], gmap)
    rows = lax.all_to_all(rows, WIDE, 0, 0, tiled=True)
    cols = column_pairs(pos, spectrum, own, other, bands[1:])
    kept, got = cols[0], shifted(cols[1], "zl", 1)
    lower = lax.axis_index("zl") == 0
    cols = jnp.concatenate([jnp.where(lower, kept, got), jnp.where(lower, got, kept)])
    rows = jnp.stack(around(rows, "zl")).reshape(2, 4, 4, 2, 16, 256)
    rows, cols = lax.optimization_barrier((rows, cols))
    near_x = neighbours(rows, "x")
    near_zh = neighbours(cols, "zh")
    near_x, near_zh = lax.optimization_barrier((near_x, near_zh))
    rows = [rows, near_x[0], jnp.concatenate(opposite(*near_x, "x")), near_x[1]]
    cols = jnp.stack([cols, near_zh[0], jnp.concatenate(opposite(*near_zh, "zh")), near_zh[1]])
    near_y = neighbours(cols, "y")
    scaled, hot, sign = prepare(pos, omega, rows, gap, gmap, jnp.asarray(tables()[-1]))
    total = product_step(0, cols, shifted(cols, "co", 1), scaled, hot, sign, None, False)
    total, near_y = lax.optimization_barrier((total, near_y))
    far = opposite(*near_y, "y")
    total = product_step(1, near_y[0], shifted(near_y[0], "co", 1), scaled, hot, sign, total, False)
    total, far = lax.optimization_barrier((total, far))
    for sy, mine in ((3, near_y[1]), (2, jnp.concatenate(far))):
        theirs = shifted(mine, "co", 1)
        total = product_step(sy, mine, theirs, scaled, hot, sign, total, sy == 2)
    return total


def solution(mesh):
    torus = Mesh(mesh.devices.reshape(4, 4, 2, 2, 4), AXES)
    return jax.shard_map(
        body,
        mesh=torus,
        in_specs=(P(None, AXES), P(AXES, None), P(), P(), P(), P()),
        out_specs=P(None, WIDE, NARROW),
        check_vma=False,
    )
```

profile of v0, /device:TPU:1, one launch (start us, length us, event | category | flops | bytes accessed | tf_op | source)
XLA Modules:
  0.0 158.4 jit_solution(1813658154111372625)
XLA Ops:
  0.0 2.0 %collective-permute-start = (f32[256,128]{1,0:T(8,128)}, f32[256,128]{1,0:T(8,128)S(1)}, u32[]{:S(2)}, u32[]{:S(2)}) collective-permute-start(f32[256,128]{1,0:T(8,128)} %bitcast.45), channel_id=1, source_target_pairs={{0,1},{1,2},{2,3},{3,0},{4,5},{5,6},{6,7},{7,4},{8,9},{9,10},{10,1... | collective-permute-start | bytes 393224 | tf_op jit(solution)/shard_map/ppermute | solution.py:364
  2.0 2.5 %collective-permute-start.1 = (f32[256,128]{1,0:T(8,128)}, f32[256,128]{1,0:T(8,128)S(1)}, u32[]{:S(2)}, u32[]{:S(2)}) collective-permute-start(f32[256,128]{1,0:T(8,128)} %bitcast.46), channel_id=1, source_target_pairs={{0,2},{1,3},{2,0},{3,1},{4,6},{5,7},{6,4},{7,5},{8,10},{9,11},{10,... | collective-permute-start | bytes 393224 | tf_op jit(solution)/shard_map/ppermute | solution.py:364
  4.5 1.2 collective-permute-start.2
  6.3 7.8 %all_to_all.10 = f32[8,8,128]{2,1,0:T(8,128)S(1)} all-to-all(f32[8,8,128]{2,1,0:T(8,128)S(1)} %broadcast_in_dim.4), channel_id=1, replica_groups=mesh['zh'=4,'y'=4,'co'=2,'zl'=2,'x'=4] {'zl','x'}, dimensions={0} | all-to-all | bytes 65536 | tf_op jit(solution)/shard_map/all_to_all | solution.py:383
  14.2 3.1 %collective-permute-start.3 = (f32[8,8,128]{2,1,0:T(8,128)S(1)}, f32[8,8,128]{2,1,0:T(8,128)S(1)}, u32[]{:S(2)}, u32[]{:S(2)}) collective-permute-start(f32[8,8,128]{2,1,0:T(8,128)S(1)} %all_to_all.10), channel_id=1, source_target_pairs={{0,64},{64,128},{128,192},{192,0},{1,65},{65,129},{129,193},{193,1... | collective-permute-start | bytes 98312 | tf_op jit(solution)/shard_map/ppermute | solution.py:364
  17.3 4.7 %collective-permute-start.4 = (f32[8,8,128]{2,1,0:T(8,128)S(1)}, f32[8,8,128]{2,1,0:T(8,128)S(1)}, u32[]{:S(2)}, u32[]{:S(2)}) collective-permute-start(f32[8,8,128]{2,1,0:T(8,128)S(1)} %all_to_all.10), channel_id=1, source_target_pairs={{0,128},{64,192},{128,0},{192,64},{1,129},{65,193},{129,1},{193,65... | collective-permute-start | bytes 98312 | tf_op jit(solution)/shard_map/ppermute | solution.py:364
  22.0 2.4 %collective-permute-start.5 = (f32[8,8,128]{2,1,0:T(8,128)S(1)}, f32[8,8,128]{2,1,0:T(8,128)S(1)}, u32[]{:S(2)}, u32[]{:S(2)}) collective-permute-start(f32[8,8,128]{2,1,0:T(8,128)S(1)} %all_to_all.10), channel_id=1, source_target_pairs={{0,192},{64,0},{128,64},{192,128},{1,193},{65,1},{129,65},{193,129... | collective-permute-start | bytes 98312 | tf_op jit(solution)/shard_map/ppermute | solution.py:364
  24.4 0.8 broadcast_subtract_fusion
  26.2 1.4 collective-permute-start.6
  27.5 2.6 %collective-permute-start.7 = (f32[4,8,8,128]{3,2,1,0:T(8,128)S(1)}, f32[4,8,8,128]{3,2,1,0:T(8,128)S(1)}, u32[]{:S(2)}, u32[]{:S(2)}) collective-permute-start(f32[4,8,8,128]{3,2,1,0:T(8,128)S(1)} %pad_maximum_fusion.5), channel_id=1, source_target_pairs={{0,32},{16,48},{32,0},{48,16},{1,33},{17,49},{33,1},{49,17},{2,34}... | collective-permute-start | bytes 393224 | tf_op jit(solution)/shard_map/ppermute | solution.py:364
  30.2 1.1 collective-permute-start.8
  31.3 2.6 %collective-permute-done.7 = f32[4,8,8,128]{3,2,1,0:T(8,128)S(1)} collective-permute-done((f32[4,8,8,128]{3,2,1,0:T(8,128)S(1)}, f32[4,8,8,128]{3,2,1,0:T(8,128)S(1)}, u32[]{:S(2)}, u32[]{:S(2)}) %collective-permute-start.7) | collective-permute-done | bytes 131104 | tf_op jit(solution)/shard_map/ppermute | solution.py:364
  34.0 6.2 %collective-permute-start.9 = (f32[4,4,8,8,128]{4,3,2,1,0:T(8,128)S(1)}, f32[4,4,8,8,128]{4,3,2,1,0:T(8,128)S(1)}, u32[]{:S(2)}, u32[]{:S(2)}) collective-permute-start(f32[4,4,8,8,128]{4,3,2,1,0:T(8,128)S(1)} %pad_maximum_fusion.1.refs_0_.refs_1_), channel_id=1, source_target_pairs={{0,8},{8,0},{1,9},{9,1},{2,10},{10,2},{3,11},{11,3},{4,12},{12,4},... | collective-permute-start | bytes 1572872 | tf_op jit(solution)/shard_map/ppermute | solution.py:364
  40.9 0.9 collective-permute-done.9.refs_1_.refs_2_
  41.7 0.8 copy-done.6
  42.5 8.8 %row_pairs.1 = (bf16[32,16,256]{2,1,0:T(8,128)(2,1)}, bf16[416,256]{1,0:T(8,128)(2,1)}) custom-call(s32[5]{0:T(128)} %stack.77.pos, f32[4,4,8,8,128]{4,3,2,1,0:T(8,128)} %copy-done.3, f32[4,4,8,8,128]{4,3,2,1,0:T(8,128)} %copy-done.6, f32[256,128]{1,0:T(8,128)} %bitcast.48, bf16[1024,512]{1,0:T(8,128)(2,1)} %constant.38.clone.refs_3_.refs_6_, ...), custom_call_target="tpu_custom_call" | custom-call | flops 4000000000 | bytes 6291456 | tf_op jit(solution)/shard_map/row_pairs/pallas_call | solution.py:229
  51.4 7.6 %all-to-all-start.1 = ((bf16[32,16,256]{2,1,0:T(8,128)(2,1)}), bf16[32,16,256]{2,1,0:T(8,128)(2,1)S(1)}, u32[]{:S(2)}, u32[]{:S(2)}) async-start(bf16[32,16,256]{2,1,0:T(8,128)(2,1)} %get-tuple-element.32), calls=%async_computation.1 | async-start | bytes 524288 | tf_op jit(solution)/shard_map/all_to_all | solution.py:392
  59.0 9.9 %column_pairs.1 = bf16[2,4,16,640]{3,2,1,0:T(8,128)(2,1)} custom-call(s32[5]{0:T(128)} %stack.77.pos, bf16[416,256]{1,0:T(8,128)(2,1)} %get-tuple-element.33.refs_0_, f32[4,4,8,8,128]{4,3,2,1,0:T(8,128)} %copy-done.3, f32[4,4,8,8,128]{4,3,2,1,0:T(8,128)} %copy-done.6, f32[256,128]{1,0:T(8,128)} %copy-done.7, f32[256,128]{1,0:T(8,128)} %copy-done.8, ...), custom_call_target="tpu_custom_call" | custom-call | flops 8000000000 | bytes 6291456 | tf_op jit(solution)/shard_map/column_pairs/pallas_call | solution.py:229
  69.0 0.9 slice_bitcast_fusion
  70.0 2.1 %all-to-all-done.1 = bf16[32,16,256]{2,1,0:T(8,128)(2,1)S(1)} async-done(((bf16[32,16,256]{2,1,0:T(8,128)(2,1)}), bf16[32,16,256]{2,1,0:T(8,128)(2,1)S(1)}, u32[]{:S(2)}, u32[]{:S(2)}) %all-to-all-start.1) | async-done | bytes 262176 | tf_op jit(solution)/shard_map/all_to_all | solution.py:392
  72.1 1.4 collective-permute-done.11
  73.5 0.9 broadcast_select_fusion.1
  74.4 5.7 %collective-permute-done.10 = bf16[32,16,256]{2,1,0:T(8,128)(2,1)S(1)} collective-permute-done((bf16[32,16,256]{2,1,0:T(8,128)(2,1)S(1)}, bf16[32,16,256]{2,1,0:T(8,128)(2,1)S(1)}, u32[]{:S(2)}, u32[]{:S(2)}) %collective-permute-start.10) | collective-permute-done | bytes 262176 | tf_op jit(solution)/shard_map/ppermute | solution.py:364
  80.6 2.4 %collective-permute-start.13 = (bf16[2,4,4,2,16,256]{5,4,3,2,1,0:T(8,128)(2,1)S(1)}, bf16[2,4,4,2,16,256]{5,4,3,2,1,0:T(8,128)(2,1)S(1)}, u32[]{:S(2)}, u32[]{:S(2)}) collective-permute-start(bf16[2,4,4,2,16,256]{5,4,3,2,1,0:T(8,128)(2,1)S(1)} %pad_maximum_fusion.2.r0), channel_id=1, source_target_pairs={{0,3},{1,0},{2,1},{3,2},{4,7},{5,4},{6,5},{7,6},{8,11},{9,8},{10,9... | collective-permute-start | bytes 1572872 | tf_op jit(solution)/shard_map/ppermute | solution.py:364
  83.0 1.6 %collective-permute-start.14 = (bf16[8,16,640]{2,1,0:T(8,128)(2,1)S(1)}, bf16[8,16,640]{2,1,0:T(8,128)(2,1)S(1)}, u32[]{:S(2)}, u32[]{:S(2)}) collective-permute-start(bf16[8,16,640]{2,1,0:T(8,128)(2,1)S(1)} %pad_maximum_fusion.4), channel_id=1, source_target_pairs={{0,64},{64,128},{128,192},{192,0},{1,65},{65,129},{129,193},{193,1... | collective-permute-start | bytes 491528 | tf_op jit(solution)/shard_map/ppermute | solution.py:364
  84.6 2.0 %collective-permute-start.15 = (bf16[8,16,640]{2,1,0:T(8,128)(2,1)S(1)}, bf16[8,16,640]{2,1,0:T(8,128)(2,1)S(1)}, u32[]{:S(2)}, u32[]{:S(2)}) collective-permute-start(bf16[8,16,640]{2,1,0:T(8,128)(2,1)S(1)} %pad_maximum_fusion.4), channel_id=1, source_target_pairs={{0,192},{64,0},{128,64},{192,128},{1,193},{65,1},{129,65},{193,129... | collective-permute-start | bytes 491528 | tf_op jit(solution)/shard_map/ppermute | solution.py:364
  86.6 7.5 %collective-permute-done.14 = bf16[8,16,640]{2,1,0:T(8,128)(2,1)S(1)} collective-permute-done((bf16[8,16,640]{2,1,0:T(8,128)(2,1)S(1)}, bf16[8,16,640]{2,1,0:T(8,128)(2,1)S(1)}, u32[]{:S(2)}, u32[]{:S(2)}) %collective-permute-start.14) | collective-permute-done | bytes 163872 | tf_op jit(solution)/shard_map/ppermute | solution.py:364
  94.0 1.4 collective-permute-done.15
  95.4 2.5 %collective-permute-start.16 = (bf16[4,16,640]{2,1,0:T(8,128)(2,1)S(1)}, bf16[4,16,640]{2,1,0:T(8,128)(2,1)S(1)}, u32[]{:S(2)}, u32[]{:S(2)}) collective-permute-start(bf16[4,16,640]{2,1,0:T(8,128)(2,1)S(1)} %slice.26), channel_id=1, source_target_pairs={{0,192},{64,0},{128,64},{192,128},{1,193},{65,1},{129,65},{193,129... | collective-permute-start | bytes 245768 | tf_op jit(solution)/shard_map/ppermute | solution.py:364
  98.1 1.6 %collective-permute-done.16 = bf16[4,16,640]{2,1,0:T(8,128)(2,1)S(1)} collective-permute-done((bf16[4,16,640]{2,1,0:T(8,128)(2,1)S(1)}, bf16[4,16,640]{2,1,0:T(8,128)(2,1)S(1)}, u32[]{:S(2)}, u32[]{:S(2)}) %collective-permute-start.16) | collective-permute-done | bytes 81952 | tf_op jit(solution)/shard_map/ppermute | solution.py:364
  99.7 3.8 %collective-permute-done.17 = bf16[4,16,640]{2,1,0:T(8,128)(2,1)S(1)} collective-permute-done((bf16[4,16,640]{2,1,0:T(8,128)(2,1)S(1)}, bf16[4,16,640]{2,1,0:T(8,128)(2,1)S(1)}, u32[]{:S(2)}, u32[]{:S(2)}) %collective-permute-start.17) | collective-permute-done | bytes 81952 | tf_op jit(solution)/shard_map/ppermute | solution.py:364
  103.6 2.6 %collective-permute-start.18 = (bf16[4,8,16,640]{3,2,1,0:T(8,128)(2,1)S(1)}, bf16[4,8,16,640]{3,2,1,0:T(8,128)(2,1)S(1)}, u32[]{:S(2)}, u32[]{:S(2)}) collective-permute-start(bf16[4,8,16,640]{3,2,1,0:T(8,128)(2,1)S(1)} %pad_maximum_fusion.mine), channel_id=1, source_target_pairs={{0,8},{8,0},{1,9},{9,1},{2,10},{10,2},{3,11},{11,3},{4,12},{12,4},... | collective-permute-start | bytes 1966088 | tf_op jit(solution)/shard_map/ppermute | solution.py:364
  106.3 2.7 %collective-permute-start.19 = (bf16[1,4,4,2,16,256]{5,4,3,2,1,0:T(8,128)(2,1)S(1)}, bf16[1,4,4,2,16,256]{5,4,3,2,1,0:T(8,128)(2,1)S(1)}, u32[]{:S(2)}, u32[]{:S(2)}) collective-permute-start(bf16[1,4,4,2,16,256]{5,4,3,2,1,0:T(8,128)(2,1)S(1)} %slice.28), channel_id=1, source_target_pairs={{0,3},{1,0},{2,1},{3,2},{4,7},{5,4},{6,5},{7,6},{8,11},{9,8},{10,9... | collective-permute-start | bytes 786440 | tf_op jit(solution)/shard_map/ppermute | solution.py:364
  109.1 1.5 collective-permute-start.21
  110.5 1.5 collective-permute-start.22
  112.0 2.6 %collective-permute-done.19 = bf16[1,4,4,2,16,256]{5,4,3,2,1,0:T(8,128)(2,1)S(1)} collective-permute-done((bf16[1,4,4,2,16,256]{5,4,3,2,1,0:T(8,128)(2,1)S(1)}, bf16[1,4,4,2,16,256]{5,4,3,2,1,0:T(8,128)(2,1)S(1)}, u32[]{:S(2)}, u32[]{:S(2)}) %collective-permute-start.19) | collective-permute-done | bytes 262176 | tf_op jit(solution)/shard_map/ppermute | solution.py:364
  114.7 3.2 %collective-permute-done.20 = bf16[1,4,4,2,16,256]{5,4,3,2,1,0:T(8,128)(2,1)S(1)} collective-permute-done((bf16[1,4,4,2,16,256]{5,4,3,2,1,0:T(8,128)(2,1)S(1)}, bf16[1,4,4,2,16,256]{5,4,3,2,1,0:T(8,128)(2,1)S(1)}, u32[]{:S(2)}, u32[]{:S(2)}) %collective-permute-start.20) | collective-permute-done | bytes 262176 | tf_op jit(solution)/shard_map/ppermute | solution.py:364
  117.9 0.9 pad_maximum_fusion.3.r2
  118.8 5.2 %scaled_rows.1 = (bf16[4,1536,1024]{2,1,0:T(8,128)(2,1)S(1)}, bf16[4,640,256]{2,1,0:T(8,128)(2,1)S(1)}, f32[4,16,256]{2,1,0:T(8,128)S(1)}) custom-call(s32[5]{0:T(128)S(1)} %copy-done, f32[6]{0:T(128)S(1)} %copy-done.1, bf16[2,4,4,2,16,256]{5,4,3,2,1,0:T(8,128)(2,1)} %copy-done.2, bf16[2,4,4,2,16,256]{5,4,3,2,1,0:T(8,128)(2,1)} %copy-done.4, ...), custom_call_target="tpu_custom_call" | custom-call | flops 1000000000 | bytes 20971520 | tf_op jit(solution)/shard_map/scaled_rows/pallas_call | solution.py:303
  124.0 5.9 %response_product.4.refs_0_ = f32[6,256,1024]{2,1,0:T(8,128)S(1)} custom-call(bf16[4,8,16,640]{3,2,1,0:T(8,128)(2,1)S(1)} %pad_maximum_fusion.mine, bf16[4,8,16,640]{3,2,1,0:T(8,128)(2,1)S(1)} %collective-permute-done.18.theirs, bf16[4,1536,1024]{2,1,0:T(8,128)(2,1)S(1)} %get-tuple-element.44.scaled, bf16[4,640,256]{2,1,0:T(8,128)(2,1)S(1)} %get-tuple-element.45.hot, ...), custom_call_target="tpu_custom_call" | custom-call | flops 4600000000 | bytes 10485760 | tf_op jit(solution)/shard_map/response_product/pallas_call | solution.py:348
  129.9 1.2 collective-permute-start.23
  131.3 2.5 %collective-permute-start.24 = (bf16[2,8,16,640]{3,2,1,0:T(8,128)(2,1)S(1)}, bf16[2,8,16,640]{3,2,1,0:T(8,128)(2,1)S(1)}, u32[]{:S(2)}, u32[]{:S(2)}) collective-permute-start(bf16[2,8,16,640]{3,2,1,0:T(8,128)(2,1)S(1)} %slice.30), channel_id=1, source_target_pairs={{0,48},{16,0},{32,16},{48,32},{1,49},{17,1},{33,17},{49,33},{2,50}... | collective-permute-start | bytes 983048 | tf_op jit(solution)/shard_map/ppermute | solution.py:364
  133.8 5.9 %response_product.5.refs_0_ = f32[6,256,1024]{2,1,0:T(8,128)S(1)} custom-call(bf16[4,8,16,640]{3,2,1,0:T(8,128)(2,1)S(1)} %collective-permute-done.21.mine, bf16[4,8,16,640]{3,2,1,0:T(8,128)(2,1)S(1)} %collective-permute-done.23.theirs, bf16[4,1536,1024]{2,1,0:T(8,128)(2,1)S(1)} %get-tuple-element.44.scaled, ...), custom_call_target="tpu_custom_call", output_to_operand_aliasing={{}: (5, {})} | custom-call | flops 4600000000 | bytes 10485760 | tf_op jit(solution)/shard_map/response_product/pallas_call | solution.py:348
  139.7 0.8 collective-permute-done.24
  140.5 3.1 %collective-permute-done.25 = bf16[2,8,16,640]{3,2,1,0:T(8,128)(2,1)S(1)} collective-permute-done((bf16[2,8,16,640]{3,2,1,0:T(8,128)(2,1)S(1)}, bf16[2,8,16,640]{3,2,1,0:T(8,128)(2,1)S(1)}, u32[]{:S(2)}, u32[]{:S(2)}) %collective-permute-start.25) | collective-permute-done | bytes 327712 | tf_op jit(solution)/shard_map/ppermute | solution.py:364
  143.6 1.7 %collective-permute-start.26 = (bf16[4,8,16,640]{3,2,1,0:T(8,128)(2,1)S(1)}, bf16[4,8,16,640]{3,2,1,0:T(8,128)(2,1)S(1)}, u32[]{:S(2)}, u32[]{:S(2)}) collective-permute-start(bf16[4,8,16,640]{3,2,1,0:T(8,128)(2,1)S(1)} %constant_dynamic-update-slice_fusion.mine), channel_id=1, source_target_pairs={{0,8},{8,0},{1,9},{9,1},{2,10},{10,2},{3,11},{11,3},{4,12},{12,4},... | collective-permute-start | bytes 1966088 | tf_op jit(solution)/shard_map/ppermute | solution.py:364
  145.3 5.9 %response_product.6.refs_0_ = f32[6,256,1024]{2,1,0:T(8,128)S(1)} custom-call(bf16[4,8,16,640]{3,2,1,0:T(8,128)(2,1)S(1)} %collective-permute-done.22.mine, bf16[4,8,16,640]{3,2,1,0:T(8,128)(2,1)S(1)} %collective-permute-done.27.theirs, bf16[4,1536,1024]{2,1,0:T(8,128)(2,1)S(1)} %get-tuple-element.44.scaled, ...), custom_call_target="tpu_custom_call", output_to_operand_aliasing={{}: (5, {})} | custom-call | flops 4600000000 | bytes 10485760 | tf_op jit(solution)/shard_map/response_product/pallas_call | solution.py:348
  151.2 7.2 %response_product.7 = f32[6,256,1024]{2,1,0:T(8,128)} custom-call(bf16[4,8,16,640]{3,2,1,0:T(8,128)(2,1)S(1)} %constant_dynamic-update-slice_fusion.mine, bf16[4,8,16,640]{3,2,1,0:T(8,128)(2,1)S(1)} %collective-permute-done.26.theirs, bf16[4,1536,1024]{2,1,0:T(8,128)(2,1)S(1)} %get-tuple-element.44.scaled, bf16[4,640,256]{2,1,0:T(8,128)(2,1)S(1)} %get-tuple-element.45.hot, ...), custom_call_target="tpu_custom_call" | custom-call | flops 4600000000 | bytes 10485760 | tf_op jit(solution)/shard_map/response_product/pallas_call | solution.py:348
  (60 shorter events, 3.7 us)
Async XLA Ops:
  0.0 14.2 %collective-permute-start = (f32[256,128]{1,0:T(8,128)}, f32[256,128]{1,0:T(8,128)S(1)}, u32[]{:S(2)}, u32[]{:S(2)}) collective-permute-start(f32[256,128]{1,0:T(8,128)} %bitcast.45), channel_id=1, source_target_pairs={{0,1},{1,2},{2,3},{3,0},{4,5},{5,6},{6,7},{7,4},{8,9},{9,10},{10,1... | collective-permute-start | bytes 393224 | tf_op jit(solution)/shard_map/ppermute | solution.py:364
  2.0 12.1 %collective-permute-start.1 = (f32[256,128]{1,0:T(8,128)}, f32[256,128]{1,0:T(8,128)S(1)}, u32[]{:S(2)}, u32[]{:S(2)}) collective-permute-start(f32[256,128]{1,0:T(8,128)} %bitcast.46), channel_id=1, source_target_pairs={{0,2},{1,3},{2,0},{3,1},{4,6},{5,7},{6,4},{7,5},{8,10},{9,11},{10,... | collective-permute-start | bytes 393224 | tf_op jit(solution)/shard_map/ppermute | solution.py:364
  4.5 9.7 %collective-permute-start.2 = (f32[256,128]{1,0:T(8,128)}, f32[256,128]{1,0:T(8,128)S(1)}, u32[]{:S(2)}, u32[]{:S(2)}) collective-permute-start(f32[256,128]{1,0:T(8,128)} %bitcast.47), channel_id=1, source_target_pairs={{0,3},{1,0},{2,1},{3,2},{4,7},{5,4},{6,5},{7,6},{8,11},{9,8},{10,9... | collective-permute-start | bytes 393224 | tf_op jit(solution)/shard_map/ppermute | solution.py:364
  14.2 37.2 %copy-start.7 = (f32[256,128]{1,0:T(8,128)}, f32[256,128]{1,0:T(8,128)S(1)}, u32[]{:S(2)}) copy-start(f32[256,128]{1,0:T(8,128)S(1)} %collective-permute-done.refs_3_) | copy-start | bytes 393220
  14.2 37.2 %copy-start.8 = (f32[256,128]{1,0:T(8,128)}, f32[256,128]{1,0:T(8,128)S(1)}, u32[]{:S(2)}) copy-start(f32[256,128]{1,0:T(8,128)S(1)} %collective-permute-done.1.refs_4_) | copy-start | bytes 393220
  14.2 37.2 %copy-start.9 = (f32[256,128]{1,0:T(8,128)}, f32[256,128]{1,0:T(8,128)S(1)}, u32[]{:S(2)}) copy-start(f32[256,128]{1,0:T(8,128)S(1)} %collective-permute-done.2.refs_5_) | copy-start | bytes 393220
  14.2 11.5 %collective-permute-start.3 = (f32[8,8,128]{2,1,0:T(8,128)S(1)}, f32[8,8,128]{2,1,0:T(8,128)S(1)}, u32[]{:S(2)}, u32[]{:S(2)}) collective-permute-start(f32[8,8,128]{2,1,0:T(8,128)S(1)} %all_to_all.10), channel_id=1, source_target_pairs={{0,64},{64,128},{128,192},{192,0},{1,65},{65,129},{129,193},{193,1... | collective-permute-start | bytes 98312 | tf_op jit(solution)/shard_map/ppermute | solution.py:364
  17.3 8.4 %collective-permute-start.4 = (f32[8,8,128]{2,1,0:T(8,128)S(1)}, f32[8,8,128]{2,1,0:T(8,128)S(1)}, u32[]{:S(2)}, u32[]{:S(2)}) collective-permute-start(f32[8,8,128]{2,1,0:T(8,128)S(1)} %all_to_all.10), channel_id=1, source_target_pairs={{0,128},{64,192},{128,0},{192,64},{1,129},{65,193},{129,1},{193,65... | collective-permute-start | bytes 98312 | tf_op jit(solution)/shard_map/ppermute | solution.py:364
  22.0 4.1 %collective-permute-start.5 = (f32[8,8,128]{2,1,0:T(8,128)S(1)}, f32[8,8,128]{2,1,0:T(8,128)S(1)}, u32[]{:S(2)}, u32[]{:S(2)}) collective-permute-start(f32[8,8,128]{2,1,0:T(8,128)S(1)} %all_to_all.10), channel_id=1, source_target_pairs={{0,192},{64,0},{128,64},{192,128},{1,193},{65,1},{129,65},{193,129... | collective-permute-start | bytes 98312 | tf_op jit(solution)/shard_map/ppermute | solution.py:364
  26.2 5.2 %collective-permute-start.6 = (f32[4,8,8,128]{3,2,1,0:T(8,128)S(1)}, f32[4,8,8,128]{3,2,1,0:T(8,128)S(1)}, u32[]{:S(2)}, u32[]{:S(2)}) collective-permute-start(f32[4,8,8,128]{3,2,1,0:T(8,128)S(1)} %pad_maximum_fusion.5), channel_id=1, source_target_pairs={{0,16},{16,32},{32,48},{48,0},{1,17},{17,33},{33,49},{49,1},{2,18}... | collective-permute-start | bytes 393224 | tf_op jit(solution)/shard_map/ppermute | solution.py:364
  27.5 6.4 %collective-permute-start.7 = (f32[4,8,8,128]{3,2,1,0:T(8,128)S(1)}, f32[4,8,8,128]{3,2,1,0:T(8,128)S(1)}, u32[]{:S(2)}, u32[]{:S(2)}) collective-permute-start(f32[4,8,8,128]{3,2,1,0:T(8,128)S(1)} %pad_maximum_fusion.5), channel_id=1, source_target_pairs={{0,32},{16,48},{32,0},{48,16},{1,33},{17,49},{33,1},{49,17},{2,34}... | collective-permute-start | bytes 393224 | tf_op jit(solution)/shard_map/ppermute | solution.py:364
  30.2 3.8 %collective-permute-start.8 = (f32[4,8,8,128]{3,2,1,0:T(8,128)S(1)}, f32[4,8,8,128]{3,2,1,0:T(8,128)S(1)}, u32[]{:S(2)}, u32[]{:S(2)}) collective-permute-start(f32[4,8,8,128]{3,2,1,0:T(8,128)S(1)} %pad_maximum_fusion.5), channel_id=1, source_target_pairs={{0,48},{16,0},{32,16},{48,32},{1,49},{17,1},{33,17},{49,33},{2,50}... | collective-permute-start | bytes 393224 | tf_op jit(solution)/shard_map/ppermute | solution.py:364
  34.0 7.7 %copy-start.3 = (f32[4,4,8,8,128]{4,3,2,1,0:T(8,128)}, f32[4,4,8,8,128]{4,3,2,1,0:T(8,128)S(1)}, u32[]{:S(2)}) copy-start(f32[4,4,8,8,128]{4,3,2,1,0:T(8,128)S(1)} %pad_maximum_fusion.1.refs_0_.refs_1_) | copy-start | bytes 1572868
  34.0 7.7 %collective-permute-start.9 = (f32[4,4,8,8,128]{4,3,2,1,0:T(8,128)S(1)}, f32[4,4,8,8,128]{4,3,2,1,0:T(8,128)S(1)}, u32[]{:S(2)}, u32[]{:S(2)}) collective-permute-start(f32[4,4,8,8,128]{4,3,2,1,0:T(8,128)S(1)} %pad_maximum_fusion.1.refs_0_.refs_1_), channel_id=1, source_target_pairs={{0,8},{8,0},{1,9},{9,1},{2,10},{10,2},{3,11},{11,3},{4,12},{12,4},... | collective-permute-start | bytes 1572872 | tf_op jit(solution)/shard_map/ppermute | solution.py:364
  41.7 0.8 copy-start.6
  51.4 20.7 %all-to-all-start.1 = ((bf16[32,16,256]{2,1,0:T(8,128)(2,1)}), bf16[32,16,256]{2,1,0:T(8,128)(2,1)S(1)}, u32[]{:S(2)}, u32[]{:S(2)}) async-start(bf16[32,16,256]{2,1,0:T(8,128)(2,1)} %get-tuple-element.32), calls=%async_computation.1 | async-start | bytes 524288 | tf_op jit(solution)/shard_map/all_to_all | solution.py:392
  59.0 59.8 %copy-start = (s32[5]{0:T(128)S(1)}, s32[5]{0:T(128)}, u32[]{:S(2)}) copy-start(s32[5]{0:T(128)} %stack.77.pos) | copy-start | bytes 64
  59.0 59.8 %copy-start.1 = (f32[6]{0:T(128)S(1)}, f32[6]{0:T(128)}, u32[]{:S(2)}) copy-start(f32[6]{0:T(128)} %omega.1) | copy-start | bytes 76
  69.9 3.6 %collective-permute-start.11 = (bf16[4,16,640]{2,1,0:T(8,128)(2,1)S(1)}, bf16[4,16,640]{2,1,0:T(8,128)(2,1)S(1)}, u32[]{:S(2)}, u32[]{:S(2)}) collective-permute-start(bf16[4,16,640]{2,1,0:T(8,128)(2,1)S(1)} %slice_bitcast_fusion), channel_id=1, source_target_pairs={{0,4},{4,0},{1,5},{5,1},{2,6},{6,2},{3,7},{7,3},{8,12},{12,8},{9,1... | collective-permute-start | bytes 245768 | tf_op jit(solution)/shard_map/ppermute | solution.py:364
  72.1 8.1 %collective-permute-start.10 = (bf16[32,16,256]{2,1,0:T(8,128)(2,1)S(1)}, bf16[32,16,256]{2,1,0:T(8,128)(2,1)S(1)}, u32[]{:S(2)}, u32[]{:S(2)}) collective-permute-start(bf16[32,16,256]{2,1,0:T(8,128)(2,1)S(1)} %all-to-all-done.1), channel_id=1, source_target_pairs={{0,4},{4,0},{1,5},{5,1},{2,6},{6,2},{3,7},{7,3},{8,12},{12,8},{9,1... | collective-permute-start | bytes 786440 | tf_op jit(solution)/shard_map/ppermute | solution.py:364
  80.2 38.5 %copy-start.2 = (bf16[2,4,4,2,16,256]{5,4,3,2,1,0:T(8,128)(2,1)}, bf16[2,4,4,2,16,256]{5,4,3,2,1,0:T(8,128)(2,1)S(1)}, u32[]{:S(2)}) copy-start(bf16[2,4,4,2,16,256]{5,4,3,2,1,0:T(8,128)(2,1)S(1)} %pad_maximum_fusion.2.r0) | copy-start | bytes 1572868
  80.2 15.2 %collective-permute-start.12 = (bf16[2,4,4,2,16,256]{5,4,3,2,1,0:T(8,128)(2,1)S(1)}, bf16[2,4,4,2,16,256]{5,4,3,2,1,0:T(8,128)(2,1)S(1)}, u32[]{:S(2)}, u32[]{:S(2)}) collective-permute-start(bf16[2,4,4,2,16,256]{5,4,3,2,1,0:T(8,128)(2,1)S(1)} %pad_maximum_fusion.2.r0), channel_id=1, source_target_pairs={{0,1},{1,2},{2,3},{3,0},{4,5},{5,6},{6,7},{7,4},{8,9},{9,10},{10,1... | collective-permute-start | bytes 1572872 | tf_op jit(solution)/shard_map/ppermute | solution.py:364
  80.6 14.8 %collective-permute-start.13 = (bf16[2,4,4,2,16,256]{5,4,3,2,1,0:T(8,128)(2,1)S(1)}, bf16[2,4,4,2,16,256]{5,4,3,2,1,0:T(8,128)(2,1)S(1)}, u32[]{:S(2)}, u32[]{:S(2)}) collective-permute-start(bf16[2,4,4,2,16,256]{5,4,3,2,1,0:T(8,128)(2,1)S(1)} %pad_maximum_fusion.2.r0), channel_id=1, source_target_pairs={{0,3},{1,0},{2,1},{3,2},{4,7},{5,4},{6,5},{7,6},{8,11},{9,8},{10,9... | collective-permute-start | bytes 1572872 | tf_op jit(solution)/shard_map/ppermute | solution.py:364
  83.0 11.1 %collective-permute-start.14 = (bf16[8,16,640]{2,1,0:T(8,128)(2,1)S(1)}, bf16[8,16,640]{2,1,0:T(8,128)(2,1)S(1)}, u32[]{:S(2)}, u32[]{:S(2)}) collective-permute-start(bf16[8,16,640]{2,1,0:T(8,128)(2,1)S(1)} %pad_maximum_fusion.4), channel_id=1, source_target_pairs={{0,64},{64,128},{128,192},{192,0},{1,65},{65,129},{129,193},{193,1... | collective-permute-start | bytes 491528 | tf_op jit(solution)/shard_map/ppermute | solution.py:364
  84.6 10.8 %collective-permute-start.15 = (bf16[8,16,640]{2,1,0:T(8,128)(2,1)S(1)}, bf16[8,16,640]{2,1,0:T(8,128)(2,1)S(1)}, u32[]{:S(2)}, u32[]{:S(2)}) collective-permute-start(bf16[8,16,640]{2,1,0:T(8,128)(2,1)S(1)} %pad_maximum_fusion.4), channel_id=1, source_target_pairs={{0,192},{64,0},{128,64},{192,128},{1,193},{65,1},{129,65},{193,129... | collective-permute-start | bytes 491528 | tf_op jit(solution)/shard_map/ppermute | solution.py:364
  95.4 23.3 %copy-start.4 = (bf16[2,4,4,2,16,256]{5,4,3,2,1,0:T(8,128)(2,1)}, bf16[2,4,4,2,16,256]{5,4,3,2,1,0:T(8,128)(2,1)S(1)}, u32[]{:S(2)}) copy-start(bf16[2,4,4,2,16,256]{5,4,3,2,1,0:T(8,128)(2,1)S(1)} %collective-permute-done.12.r1) | copy-start | bytes 1572868
  95.4 23.3 %copy-start.5 = (bf16[2,4,4,2,16,256]{5,4,3,2,1,0:T(8,128)(2,1)}, bf16[2,4,4,2,16,256]{5,4,3,2,1,0:T(8,128)(2,1)S(1)}, u32[]{:S(2)}) copy-start(bf16[2,4,4,2,16,256]{5,4,3,2,1,0:T(8,128)(2,1)S(1)} %collective-permute-done.13.r3) | copy-start | bytes 1572868
  95.4 4.3 %collective-permute-start.16 = (bf16[4,16,640]{2,1,0:T(8,128)(2,1)S(1)}, bf16[4,16,640]{2,1,0:T(8,128)(2,1)S(1)}, u32[]{:S(2)}, u32[]{:S(2)}) collective-permute-start(bf16[4,16,640]{2,1,0:T(8,128)(2,1)S(1)} %slice.26), channel_id=1, source_target_pairs={{0,192},{64,0},{128,64},{192,128},{1,193},{65,1},{129,65},{193,129... | collective-permute-start | bytes 245768 | tf_op jit(solution)/shard_map/ppermute | solution.py:364
  98.0 5.5 %collective-permute-start.17 = (bf16[4,16,640]{2,1,0:T(8,128)(2,1)S(1)}, bf16[4,16,640]{2,1,0:T(8,128)(2,1)S(1)}, u32[]{:S(2)}, u32[]{:S(2)}) collective-permute-start(bf16[4,16,640]{2,1,0:T(8,128)(2,1)S(1)} %slice.27), channel_id=1, source_target_pairs={{0,64},{64,128},{128,192},{192,0},{1,65},{65,129},{129,193},{193,1... | collective-permute-start | bytes 245768 | tf_op jit(solution)/shard_map/ppermute | solution.py:364
  103.6 20.4 %collective-permute-start.18 = (bf16[4,8,16,640]{3,2,1,0:T(8,128)(2,1)S(1)}, bf16[4,8,16,640]{3,2,1,0:T(8,128)(2,1)S(1)}, u32[]{:S(2)}, u32[]{:S(2)}) collective-permute-start(bf16[4,8,16,640]{3,2,1,0:T(8,128)(2,1)S(1)} %pad_maximum_fusion.mine), channel_id=1, source_target_pairs={{0,8},{8,0},{1,9},{9,1},{2,10},{10,2},{3,11},{11,3},{4,12},{12,4},... | collective-permute-start | bytes 1966088 | tf_op jit(solution)/shard_map/ppermute | solution.py:364
  106.3 8.4 %collective-permute-start.19 = (bf16[1,4,4,2,16,256]{5,4,3,2,1,0:T(8,128)(2,1)S(1)}, bf16[1,4,4,2,16,256]{5,4,3,2,1,0:T(8,128)(2,1)S(1)}, u32[]{:S(2)}, u32[]{:S(2)}) collective-permute-start(bf16[1,4,4,2,16,256]{5,4,3,2,1,0:T(8,128)(2,1)S(1)} %slice.28), channel_id=1, source_target_pairs={{0,3},{1,0},{2,1},{3,2},{4,7},{5,4},{6,5},{7,6},{8,11},{9,8},{10,9... | collective-permute-start | bytes 786440 | tf_op jit(solution)/shard_map/ppermute | solution.py:364
  109.0 8.9 %collective-permute-start.20 = (bf16[1,4,4,2,16,256]{5,4,3,2,1,0:T(8,128)(2,1)S(1)}, bf16[1,4,4,2,16,256]{5,4,3,2,1,0:T(8,128)(2,1)S(1)}, u32[]{:S(2)}, u32[]{:S(2)}) collective-permute-start(bf16[1,4,4,2,16,256]{5,4,3,2,1,0:T(8,128)(2,1)S(1)} %slice.29), channel_id=1, source_target_pairs={{0,1},{1,2},{2,3},{3,0},{4,5},{5,6},{6,7},{7,4},{8,9},{9,10},{10,1... | collective-permute-start | bytes 786440 | tf_op jit(solution)/shard_map/ppermute | solution.py:364
  109.1 20.8 %collective-permute-start.21 = (bf16[4,8,16,640]{3,2,1,0:T(8,128)(2,1)S(1)}, bf16[4,8,16,640]{3,2,1,0:T(8,128)(2,1)S(1)}, u32[]{:S(2)}, u32[]{:S(2)}) collective-permute-start(bf16[4,8,16,640]{3,2,1,0:T(8,128)(2,1)S(1)} %pad_maximum_fusion.mine), channel_id=1, source_target_pairs={{0,16},{16,32},{32,48},{48,0},{1,17},{17,33},{33,49},{49,1},{2,18}... | collective-permute-start | bytes 1966088 | tf_op jit(solution)/shard_map/ppermute | solution.py:364
  110.5 19.4 %collective-permute-start.22 = (bf16[4,8,16,640]{3,2,1,0:T(8,128)(2,1)S(1)}, bf16[4,8,16,640]{3,2,1,0:T(8,128)(2,1)S(1)}, u32[]{:S(2)}, u32[]{:S(2)}) collective-permute-start(bf16[4,8,16,640]{3,2,1,0:T(8,128)(2,1)S(1)} %pad_maximum_fusion.mine), channel_id=1, source_target_pairs={{0,48},{16,0},{32,16},{48,32},{1,49},{17,1},{33,17},{49,33},{2,50}... | collective-permute-start | bytes 1966088 | tf_op jit(solution)/shard_map/ppermute | solution.py:364
  129.9 3.9 %collective-permute-start.23 = (bf16[4,8,16,640]{3,2,1,0:T(8,128)(2,1)S(1)}, bf16[4,8,16,640]{3,2,1,0:T(8,128)(2,1)S(1)}, u32[]{:S(2)}, u32[]{:S(2)}) collective-permute-start(bf16[4,8,16,640]{3,2,1,0:T(8,128)(2,1)S(1)} %collective-permute-done.21.mine), channel_id=1, source_target_pairs={{0,8},{8,0},{1,9},{9,1},{2,10},{10,2},{3,11},{11,3},{4,12},{12,4},... | collective-permute-start | bytes 1966088 | tf_op jit(solution)/shard_map/ppermute | solution.py:364
  131.2 14.1 %collective-permute-start.27 = (bf16[4,8,16,640]{3,2,1,0:T(8,128)(2,1)S(1)}, bf16[4,8,16,640]{3,2,1,0:T(8,128)(2,1)S(1)}, u32[]{:S(2)}, u32[]{:S(2)}) collective-permute-start(bf16[4,8,16,640]{3,2,1,0:T(8,128)(2,1)S(1)} %collective-permute-done.22.mine), channel_id=1, source_target_pairs={{0,8},{8,0},{1,9},{9,1},{2,10},{10,2},{3,11},{11,3},{4,12},{12,4},... | collective-permute-start | bytes 1966088 | tf_op jit(solution)/shard_map/ppermute | solution.py:364
  131.3 9.2 %collective-permute-start.24 = (bf16[2,8,16,640]{3,2,1,0:T(8,128)(2,1)S(1)}, bf16[2,8,16,640]{3,2,1,0:T(8,128)(2,1)S(1)}, u32[]{:S(2)}, u32[]{:S(2)}) collective-permute-start(bf16[2,8,16,640]{3,2,1,0:T(8,128)(2,1)S(1)} %slice.30), channel_id=1, source_target_pairs={{0,48},{16,0},{32,16},{48,32},{1,49},{17,1},{33,17},{49,33},{2,50}... | collective-permute-start | bytes 983048 | tf_op jit(solution)/shard_map/ppermute | solution.py:364
  133.8 9.8 %collective-permute-start.25 = (bf16[2,8,16,640]{3,2,1,0:T(8,128)(2,1)S(1)}, bf16[2,8,16,640]{3,2,1,0:T(8,128)(2,1)S(1)}, u32[]{:S(2)}, u32[]{:S(2)}) collective-permute-start(bf16[2,8,16,640]{3,2,1,0:T(8,128)(2,1)S(1)} %slice.31), channel_id=1, source_target_pairs={{0,16},{16,32},{32,48},{48,0},{1,17},{17,33},{33,49},{49,1},{2,18}... | collective-permute-start | bytes 983048 | tf_op jit(solution)/shard_map/ppermute | solution.py:364
  143.6 7.6 %collective-permute-start.26 = (bf16[4,8,16,640]{3,2,1,0:T(8,128)(2,1)S(1)}, bf16[4,8,16,640]{3,2,1,0:T(8,128)(2,1)S(1)}, u32[]{:S(2)}, u32[]{:S(2)}) collective-permute-start(bf16[4,8,16,640]{3,2,1,0:T(8,128)(2,1)S(1)} %constant_dynamic-update-slice_fusion.mine), channel_id=1, source_target_pairs={{0,8},{8,0},{1,9},{9,1},{2,10},{10,2},{3,11},{11,3},{4,12},{12,4},... | collective-permute-start | bytes 1966088 | tf_op jit(solution)/shard_map/ppermute | solution.py:364
where the time goes:
time: 159 us; the launch traced here: 158 us
  starting transfers between devices  57.6 us (36%)
  Pallas kernels  48.9 us (31%)
  waiting for transfers between devices  37.2 us (23%)
  blocking collectives  7.84 us (5%)
  local copies, waits for them, and re-layouts  3.72 us (2%)
  other arithmetic  2.82 us (2%)
    ppermute x28, starting transfers between devices, shifted(): lax.ppermute(value, axis, [(i, (i + shift) % size) for i in range(size)])  50 us
    ppermute x28, waiting for transfers between devices, shifted(): lax.ppermute(value, axis, [(i, (i + shift) % size) for i in range(size)])  35.2 us
    pallas_call x4, Pallas kernels, product_step(): pl.pallas_call(kernel, grid=(4 if last else 1,), in_specs=[resident()] *...  24.8 us
    pallas_call x2, Pallas kernels, transform_call(): pl.pallas_call(kernel, grid_spec=pltpu.PrefetchScalarGridSpec(num_scalar_...  18.8 us
    all_to_all x1, blocking collectives, body(): lax.all_to_all(jnp.broadcast_to(valence, (8, *valence.shape)), NARROW, 0,...  7.84 us
    all_to_all x1, starting transfers between devices, body(): rows = lax.all_to_all(rows, WIDE, 0, 0, tiled=True)  7.59 us
    pallas_call x1, Pallas kernels, prepare(): pl.pallas_call(prepare_kernel, grid_spec=pltpu.PrefetchScalarGridSpec(num...  5.23 us
  transfers between devices with their start and end apart: 29, of which 16 were waited for; matrix products, arithmetic and copies ran while one was open for 3% of the time, Pallas kernels for 21%

commit v1 on v0

--- a/solution.py
+++ b/solution.py
@@ -341,7 +341,7 @@
         if last:
             quarter(pl.program_id(0))
         else:
-            pl.loop(0, 4)(quarter)
+            pl.loop(0, 4, unroll=2)(quarter)
 
     operands = [mine, theirs, scaled, hot, sign] + ([] if total is None else [total])
     aliases = {} if total is None or last else {5: 0}
@@ -399,8 +399,9 @@
     near_x = neighbours(rows, "x")
     near_zh = neighbours(cols, "zh")
     near_x, near_zh = lax.optimization_barrier((near_x, near_zh))
-    rows = [rows, near_x[0], jnp.concatenate(opposite(*near_x, "x")), near_x[1]]
-    cols = jnp.stack([cols, near_zh[0], jnp.concatenate(opposite(*near_zh, "zh")), near_zh[1]])
+    far_x, far_zh = lax.optimization_barrier((opposite(*near_x, "x"), opposite(*near_zh, "zh")))
+    rows = [rows, near_x[0], jnp.concatenate(far_x), near_x[1]]
+    cols = jnp.stack([cols, near_zh[0], jnp.concatenate(far_zh), near_zh[1]])
     near_y = neighbours(cols, "y")
     scaled, hot, sign = prepare(pos, omega, rows, gap, gmap, jnp.asarray(tables()[-1]))
     total = product_step(0, cols, shifted(cols, "co", 1), scaled, hot, sign, None, False)

time: 159 us -> 156 us (0.981)
  waiting for transfers between devices: 37.2 us -> 34.4 us
    ppermute x28, waiting for transfers between devices: 35.2 us -> 32.3 us  [shifted(): lax.ppermute(value, axis, [(i, (i + shift) % size) for i in range(size)])]
  transfers between devices with their start and end apart: 29 -> 29, of which waited for: 16 -> 15; matrix products, arithmetic and copies ran while one was open for 3% -> 4% of each run, Pallas kernels for 21% -> 21%
where the time goes in v1:
time: 156 us
  starting transfers between devices  58 us (37%)
  Pallas kernels  48.4 us (31%)
  waiting for transfers between devices  34.4 us (22%)
  blocking collectives  7.84 us (5%)
  local copies, waits for them, and re-layouts  3.72 us (2%)
  other arithmetic  2.83 us (2%)
    ppermute x28, starting transfers between devices, shifted(): lax.ppermute(value, axis, [(i, (i + shift) % size) for i in range(size)])  50.4 us
    ppermute x28, waiting for transfers between devices, shifted(): lax.ppermute(value, axis, [(i, (i + shift) % size) for i in range(size)])  32.3 us
    pallas_call x4, Pallas kernels, product_step(): pl.pallas_call(kernel, grid=(4 if last else 1,), in_specs=[resident()] *...  24.4 us
    pallas_call x2, Pallas kernels, transform_call(): pl.pallas_call(kernel, grid_spec=pltpu.PrefetchScalarGridSpec(num_scalar_...  18.8 us
    all_to_all x1, blocking collectives, body(): lax.all_to_all(jnp.broadcast_to(valence, (8, *valence.shape)), NARROW, 0,...  7.84 us
    all_to_all x1, starting transfers between devices, body(): rows = lax.all_to_all(rows, WIDE, 0, 0, tiled=True)  7.58 us
    pallas_call x1, Pallas kernels, prepare(): pl.pallas_call(prepare_kernel, grid_spec=pltpu.PrefetchScalarGridSpec(num...  5.24 us
  transfers between devices with their start and end apart: 29, of which 15 were waited for; matrix products, arithmetic and copies ran while one was open for 4% of the time, Pallas kernels for 21%

profile of v1, /device:TPU:1, one launch (start us, length us, event | category | flops | bytes accessed | tf_op | source)
XLA Modules:
  0.0 155.6 jit_solution(9190043467833528665)
XLA Ops:
  0.0 2.0 %collective-permute-start = (f32[256,128]{1,0:T(8,128)}, f32[256,128]{1,0:T(8,128)S(1)}, u32[]{:S(2)}, u32[]{:S(2)}) collective-permute-start(f32[256,128]{1,0:T(8,128)} %bitcast.45), channel_id=1, source_target_pairs={{0,1},{1,2},{2,3},{3,0},{4,5},{5,6},{6,7},{7,4},{8,9},{9,10},{10,1... | collective-permute-start | bytes 393224 | tf_op jit(solution)/shard_map/ppermute | solution.py:364
  2.0 2.5 %collective-permute-start.1 = (f32[256,128]{1,0:T(8,128)}, f32[256,128]{1,0:T(8,128)S(1)}, u32[]{:S(2)}, u32[]{:S(2)}) collective-permute-start(f32[256,128]{1,0:T(8,128)} %bitcast.46), channel_id=1, source_target_pairs={{0,2},{1,3},{2,0},{3,1},{4,6},{5,7},{6,4},{7,5},{8,10},{9,11},{10,... | collective-permute-start | bytes 393224 | tf_op jit(solution)/shard_map/ppermute | solution.py:364
  4.5 1.2 collective-permute-start.2
  5.6 0.7 broadcast_in_dim.4
  6.3 7.8 %all_to_all.10 = f32[8,8,128]{2,1,0:T(8,128)S(1)} all-to-all(f32[8,8,128]{2,1,0:T(8,128)S(1)} %broadcast_in_dim.4), channel_id=1, replica_groups=mesh['zh'=4,'y'=4,'co'=2,'zl'=2,'x'=4] {'zl','x'}, dimensions={0} | all-to-all | bytes 65536 | tf_op jit(solution)/shard_map/all_to_all | solution.py:383
  14.2 3.1 %collective-permute-start.3 = (f32[8,8,128]{2,1,0:T(8,128)S(1)}, f32[8,8,128]{2,1,0:T(8,128)S(1)}, u32[]{:S(2)}, u32[]{:S(2)}) collective-permute-start(f32[8,8,128]{2,1,0:T(8,128)S(1)} %all_to_all.10), channel_id=1, source_target_pairs={{0,64},{64,128},{128,192},{192,0},{1,65},{65,129},{129,193},{193,1... | collective-permute-start | bytes 98312 | tf_op jit(solution)/shard_map/ppermute | solution.py:364
  17.3 4.7 %collective-permute-start.4 = (f32[8,8,128]{2,1,0:T(8,128)S(1)}, f32[8,8,128]{2,1,0:T(8,128)S(1)}, u32[]{:S(2)}, u32[]{:S(2)}) collective-permute-start(f32[8,8,128]{2,1,0:T(8,128)S(1)} %all_to_all.10), channel_id=1, source_target_pairs={{0,128},{64,192},{128,0},{192,64},{1,129},{65,193},{129,1},{193,65... | collective-permute-start | bytes 98312 | tf_op jit(solution)/shard_map/ppermute | solution.py:364
  22.0 2.4 %collective-permute-start.5 = (f32[8,8,128]{2,1,0:T(8,128)S(1)}, f32[8,8,128]{2,1,0:T(8,128)S(1)}, u32[]{:S(2)}, u32[]{:S(2)}) collective-permute-start(f32[8,8,128]{2,1,0:T(8,128)S(1)} %all_to_all.10), channel_id=1, source_target_pairs={{0,192},{64,0},{128,64},{192,128},{1,193},{65,1},{129,65},{193,129... | collective-permute-start | bytes 98312 | tf_op jit(solution)/shard_map/ppermute | solution.py:364
  24.4 0.8 broadcast_subtract_fusion
  26.2 1.4 collective-permute-start.6
  27.5 2.6 %collective-permute-start.7 = (f32[4,8,8,128]{3,2,1,0:T(8,128)S(1)}, f32[4,8,8,128]{3,2,1,0:T(8,128)S(1)}, u32[]{:S(2)}, u32[]{:S(2)}) collective-permute-start(f32[4,8,8,128]{3,2,1,0:T(8,128)S(1)} %pad_maximum_fusion.5), channel_id=1, source_target_pairs={{0,32},{16,48},{32,0},{48,16},{1,33},{17,49},{33,1},{49,17},{2,34}... | collective-permute-start | bytes 393224 | tf_op jit(solution)/shard_map/ppermute | solution.py:364
  30.2 1.1 collective-permute-start.8
  31.3 2.6 %collective-permute-done.7 = f32[4,8,8,128]{3,2,1,0:T(8,128)S(1)} collective-permute-done((f32[4,8,8,128]{3,2,1,0:T(8,128)S(1)}, f32[4,8,8,128]{3,2,1,0:T(8,128)S(1)}, u32[]{:S(2)}, u32[]{:S(2)}) %collective-permute-start.7) | collective-permute-done | bytes 131104 | tf_op jit(solution)/shard_map/ppermute | solution.py:364
  34.0 6.2 %collective-permute-start.9 = (f32[4,4,8,8,128]{4,3,2,1,0:T(8,128)S(1)}, f32[4,4,8,8,128]{4,3,2,1,0:T(8,128)S(1)}, u32[]{:S(2)}, u32[]{:S(2)}) collective-permute-start(f32[4,4,8,8,128]{4,3,2,1,0:T(8,128)S(1)} %pad_maximum_fusion.1.refs_0_.refs_1_), channel_id=1, source_target_pairs={{0,8},{8,0},{1,9},{9,1},{2,10},{10,2},{3,11},{11,3},{4,12},{12,4},... | collective-permute-start | bytes 1572872 | tf_op jit(solution)/shard_map/ppermute | solution.py:364
  40.9 0.9 collective-permute-done.9.refs_1_.refs_2_
  41.7 0.8 copy-done.6
  42.5 8.8 %row_pairs.1 = (bf16[32,16,256]{2,1,0:T(8,128)(2,1)}, bf16[416,256]{1,0:T(8,128)(2,1)}) custom-call(s32[5]{0:T(128)} %stack.77.pos, f32[4,4,8,8,128]{4,3,2,1,0:T(8,128)} %copy-done.3, f32[4,4,8,8,128]{4,3,2,1,0:T(8,128)} %copy-done.6, f32[256,128]{1,0:T(8,128)} %bitcast.48, bf16[1024,512]{1,0:T(8,128)(2,1)} %constant.38.clone.refs_3_.refs_6_, ...), custom_call_target="tpu_custom_call" | custom-call | flops 4000000000 | bytes 6291456 | tf_op jit(solution)/shard_map/row_pairs/pallas_call | solution.py:229
  51.4 7.6 %all-to-all-start.1 = ((bf16[32,16,256]{2,1,0:T(8,128)(2,1)}), bf16[32,16,256]{2,1,0:T(8,128)(2,1)S(1)}, u32[]{:S(2)}, u32[]{:S(2)}) async-start(bf16[32,16,256]{2,1,0:T(8,128)(2,1)} %get-tuple-element.36), calls=%async_computation.1 | async-start | bytes 524288 | tf_op jit(solution)/shard_map/all_to_all | solution.py:392
  59.0 9.9 %column_pairs.1 = bf16[2,4,16,640]{3,2,1,0:T(8,128)(2,1)} custom-call(s32[5]{0:T(128)} %stack.77.pos, bf16[416,256]{1,0:T(8,128)(2,1)} %get-tuple-element.37.refs_0_, f32[4,4,8,8,128]{4,3,2,1,0:T(8,128)} %copy-done.3, f32[4,4,8,8,128]{4,3,2,1,0:T(8,128)} %copy-done.6, f32[256,128]{1,0:T(8,128)} %copy-done.7, f32[256,128]{1,0:T(8,128)} %copy-done.8, ...), custom_call_target="tpu_custom_call" | custom-call | flops 8000000000 | bytes 6291456 | tf_op jit(solution)/shard_map/column_pairs/pallas_call | solution.py:229
  69.0 0.9 slice_bitcast_fusion
  70.0 2.1 %all-to-all-done.1 = bf16[32,16,256]{2,1,0:T(8,128)(2,1)S(1)} async-done(((bf16[32,16,256]{2,1,0:T(8,128)(2,1)}), bf16[32,16,256]{2,1,0:T(8,128)(2,1)S(1)}, u32[]{:S(2)}, u32[]{:S(2)}) %all-to-all-start.1) | async-done | bytes 262176 | tf_op jit(solution)/shard_map/all_to_all | solution.py:392
  72.1 1.4 collective-permute-done.11
  73.5 0.9 broadcast_select_fusion.1
  74.4 5.7 %collective-permute-done.10 = bf16[32,16,256]{2,1,0:T(8,128)(2,1)S(1)} collective-permute-done((bf16[32,16,256]{2,1,0:T(8,128)(2,1)S(1)}, bf16[32,16,256]{2,1,0:T(8,128)(2,1)S(1)}, u32[]{:S(2)}, u32[]{:S(2)}) %collective-permute-start.10) | collective-permute-done | bytes 262176 | tf_op jit(solution)/shard_map/ppermute | solution.py:364
  80.6 2.4 %collective-permute-start.13 = (bf16[2,4,4,2,16,256]{5,4,3,2,1,0:T(8,128)(2,1)S(1)}, bf16[2,4,4,2,16,256]{5,4,3,2,1,0:T(8,128)(2,1)S(1)}, u32[]{:S(2)}, u32[]{:S(2)}) collective-permute-start(bf16[2,4,4,2,16,256]{5,4,3,2,1,0:T(8,128)(2,1)S(1)} %pad_maximum_fusion.2.r0), channel_id=1, source_target_pairs={{0,3},{1,0},{2,1},{3,2},{4,7},{5,4},{6,5},{7,6},{8,11},{9,8},{10,9... | collective-permute-start | bytes 1572872 | tf_op jit(solution)/shard_map/ppermute | solution.py:364
  83.0 1.6 %collective-permute-start.14 = (bf16[8,16,640]{2,1,0:T(8,128)(2,1)S(1)}, bf16[8,16,640]{2,1,0:T(8,128)(2,1)S(1)}, u32[]{:S(2)}, u32[]{:S(2)}) collective-permute-start(bf16[8,16,640]{2,1,0:T(8,128)(2,1)S(1)} %pad_maximum_fusion.4), channel_id=1, source_target_pairs={{0,64},{64,128},{128,192},{192,0},{1,65},{65,129},{129,193},{193,1... | collective-permute-start | bytes 491528 | tf_op jit(solution)/shard_map/ppermute | solution.py:364
  84.5 2.0 %collective-permute-start.15 = (bf16[8,16,640]{2,1,0:T(8,128)(2,1)S(1)}, bf16[8,16,640]{2,1,0:T(8,128)(2,1)S(1)}, u32[]{:S(2)}, u32[]{:S(2)}) collective-permute-start(bf16[8,16,640]{2,1,0:T(8,128)(2,1)S(1)} %pad_maximum_fusion.4), channel_id=1, source_target_pairs={{0,192},{64,0},{128,64},{192,128},{1,193},{65,1},{129,65},{193,129... | collective-permute-start | bytes 491528 | tf_op jit(solution)/shard_map/ppermute | solution.py:364
  86.6 7.5 %collective-permute-done.14 = bf16[8,16,640]{2,1,0:T(8,128)(2,1)S(1)} collective-permute-done((bf16[8,16,640]{2,1,0:T(8,128)(2,1)S(1)}, bf16[8,16,640]{2,1,0:T(8,128)(2,1)S(1)}, u32[]{:S(2)}, u32[]{:S(2)}) %collective-permute-start.14) | collective-permute-done | bytes 163872 | tf_op jit(solution)/shard_map/ppermute | solution.py:364
  94.0 1.4 collective-permute-done.15
  95.4 1.3 collective-permute-start.16
  97.1 2.5 %collective-permute-start.18 = (bf16[4,16,640]{2,1,0:T(8,128)(2,1)S(1)}, bf16[4,16,640]{2,1,0:T(8,128)(2,1)S(1)}, u32[]{:S(2)}, u32[]{:S(2)}) collective-permute-start(bf16[4,16,640]{2,1,0:T(8,128)(2,1)S(1)} %slice.28), channel_id=1, source_target_pairs={{0,192},{64,0},{128,64},{192,128},{1,193},{65,1},{129,65},{193,129... | collective-permute-start | bytes 245768 | tf_op jit(solution)/shard_map/ppermute | solution.py:364
  99.7 2.1 %collective-permute-done.18 = bf16[4,16,640]{2,1,0:T(8,128)(2,1)S(1)} collective-permute-done((bf16[4,16,640]{2,1,0:T(8,128)(2,1)S(1)}, bf16[4,16,640]{2,1,0:T(8,128)(2,1)S(1)}, u32[]{:S(2)}, u32[]{:S(2)}) %collective-permute-start.18) | collective-permute-done | bytes 81952 | tf_op jit(solution)/shard_map/ppermute | solution.py:364
  101.8 3.4 %collective-permute-done.19 = bf16[4,16,640]{2,1,0:T(8,128)(2,1)S(1)} collective-permute-done((bf16[4,16,640]{2,1,0:T(8,128)(2,1)S(1)}, bf16[4,16,640]{2,1,0:T(8,128)(2,1)S(1)}, u32[]{:S(2)}, u32[]{:S(2)}) %collective-permute-start.19) | collective-permute-done | bytes 81952 | tf_op jit(solution)/shard_map/ppermute | solution.py:364
  105.4 4.0 %collective-permute-start.20 = (bf16[4,8,16,640]{3,2,1,0:T(8,128)(2,1)S(1)}, bf16[4,8,16,640]{3,2,1,0:T(8,128)(2,1)S(1)}, u32[]{:S(2)}, u32[]{:S(2)}) collective-permute-start(bf16[4,8,16,640]{3,2,1,0:T(8,128)(2,1)S(1)} %pad_maximum_fusion.mine), channel_id=1, source_target_pairs={{0,8},{8,0},{1,9},{9,1},{2,10},{10,2},{3,11},{11,3},{4,12},{12,4},... | collective-permute-start | bytes 1966088 | tf_op jit(solution)/shard_map/ppermute | solution.py:364
  109.4 1.2 collective-permute-start.21
  110.6 1.5 collective-permute-start.22
  112.1 0.9 pad_maximum_fusion.3.r2
  113.0 5.2 %scaled_rows.1 = (bf16[4,1536,1024]{2,1,0:T(8,128)(2,1)S(1)}, bf16[4,640,256]{2,1,0:T(8,128)(2,1)S(1)}, f32[4,16,256]{2,1,0:T(8,128)S(1)}) custom-call(s32[5]{0:T(128)S(1)} %copy-done, f32[6]{0:T(128)S(1)} %copy-done.1, bf16[2,4,4,2,16,256]{5,4,3,2,1,0:T(8,128)(2,1)} %copy-done.2, bf16[2,4,4,2,16,256]{5,4,3,2,1,0:T(8,128)(2,1)} %copy-done.4, ...), custom_call_target="tpu_custom_call" | custom-call | flops 1000000000 | bytes 20971520 | tf_op jit(solution)/shard_map/scaled_rows/pallas_call | solution.py:303
  118.2 5.4 %response_product.4.refs_0_ = f32[6,256,1024]{2,1,0:T(8,128)S(1)} custom-call(bf16[4,8,16,640]{3,2,1,0:T(8,128)(2,1)S(1)} %pad_maximum_fusion.mine, bf16[4,8,16,640]{3,2,1,0:T(8,128)(2,1)S(1)} %collective-permute-done.20.theirs, bf16[4,1536,1024]{2,1,0:T(8,128)(2,1)S(1)} %get-tuple-element.52.scaled, bf16[4,640,256]{2,1,0:T(8,128)(2,1)S(1)} %get-tuple-element.53.hot, ...), custom_call_target="tpu_custom_call" | custom-call | flops 4600000000 | bytes 10485760 | tf_op jit(solution)/shard_map/response_product/pallas_call | solution.py:348
  123.7 2.9 %collective-permute-done.21.mine = bf16[4,8,16,640]{3,2,1,0:T(8,128)(2,1)S(1)} collective-permute-done((bf16[4,8,16,640]{3,2,1,0:T(8,128)(2,1)S(1)}, bf16[4,8,16,640]{3,2,1,0:T(8,128)(2,1)S(1)}, u32[]{:S(2)}, u32[]{:S(2)}) %collective-permute-start.21) | collective-permute-done | bytes 655392 | tf_op jit(solution)/shard_map/ppermute | solution.py:364
  126.6 1.1 collective-permute-start.23
  127.9 2.8 %collective-permute-start.24 = (bf16[2,8,16,640]{3,2,1,0:T(8,128)(2,1)S(1)}, bf16[2,8,16,640]{3,2,1,0:T(8,128)(2,1)S(1)}, u32[]{:S(2)}, u32[]{:S(2)}) collective-permute-start(bf16[2,8,16,640]{3,2,1,0:T(8,128)(2,1)S(1)} %slice.30), channel_id=1, source_target_pairs={{0,48},{16,0},{32,16},{48,32},{1,49},{17,1},{33,17},{49,33},{2,50}... | collective-permute-start | bytes 983048 | tf_op jit(solution)/shard_map/ppermute | solution.py:364
  130.7 5.9 %response_product.5.refs_0_ = f32[6,256,1024]{2,1,0:T(8,128)S(1)} custom-call(bf16[4,8,16,640]{3,2,1,0:T(8,128)(2,1)S(1)} %collective-permute-done.21.mine, bf16[4,8,16,640]{3,2,1,0:T(8,128)(2,1)S(1)} %collective-permute-done.23.theirs, bf16[4,1536,1024]{2,1,0:T(8,128)(2,1)S(1)} %get-tuple-element.52.scaled, ...), custom_call_target="tpu_custom_call", output_to_operand_aliasing={{}: (5, {})} | custom-call | flops 4600000000 | bytes 10485760 | tf_op jit(solution)/shard_map/response_product/pallas_call | solution.py:348
  136.6 0.8 collective-permute-done.24
  137.3 3.1 %collective-permute-done.25 = bf16[2,8,16,640]{3,2,1,0:T(8,128)(2,1)S(1)} collective-permute-done((bf16[2,8,16,640]{3,2,1,0:T(8,128)(2,1)S(1)}, bf16[2,8,16,640]{3,2,1,0:T(8,128)(2,1)S(1)}, u32[]{:S(2)}, u32[]{:S(2)}) %collective-permute-start.25) | collective-permute-done | bytes 327712 | tf_op jit(solution)/shard_map/ppermute | solution.py:364
  140.5 1.9 %collective-permute-start.26 = (bf16[4,8,16,640]{3,2,1,0:T(8,128)(2,1)S(1)}, bf16[4,8,16,640]{3,2,1,0:T(8,128)(2,1)S(1)}, u32[]{:S(2)}, u32[]{:S(2)}) collective-permute-start(bf16[4,8,16,640]{3,2,1,0:T(8,128)(2,1)S(1)} %constant_dynamic-update-slice_fusion.mine), channel_id=1, source_target_pairs={{0,8},{8,0},{1,9},{9,1},{2,10},{10,2},{3,11},{11,3},{4,12},{12,4},... | collective-permute-start | bytes 1966088 | tf_op jit(solution)/shard_map/ppermute | solution.py:364
  142.4 5.9 %response_product.6.refs_0_ = f32[6,256,1024]{2,1,0:T(8,128)S(1)} custom-call(bf16[4,8,16,640]{3,2,1,0:T(8,128)(2,1)S(1)} %collective-permute-done.22.mine, bf16[4,8,16,640]{3,2,1,0:T(8,128)(2,1)S(1)} %collective-permute-done.27.theirs, bf16[4,1536,1024]{2,1,0:T(8,128)(2,1)S(1)} %get-tuple-element.52.scaled, ...), custom_call_target="tpu_custom_call", output_to_operand_aliasing={{}: (5, {})} | custom-call | flops 4600000000 | bytes 10485760 | tf_op jit(solution)/shard_map/response_product/pallas_call | solution.py:348
  148.3 7.2 %response_product.7 = f32[6,256,1024]{2,1,0:T(8,128)} custom-call(bf16[4,8,16,640]{3,2,1,0:T(8,128)(2,1)S(1)} %constant_dynamic-update-slice_fusion.mine, bf16[4,8,16,640]{3,2,1,0:T(8,128)(2,1)S(1)} %collective-permute-done.26.theirs, bf16[4,1536,1024]{2,1,0:T(8,128)(2,1)S(1)} %get-tuple-element.52.scaled, bf16[4,640,256]{2,1,0:T(8,128)(2,1)S(1)} %get-tuple-element.53.hot, ...), custom_call_target="tpu_custom_call" | custom-call | flops 4600000000 | bytes 10485760 | tf_op jit(solution)/shard_map/response_product/pallas_call | solution.py:348
  (60 shorter events, 3.3 us)
Async XLA Ops:
  0.0 14.2 %collective-permute-start = (f32[256,128]{1,0:T(8,128)}, f32[256,128]{1,0:T(8,128)S(1)}, u32[]{:S(2)}, u32[]{:S(2)}) collective-permute-start(f32[256,128]{1,0:T(8,128)} %bitcast.45), channel_id=1, source_target_pairs={{0,1},{1,2},{2,3},{3,0},{4,5},{5,6},{6,7},{7,4},{8,9},{9,10},{10,1... | collective-permute-start | bytes 393224 | tf_op jit(solution)/shard_map/ppermute | solution.py:364
  2.0 12.1 %collective-permute-start.1 = (f32[256,128]{1,0:T(8,128)}, f32[256,128]{1,0:T(8,128)S(1)}, u32[]{:S(2)}, u32[]{:S(2)}) collective-permute-start(f32[256,128]{1,0:T(8,128)} %bitcast.46), channel_id=1, source_target_pairs={{0,2},{1,3},{2,0},{3,1},{4,6},{5,7},{6,4},{7,5},{8,10},{9,11},{10,... | collective-permute-start | bytes 393224 | tf_op jit(solution)/shard_map/ppermute | solution.py:364
  4.5 9.7 %collective-permute-start.2 = (f32[256,128]{1,0:T(8,128)}, f32[256,128]{1,0:T(8,128)S(1)}, u32[]{:S(2)}, u32[]{:S(2)}) collective-permute-start(f32[256,128]{1,0:T(8,128)} %bitcast.47), channel_id=1, source_target_pairs={{0,3},{1,0},{2,1},{3,2},{4,7},{5,4},{6,5},{7,6},{8,11},{9,8},{10,9... | collective-permute-start | bytes 393224 | tf_op jit(solution)/shard_map/ppermute | solution.py:364
  14.2 37.2 %copy-start.7 = (f32[256,128]{1,0:T(8,128)}, f32[256,128]{1,0:T(8,128)S(1)}, u32[]{:S(2)}) copy-start(f32[256,128]{1,0:T(8,128)S(1)} %collective-permute-done.refs_3_) | copy-start | bytes 393220
  14.2 37.2 %copy-start.8 = (f32[256,128]{1,0:T(8,128)}, f32[256,128]{1,0:T(8,128)S(1)}, u32[]{:S(2)}) copy-start(f32[256,128]{1,0:T(8,128)S(1)} %collective-permute-done.1.refs_4_) | copy-start | bytes 393220
  14.2 37.2 %copy-start.9 = (f32[256,128]{1,0:T(8,128)}, f32[256,128]{1,0:T(8,128)S(1)}, u32[]{:S(2)}) copy-start(f32[256,128]{1,0:T(8,128)S(1)} %collective-permute-done.2.refs_5_) | copy-start | bytes 393220
  14.2 11.5 %collective-permute-start.3 = (f32[8,8,128]{2,1,0:T(8,128)S(1)}, f32[8,8,128]{2,1,0:T(8,128)S(1)}, u32[]{:S(2)}, u32[]{:S(2)}) collective-permute-start(f32[8,8,128]{2,1,0:T(8,128)S(1)} %all_to_all.10), channel_id=1, source_target_pairs={{0,64},{64,128},{128,192},{192,0},{1,65},{65,129},{129,193},{193,1... | collective-permute-start | bytes 98312 | tf_op jit(solution)/shard_map/ppermute | solution.py:364
  17.3 8.4 %collective-permute-start.4 = (f32[8,8,128]{2,1,0:T(8,128)S(1)}, f32[8,8,128]{2,1,0:T(8,128)S(1)}, u32[]{:S(2)}, u32[]{:S(2)}) collective-permute-start(f32[8,8,128]{2,1,0:T(8,128)S(1)} %all_to_all.10), channel_id=1, source_target_pairs={{0,128},{64,192},{128,0},{192,64},{1,129},{65,193},{129,1},{193,65... | collective-permute-start | bytes 98312 | tf_op jit(solution)/shard_map/ppermute | solution.py:364
  22.0 4.1 %collective-permute-start.5 = (f32[8,8,128]{2,1,0:T(8,128)S(1)}, f32[8,8,128]{2,1,0:T(8,128)S(1)}, u32[]{:S(2)}, u32[]{:S(2)}) collective-permute-start(f32[8,8,128]{2,1,0:T(8,128)S(1)} %all_to_all.10), channel_id=1, source_target_pairs={{0,192},{64,0},{128,64},{192,128},{1,193},{65,1},{129,65},{193,129... | collective-permute-start | bytes 98312 | tf_op jit(solution)/shard_map/ppermute | solution.py:364
  26.2 5.2 %collective-permute-start.6 = (f32[4,8,8,128]{3,2,1,0:T(8,128)S(1)}, f32[4,8,8,128]{3,2,1,0:T(8,128)S(1)}, u32[]{:S(2)}, u32[]{:S(2)}) collective-permute-start(f32[4,8,8,128]{3,2,1,0:T(8,128)S(1)} %pad_maximum_fusion.5), channel_id=1, source_target_pairs={{0,16},{16,32},{32,48},{48,0},{1,17},{17,33},{33,49},{49,1},{2,18}... | collective-permute-start | bytes 393224 | tf_op jit(solution)/shard_map/ppermute | solution.py:364
  27.5 6.4 %collective-permute-start.7 = (f32[4,8,8,128]{3,2,1,0:T(8,128)S(1)}, f32[4,8,8,128]{3,2,1,0:T(8,128)S(1)}, u32[]{:S(2)}, u32[]{:S(2)}) collective-permute-start(f32[4,8,8,128]{3,2,1,0:T(8,128)S(1)} %pad_maximum_fusion.5), channel_id=1, source_target_pairs={{0,32},{16,48},{32,0},{48,16},{1,33},{17,49},{33,1},{49,17},{2,34}... | collective-permute-start | bytes 393224 | tf_op jit(solution)/shard_map/ppermute | solution.py:364
  30.2 3.8 %collective-permute-start.8 = (f32[4,8,8,128]{3,2,1,0:T(8,128)S(1)}, f32[4,8,8,128]{3,2,1,0:T(8,128)S(1)}, u32[]{:S(2)}, u32[]{:S(2)}) collective-permute-start(f32[4,8,8,128]{3,2,1,0:T(8,128)S(1)} %pad_maximum_fusion.5), channel_id=1, source_target_pairs={{0,48},{16,0},{32,16},{48,32},{1,49},{17,1},{33,17},{49,33},{2,50}... | collective-permute-start | bytes 393224 | tf_op jit(solution)/shard_map/ppermute | solution.py:364
  34.0 7.7 %copy-start.3 = (f32[4,4,8,8,128]{4,3,2,1,0:T(8,128)}, f32[4,4,8,8,128]{4,3,2,1,0:T(8,128)S(1)}, u32[]{:S(2)}) copy-start(f32[4,4,8,8,128]{4,3,2,1,0:T(8,128)S(1)} %pad_maximum_fusion.1.refs_0_.refs_1_) | copy-start | bytes 1572868
  34.0 7.7 %collective-permute-start.9 = (f32[4,4,8,8,128]{4,3,2,1,0:T(8,128)S(1)}, f32[4,4,8,8,128]{4,3,2,1,0:T(8,128)S(1)}, u32[]{:S(2)}, u32[]{:S(2)}) collective-permute-start(f32[4,4,8,8,128]{4,3,2,1,0:T(8,128)S(1)} %pad_maximum_fusion.1.refs_0_.refs_1_), channel_id=1, source_target_pairs={{0,8},{8,0},{1,9},{9,1},{2,10},{10,2},{3,11},{11,3},{4,12},{12,4},... | collective-permute-start | bytes 1572872 | tf_op jit(solution)/shard_map/ppermute | solution.py:364
  41.7 0.8 copy-start.6
  51.4 20.7 %all-to-all-start.1 = ((bf16[32,16,256]{2,1,0:T(8,128)(2,1)}), bf16[32,16,256]{2,1,0:T(8,128)(2,1)S(1)}, u32[]{:S(2)}, u32[]{:S(2)}) async-start(bf16[32,16,256]{2,1,0:T(8,128)(2,1)} %get-tuple-element.36), calls=%async_computation.1 | async-start | bytes 524288 | tf_op jit(solution)/shard_map/all_to_all | solution.py:392
  59.0 54.0 %copy-start = (s32[5]{0:T(128)S(1)}, s32[5]{0:T(128)}, u32[]{:S(2)}) copy-start(s32[5]{0:T(128)} %stack.77.pos) | copy-start | bytes 64
  59.0 54.0 %copy-start.1 = (f32[6]{0:T(128)S(1)}, f32[6]{0:T(128)}, u32[]{:S(2)}) copy-start(f32[6]{0:T(128)} %omega.1) | copy-start | bytes 76
  69.9 3.6 %collective-permute-start.11 = (bf16[4,16,640]{2,1,0:T(8,128)(2,1)S(1)}, bf16[4,16,640]{2,1,0:T(8,128)(2,1)S(1)}, u32[]{:S(2)}, u32[]{:S(2)}) collective-permute-start(bf16[4,16,640]{2,1,0:T(8,128)(2,1)S(1)} %slice_bitcast_fusion), channel_id=1, source_target_pairs={{0,4},{4,0},{1,5},{5,1},{2,6},{6,2},{3,7},{7,3},{8,12},{12,8},{9,1... | collective-permute-start | bytes 245768 | tf_op jit(solution)/shard_map/ppermute | solution.py:364
  72.1 8.1 %collective-permute-start.10 = (bf16[32,16,256]{2,1,0:T(8,128)(2,1)S(1)}, bf16[32,16,256]{2,1,0:T(8,128)(2,1)S(1)}, u32[]{:S(2)}, u32[]{:S(2)}) collective-permute-start(bf16[32,16,256]{2,1,0:T(8,128)(2,1)S(1)} %all-to-all-done.1), channel_id=1, source_target_pairs={{0,4},{4,0},{1,5},{5,1},{2,6},{6,2},{3,7},{7,3},{8,12},{12,8},{9,1... | collective-permute-start | bytes 786440 | tf_op jit(solution)/shard_map/ppermute | solution.py:364
  80.2 32.7 %copy-start.2 = (bf16[2,4,4,2,16,256]{5,4,3,2,1,0:T(8,128)(2,1)}, bf16[2,4,4,2,16,256]{5,4,3,2,1,0:T(8,128)(2,1)S(1)}, u32[]{:S(2)}) copy-start(bf16[2,4,4,2,16,256]{5,4,3,2,1,0:T(8,128)(2,1)S(1)} %pad_maximum_fusion.2.r0) | copy-start | bytes 1572868
  80.2 15.2 %collective-permute-start.12 = (bf16[2,4,4,2,16,256]{5,4,3,2,1,0:T(8,128)(2,1)S(1)}, bf16[2,4,4,2,16,256]{5,4,3,2,1,0:T(8,128)(2,1)S(1)}, u32[]{:S(2)}, u32[]{:S(2)}) collective-permute-start(bf16[2,4,4,2,16,256]{5,4,3,2,1,0:T(8,128)(2,1)S(1)} %pad_maximum_fusion.2.r0), channel_id=1, source_target_pairs={{0,1},{1,2},{2,3},{3,0},{4,5},{5,6},{6,7},{7,4},{8,9},{9,10},{10,1... | collective-permute-start | bytes 1572872 | tf_op jit(solution)/shard_map/ppermute | solution.py:364
  80.6 14.8 %collective-permute-start.13 = (bf16[2,4,4,2,16,256]{5,4,3,2,1,0:T(8,128)(2,1)S(1)}, bf16[2,4,4,2,16,256]{5,4,3,2,1,0:T(8,128)(2,1)S(1)}, u32[]{:S(2)}, u32[]{:S(2)}) collective-permute-start(bf16[2,4,4,2,16,256]{5,4,3,2,1,0:T(8,128)(2,1)S(1)} %pad_maximum_fusion.2.r0), channel_id=1, source_target_pairs={{0,3},{1,0},{2,1},{3,2},{4,7},{5,4},{6,5},{7,6},{8,11},{9,8},{10,9... | collective-permute-start | bytes 1572872 | tf_op jit(solution)/shard_map/ppermute | solution.py:364
  83.0 11.0 %collective-permute-start.14 = (bf16[8,16,640]{2,1,0:T(8,128)(2,1)S(1)}, bf16[8,16,640]{2,1,0:T(8,128)(2,1)S(1)}, u32[]{:S(2)}, u32[]{:S(2)}) collective-permute-start(bf16[8,16,640]{2,1,0:T(8,128)(2,1)S(1)} %pad_maximum_fusion.4), channel_id=1, source_target_pairs={{0,64},{64,128},{128,192},{192,0},{1,65},{65,129},{129,193},{193,1... | collective-permute-start | bytes 491528 | tf_op jit(solution)/shard_map/ppermute | solution.py:364
  84.5 10.9 %collective-permute-start.15 = (bf16[8,16,640]{2,1,0:T(8,128)(2,1)S(1)}, bf16[8,16,640]{2,1,0:T(8,128)(2,1)S(1)}, u32[]{:S(2)}, u32[]{:S(2)}) collective-permute-start(bf16[8,16,640]{2,1,0:T(8,128)(2,1)S(1)} %pad_maximum_fusion.4), channel_id=1, source_target_pairs={{0,192},{64,0},{128,64},{192,128},{1,193},{65,1},{129,65},{193,129... | collective-permute-start | bytes 491528 | tf_op jit(solution)/shard_map/ppermute | solution.py:364
  95.4 17.5 %copy-start.4 = (bf16[2,4,4,2,16,256]{5,4,3,2,1,0:T(8,128)(2,1)}, bf16[2,4,4,2,16,256]{5,4,3,2,1,0:T(8,128)(2,1)S(1)}, u32[]{:S(2)}) copy-start(bf16[2,4,4,2,16,256]{5,4,3,2,1,0:T(8,128)(2,1)S(1)} %collective-permute-done.12.r1) | copy-start | bytes 1572868
  95.4 17.5 %copy-start.5 = (bf16[2,4,4,2,16,256]{5,4,3,2,1,0:T(8,128)(2,1)}, bf16[2,4,4,2,16,256]{5,4,3,2,1,0:T(8,128)(2,1)S(1)}, u32[]{:S(2)}) copy-start(bf16[2,4,4,2,16,256]{5,4,3,2,1,0:T(8,128)(2,1)S(1)} %collective-permute-done.13.r3) | copy-start | bytes 1572868
  95.4 9.8 %collective-permute-start.16 = (bf16[1,4,4,2,16,256]{5,4,3,2,1,0:T(8,128)(2,1)S(1)}, bf16[1,4,4,2,16,256]{5,4,3,2,1,0:T(8,128)(2,1)S(1)}, u32[]{:S(2)}, u32[]{:S(2)}) collective-permute-start(bf16[1,4,4,2,16,256]{5,4,3,2,1,0:T(8,128)(2,1)S(1)} %slice.26), channel_id=1, source_target_pairs={{0,3},{1,0},{2,1},{3,2},{4,7},{5,4},{6,5},{7,6},{8,11},{9,8},{10,9... | collective-permute-start | bytes 786440 | tf_op jit(solution)/shard_map/ppermute | solution.py:364
  96.8 8.4 %collective-permute-start.17 = (bf16[1,4,4,2,16,256]{5,4,3,2,1,0:T(8,128)(2,1)S(1)}, bf16[1,4,4,2,16,256]{5,4,3,2,1,0:T(8,128)(2,1)S(1)}, u32[]{:S(2)}, u32[]{:S(2)}) collective-permute-start(bf16[1,4,4,2,16,256]{5,4,3,2,1,0:T(8,128)(2,1)S(1)} %slice.27), channel_id=1, source_target_pairs={{0,1},{1,2},{2,3},{3,0},{4,5},{5,6},{6,7},{7,4},{8,9},{9,10},{10,1... | collective-permute-start | bytes 786440 | tf_op jit(solution)/shard_map/ppermute | solution.py:364
  97.1 4.7 %collective-permute-start.18 = (bf16[4,16,640]{2,1,0:T(8,128)(2,1)S(1)}, bf16[4,16,640]{2,1,0:T(8,128)(2,1)S(1)}, u32[]{:S(2)}, u32[]{:S(2)}) collective-permute-start(bf16[4,16,640]{2,1,0:T(8,128)(2,1)S(1)} %slice.28), channel_id=1, source_target_pairs={{0,192},{64,0},{128,64},{192,128},{1,193},{65,1},{129,65},{193,129... | collective-permute-start | bytes 245768 | tf_op jit(solution)/shard_map/ppermute | solution.py:364
  99.6 5.6 %collective-permute-start.19 = (bf16[4,16,640]{2,1,0:T(8,128)(2,1)S(1)}, bf16[4,16,640]{2,1,0:T(8,128)(2,1)S(1)}, u32[]{:S(2)}, u32[]{:S(2)}) collective-permute-start(bf16[4,16,640]{2,1,0:T(8,128)(2,1)S(1)} %slice.29), channel_id=1, source_target_pairs={{0,64},{64,128},{128,192},{192,0},{1,65},{65,129},{129,193},{193,1... | collective-permute-start | bytes 245768 | tf_op jit(solution)/shard_map/ppermute | solution.py:364
  105.4 12.9 %collective-permute-start.20 = (bf16[4,8,16,640]{3,2,1,0:T(8,128)(2,1)S(1)}, bf16[4,8,16,640]{3,2,1,0:T(8,128)(2,1)S(1)}, u32[]{:S(2)}, u32[]{:S(2)}) collective-permute-start(bf16[4,8,16,640]{3,2,1,0:T(8,128)(2,1)S(1)} %pad_maximum_fusion.mine), channel_id=1, source_target_pairs={{0,8},{8,0},{1,9},{9,1},{2,10},{10,2},{3,11},{11,3},{4,12},{12,4},... | collective-permute-start | bytes 1966088 | tf_op jit(solution)/shard_map/ppermute | solution.py:364
  109.4 17.2 %collective-permute-start.21 = (bf16[4,8,16,640]{3,2,1,0:T(8,128)(2,1)S(1)}, bf16[4,8,16,640]{3,2,1,0:T(8,128)(2,1)S(1)}, u32[]{:S(2)}, u32[]{:S(2)}) collective-permute-start(bf16[4,8,16,640]{3,2,1,0:T(8,128)(2,1)S(1)} %pad_maximum_fusion.mine), channel_id=1, source_target_pairs={{0,16},{16,32},{32,48},{48,0},{1,17},{17,33},{33,49},{49,1},{2,18}... | collective-permute-start | bytes 1966088 | tf_op jit(solution)/shard_map/ppermute | solution.py:364
  110.6 16.0 %collective-permute-start.22 = (bf16[4,8,16,640]{3,2,1,0:T(8,128)(2,1)S(1)}, bf16[4,8,16,640]{3,2,1,0:T(8,128)(2,1)S(1)}, u32[]{:S(2)}, u32[]{:S(2)}) collective-permute-start(bf16[4,8,16,640]{3,2,1,0:T(8,128)(2,1)S(1)} %pad_maximum_fusion.mine), channel_id=1, source_target_pairs={{0,48},{16,0},{32,16},{48,32},{1,49},{17,1},{33,17},{49,33},{2,50}... | collective-permute-start | bytes 1966088 | tf_op jit(solution)/shard_map/ppermute | solution.py:364
  126.6 4.1 %collective-permute-start.23 = (bf16[4,8,16,640]{3,2,1,0:T(8,128)(2,1)S(1)}, bf16[4,8,16,640]{3,2,1,0:T(8,128)(2,1)S(1)}, u32[]{:S(2)}, u32[]{:S(2)}) collective-permute-start(bf16[4,8,16,640]{3,2,1,0:T(8,128)(2,1)S(1)} %collective-permute-done.21.mine), channel_id=1, source_target_pairs={{0,8},{8,0},{1,9},{9,1},{2,10},{10,2},{3,11},{11,3},{4,12},{12,4},... | collective-permute-start | bytes 1966088 | tf_op jit(solution)/shard_map/ppermute | solution.py:364
  127.8 14.6 %collective-permute-start.27 = (bf16[4,8,16,640]{3,2,1,0:T(8,128)(2,1)S(1)}, bf16[4,8,16,640]{3,2,1,0:T(8,128)(2,1)S(1)}, u32[]{:S(2)}, u32[]{:S(2)}) collective-permute-start(bf16[4,8,16,640]{3,2,1,0:T(8,128)(2,1)S(1)} %collective-permute-done.22.mine), channel_id=1, source_target_pairs={{0,8},{8,0},{1,9},{9,1},{2,10},{10,2},{3,11},{11,3},{4,12},{12,4},... | collective-permute-start | bytes 1966088 | tf_op jit(solution)/shard_map/ppermute | solution.py:364
  127.9 9.4 %collective-permute-start.24 = (bf16[2,8,16,640]{3,2,1,0:T(8,128)(2,1)S(1)}, bf16[2,8,16,640]{3,2,1,0:T(8,128)(2,1)S(1)}, u32[]{:S(2)}, u32[]{:S(2)}) collective-permute-start(bf16[2,8,16,640]{3,2,1,0:T(8,128)(2,1)S(1)} %slice.30), channel_id=1, source_target_pairs={{0,48},{16,0},{32,16},{48,32},{1,49},{17,1},{33,17},{49,33},{2,50}... | collective-permute-start | bytes 983048 | tf_op jit(solution)/shard_map/ppermute | solution.py:364
  130.7 9.8 %collective-permute-start.25 = (bf16[2,8,16,640]{3,2,1,0:T(8,128)(2,1)S(1)}, bf16[2,8,16,640]{3,2,1,0:T(8,128)(2,1)S(1)}, u32[]{:S(2)}, u32[]{:S(2)}) collective-permute-start(bf16[2,8,16,640]{3,2,1,0:T(8,128)(2,1)S(1)} %slice.31), channel_id=1, source_target_pairs={{0,16},{16,32},{32,48},{48,0},{1,17},{17,33},{33,49},{49,1},{2,18}... | collective-permute-start | bytes 983048 | tf_op jit(solution)/shard_map/ppermute | solution.py:364
  140.5 7.8 %collective-permute-start.26 = (bf16[4,8,16,640]{3,2,1,0:T(8,128)(2,1)S(1)}, bf16[4,8,16,640]{3,2,1,0:T(8,128)(2,1)S(1)}, u32[]{:S(2)}, u32[]{:S(2)}) collective-permute-start(bf16[4,8,16,640]{3,2,1,0:T(8,128)(2,1)S(1)} %constant_dynamic-update-slice_fusion.mine), channel_id=1, source_target_pairs={{0,8},{8,0},{1,9},{9,1},{2,10},{10,2},{3,11},{11,3},{4,12},{12,4},... | collective-permute-start | bytes 1966088 | tf_op jit(solution)/shard_map/ppermute | solution.py:364

commit v2 on v1

--- a/solution.py
+++ b/solution.py
@@ -404,9 +404,9 @@
     cols = jnp.stack([cols, near_zh[0], jnp.concatenate(far_zh), near_zh[1]])
     near_y = neighbours(cols, "y")
     scaled, hot, sign = prepare(pos, omega, rows, gap, gmap, jnp.asarray(tables()[-1]))
+    scaled, hot, sign, near_y = lax.optimization_barrier((scaled, hot, sign, near_y))
+    far = opposite(*near_y, "y")
     total = product_step(0, cols, shifted(cols, "co", 1), scaled, hot, sign, None, False)
-    total, near_y = lax.optimization_barrier((total, near_y))
-    far = opposite(*near_y, "y")
     total = product_step(1, near_y[0], shifted(near_y[0], "co", 1), scaled, hot, sign, total, False)
     total, far = lax.optimization_barrier((total, far))
     for sy, mine in ((3, near_y[1]), (2, jnp.concatenate(far))):

time: 156 us -> 153 us (0.981)
  waiting for transfers between devices: 34.4 us -> 27.8 us
  starting transfers between devices: 58 us -> 61.4 us
    ppermute x28, waiting for transfers between devices: 32.3 us -> 25.7 us  [shifted(): lax.ppermute(value, axis, [(i, (i + shift) % size) for i in range(size)])]
    ppermute x28, starting transfers between devices: 50.4 us -> 53.9 us  [shifted(): lax.ppermute(value, axis, [(i, (i + shift) % size) for i in range(size)])]
  transfers between devices with their start and end apart: 29 -> 29, of which waited for: 15 -> 13; matrix products, arithmetic and copies ran while one was open for 4% -> 4% of each run, Pallas kernels for 21% -> 21%
where the time goes in v2:
time: 153 us; the launch traced here: 152 us
  starting transfers between devices  61.4 us (40%)
  Pallas kernels  48.5 us (32%)
  waiting for transfers between devices  27.8 us (18%)
  blocking collectives  7.84 us (5%)
  local copies, waits for them, and re-layouts  3.72 us (2%)
  other arithmetic  2.83 us (2%)
    ppermute x28, starting transfers between devices, shifted(): lax.ppermute(value, axis, [(i, (i + shift) % size) for i in range(size)])  53.9 us
    ppermute x28, waiting for transfers between devices, shifted(): lax.ppermute(value, axis, [(i, (i + shift) % size) for i in range(size)])  25.7 us
    pallas_call x4, Pallas kernels, product_step(): pl.pallas_call(kernel, grid=(4 if last else 1,), in_specs=[resident()] *...  24.4 us
    pallas_call x2, Pallas kernels, transform_call(): pl.pallas_call(kernel, grid_spec=pltpu.PrefetchScalarGridSpec(num_scalar_...  18.8 us
    all_to_all x1, blocking collectives, body(): lax.all_to_all(jnp.broadcast_to(valence, (8, *valence.shape)), NARROW, 0,...  7.84 us
    all_to_all x1, starting transfers between devices, body(): rows = lax.all_to_all(rows, WIDE, 0, 0, tiled=True)  7.58 us
    pallas_call x1, Pallas kernels, prepare(): pl.pallas_call(prepare_kernel, grid_spec=pltpu.PrefetchScalarGridSpec(num...  5.24 us
  transfers between devices with their start and end apart: 29, of which 13 were waited for; matrix products, arithmetic and copies ran while one was open for 4% of the time, Pallas kernels for 21%

profile of v2, /device:TPU:1, one launch (start us, length us, event | category | flops | bytes accessed | tf_op | source)
XLA Modules:
  0.0 152.4 jit_solution(17458236129900648044)
XLA Ops:
  0.0 2.0 %collective-permute-start = (f32[256,128]{1,0:T(8,128)}, f32[256,128]{1,0:T(8,128)S(1)}, u32[]{:S(2)}, u32[]{:S(2)}) collective-permute-start(f32[256,128]{1,0:T(8,128)} %bitcast.45), channel_id=1, source_target_pairs={{0,1},{1,2},{2,3},{3,0},{4,5},{5,6},{6,7},{7,4},{8,9},{9,10},{10,1... | collective-permute-start | bytes 393224 | tf_op jit(solution)/shard_map/ppermute | solution.py:364
  2.0 2.5 %collective-permute-start.1 = (f32[256,128]{1,0:T(8,128)}, f32[256,128]{1,0:T(8,128)S(1)}, u32[]{:S(2)}, u32[]{:S(2)}) collective-permute-start(f32[256,128]{1,0:T(8,128)} %bitcast.46), channel_id=1, source_target_pairs={{0,2},{1,3},{2,0},{3,1},{4,6},{5,7},{6,4},{7,5},{8,10},{9,11},{10,... | collective-permute-start | bytes 393224 | tf_op jit(solution)/shard_map/ppermute | solution.py:364
  4.5 1.2 collective-permute-start.2
  5.6 0.7 broadcast_in_dim.4
  6.3 7.8 %all_to_all.10 = f32[8,8,128]{2,1,0:T(8,128)S(1)} all-to-all(f32[8,8,128]{2,1,0:T(8,128)S(1)} %broadcast_in_dim.4), channel_id=1, replica_groups=mesh['zh'=4,'y'=4,'co'=2,'zl'=2,'x'=4] {'zl','x'}, dimensions={0} | all-to-all | bytes 65536 | tf_op jit(solution)/shard_map/all_to_all | solution.py:383
  14.2 3.1 %collective-permute-start.3 = (f32[8,8,128]{2,1,0:T(8,128)S(1)}, f32[8,8,128]{2,1,0:T(8,128)S(1)}, u32[]{:S(2)}, u32[]{:S(2)}) collective-permute-start(f32[8,8,128]{2,1,0:T(8,128)S(1)} %all_to_all.10), channel_id=1, source_target_pairs={{0,64},{64,128},{128,192},{192,0},{1,65},{65,129},{129,193},{193,1... | collective-permute-start | bytes 98312 | tf_op jit(solution)/shard_map/ppermute | solution.py:364
  17.3 4.7 %collective-permute-start.4 = (f32[8,8,128]{2,1,0:T(8,128)S(1)}, f32[8,8,128]{2,1,0:T(8,128)S(1)}, u32[]{:S(2)}, u32[]{:S(2)}) collective-permute-start(f32[8,8,128]{2,1,0:T(8,128)S(1)} %all_to_all.10), channel_id=1, source_target_pairs={{0,128},{64,192},{128,0},{192,64},{1,129},{65,193},{129,1},{193,65... | collective-permute-start | bytes 98312 | tf_op jit(solution)/shard_map/ppermute | solution.py:364
  22.0 2.4 %collective-permute-start.5 = (f32[8,8,128]{2,1,0:T(8,128)S(1)}, f32[8,8,128]{2,1,0:T(8,128)S(1)}, u32[]{:S(2)}, u32[]{:S(2)}) collective-permute-start(f32[8,8,128]{2,1,0:T(8,128)S(1)} %all_to_all.10), channel_id=1, source_target_pairs={{0,192},{64,0},{128,64},{192,128},{1,193},{65,1},{129,65},{193,129... | collective-permute-start | bytes 98312 | tf_op jit(solution)/shard_map/ppermute | solution.py:364
  24.4 0.8 broadcast_subtract_fusion
  25.3 0.4 reshape.39
  25.7 0.4 collective-permute-done.5
  26.2 1.4 collective-permute-start.6
  27.5 2.6 %collective-permute-start.7 = (f32[4,8,8,128]{3,2,1,0:T(8,128)S(1)}, f32[4,8,8,128]{3,2,1,0:T(8,128)S(1)}, u32[]{:S(2)}, u32[]{:S(2)}) collective-permute-start(f32[4,8,8,128]{3,2,1,0:T(8,128)S(1)} %pad_maximum_fusion.5), channel_id=1, source_target_pairs={{0,32},{16,48},{32,0},{48,16},{1,33},{17,49},{33,1},{49,17},{2,34}... | collective-permute-start | bytes 393224 | tf_op jit(solution)/shard_map/ppermute | solution.py:364
  30.2 1.1 collective-permute-start.8
  31.3 2.6 %collective-permute-done.7 = f32[4,8,8,128]{3,2,1,0:T(8,128)S(1)} collective-permute-done((f32[4,8,8,128]{3,2,1,0:T(8,128)S(1)}, f32[4,8,8,128]{3,2,1,0:T(8,128)S(1)}, u32[]{:S(2)}, u32[]{:S(2)}) %collective-permute-start.7) | collective-permute-done | bytes 131104 | tf_op jit(solution)/shard_map/ppermute | solution.py:364
  34.0 6.2 %collective-permute-start.9 = (f32[4,4,8,8,128]{4,3,2,1,0:T(8,128)S(1)}, f32[4,4,8,8,128]{4,3,2,1,0:T(8,128)S(1)}, u32[]{:S(2)}, u32[]{:S(2)}) collective-permute-start(f32[4,4,8,8,128]{4,3,2,1,0:T(8,128)S(1)} %pad_maximum_fusion.1.refs_0_.refs_1_), channel_id=1, source_target_pairs={{0,8},{8,0},{1,9},{9,1},{2,10},{10,2},{3,11},{11,3},{4,12},{12,4},... | collective-permute-start | bytes 1572872 | tf_op jit(solution)/shard_map/ppermute | solution.py:364
  40.2 0.7 stack.77.pos
  40.9 0.9 collective-permute-done.9.refs_1_.refs_2_
  41.7 0.8 copy-done.6
  42.5 8.8 %row_pairs.1 = (bf16[32,16,256]{2,1,0:T(8,128)(2,1)}, bf16[416,256]{1,0:T(8,128)(2,1)}) custom-call(s32[5]{0:T(128)} %stack.77.pos, f32[4,4,8,8,128]{4,3,2,1,0:T(8,128)} %copy-done.3, f32[4,4,8,8,128]{4,3,2,1,0:T(8,128)} %copy-done.6, f32[256,128]{1,0:T(8,128)} %bitcast.48, bf16[1024,512]{1,0:T(8,128)(2,1)} %constant.38.clone.refs_3_.refs_6_, ...), custom_call_target="tpu_custom_call" | custom-call | flops 4000000000 | bytes 6291456 | tf_op jit(solution)/shard_map/row_pairs/pallas_call | solution.py:229
  51.4 7.6 %all-to-all-start.1 = ((bf16[32,16,256]{2,1,0:T(8,128)(2,1)}), bf16[32,16,256]{2,1,0:T(8,128)(2,1)S(1)}, u32[]{:S(2)}, u32[]{:S(2)}) async-start(bf16[32,16,256]{2,1,0:T(8,128)(2,1)} %get-tuple-element.38), calls=%async_computation.1 | async-start | bytes 524288 | tf_op jit(solution)/shard_map/all_to_all | solution.py:392
  59.0 9.9 %column_pairs.1 = bf16[2,4,16,640]{3,2,1,0:T(8,128)(2,1)} custom-call(s32[5]{0:T(128)} %stack.77.pos, bf16[416,256]{1,0:T(8,128)(2,1)} %get-tuple-element.39.refs_0_, f32[4,4,8,8,128]{4,3,2,1,0:T(8,128)} %copy-done.3, f32[4,4,8,8,128]{4,3,2,1,0:T(8,128)} %copy-done.6, f32[256,128]{1,0:T(8,128)} %copy-done.7, f32[256,128]{1,0:T(8,128)} %copy-done.8, ...), custom_call_target="tpu_custom_call" | custom-call | flops 8000000000 | bytes 6291456 | tf_op jit(solution)/shard_map/column_pairs/pallas_call | solution.py:229
  69.0 0.9 slice_bitcast_fusion
  70.0 2.1 %all-to-all-done.1 = bf16[32,16,256]{2,1,0:T(8,128)(2,1)S(1)} async-done(((bf16[32,16,256]{2,1,0:T(8,128)(2,1)}), bf16[32,16,256]{2,1,0:T(8,128)(2,1)S(1)}, u32[]{:S(2)}, u32[]{:S(2)}) %all-to-all-start.1) | async-done | bytes 262176 | tf_op jit(solution)/shard_map/all_to_all | solution.py:392
  72.1 1.4 collective-permute-done.11
  73.5 0.9 broadcast_select_fusion.1
  74.4 5.7 %collective-permute-done.10 = bf16[32,16,256]{2,1,0:T(8,128)(2,1)S(1)} collective-permute-done((bf16[32,16,256]{2,1,0:T(8,128)(2,1)S(1)}, bf16[32,16,256]{2,1,0:T(8,128)(2,1)S(1)}, u32[]{:S(2)}, u32[]{:S(2)}) %collective-permute-start.10) | collective-permute-done | bytes 262176 | tf_op jit(solution)/shard_map/ppermute | solution.py:364
  80.6 2.4 %collective-permute-start.13 = (bf16[2,4,4,2,16,256]{5,4,3,2,1,0:T(8,128)(2,1)S(1)}, bf16[2,4,4,2,16,256]{5,4,3,2,1,0:T(8,128)(2,1)S(1)}, u32[]{:S(2)}, u32[]{:S(2)}) collective-permute-start(bf16[2,4,4,2,16,256]{5,4,3,2,1,0:T(8,128)(2,1)S(1)} %pad_maximum_fusion.2.r0), channel_id=1, source_target_pairs={{0,3},{1,0},{2,1},{3,2},{4,7},{5,4},{6,5},{7,6},{8,11},{9,8},{10,9... | collective-permute-start | bytes 1572872 | tf_op jit(solution)/shard_map/ppermute | solution.py:364
  83.0 1.6 %collective-permute-start.14 = (bf16[8,16,640]{2,1,0:T(8,128)(2,1)S(1)}, bf16[8,16,640]{2,1,0:T(8,128)(2,1)S(1)}, u32[]{:S(2)}, u32[]{:S(2)}) collective-permute-start(bf16[8,16,640]{2,1,0:T(8,128)(2,1)S(1)} %pad_maximum_fusion.4), channel_id=1, source_target_pairs={{0,64},{64,128},{128,192},{192,0},{1,65},{65,129},{129,193},{193,1... | collective-permute-start | bytes 491528 | tf_op jit(solution)/shard_map/ppermute | solution.py:364
  84.5 2.0 %collective-permute-start.15 = (bf16[8,16,640]{2,1,0:T(8,128)(2,1)S(1)}, bf16[8,16,640]{2,1,0:T(8,128)(2,1)S(1)}, u32[]{:S(2)}, u32[]{:S(2)}) collective-permute-start(bf16[8,16,640]{2,1,0:T(8,128)(2,1)S(1)} %pad_maximum_fusion.4), channel_id=1, source_target_pairs={{0,192},{64,0},{128,64},{192,128},{1,193},{65,1},{129,65},{193,129... | collective-permute-start | bytes 491528 | tf_op jit(solution)/shard_map/ppermute | solution.py:364
  86.6 7.5 %collective-permute-done.14 = bf16[8,16,640]{2,1,0:T(8,128)(2,1)S(1)} collective-permute-done((bf16[8,16,640]{2,1,0:T(8,128)(2,1)S(1)}, bf16[8,16,640]{2,1,0:T(8,128)(2,1)S(1)}, u32[]{:S(2)}, u32[]{:S(2)}) %collective-permute-start.14) | collective-permute-done | bytes 163872 | tf_op jit(solution)/shard_map/ppermute | solution.py:364
  94.0 1.4 collective-permute-done.15
  95.4 1.3 collective-permute-start.16
  97.1 2.5 %collective-permute-start.18 = (bf16[4,16,640]{2,1,0:T(8,128)(2,1)S(1)}, bf16[4,16,640]{2,1,0:T(8,128)(2,1)S(1)}, u32[]{:S(2)}, u32[]{:S(2)}) collective-permute-start(bf16[4,16,640]{2,1,0:T(8,128)(2,1)S(1)} %slice.28), channel_id=1, source_target_pairs={{0,192},{64,0},{128,64},{192,128},{1,193},{65,1},{129,65},{193,129... | collective-permute-start | bytes 245768 | tf_op jit(solution)/shard_map/ppermute | solution.py:364
  99.7 2.1 %collective-permute-done.18 = bf16[4,16,640]{2,1,0:T(8,128)(2,1)S(1)} collective-permute-done((bf16[4,16,640]{2,1,0:T(8,128)(2,1)S(1)}, bf16[4,16,640]{2,1,0:T(8,128)(2,1)S(1)}, u32[]{:S(2)}, u32[]{:S(2)}) %collective-permute-start.18) | collective-permute-done | bytes 81952 | tf_op jit(solution)/shard_map/ppermute | solution.py:364
  101.8 3.4 %collective-permute-done.19 = bf16[4,16,640]{2,1,0:T(8,128)(2,1)S(1)} collective-permute-done((bf16[4,16,640]{2,1,0:T(8,128)(2,1)S(1)}, bf16[4,16,640]{2,1,0:T(8,128)(2,1)S(1)}, u32[]{:S(2)}, u32[]{:S(2)}) %collective-permute-start.19) | collective-permute-done | bytes 81952 | tf_op jit(solution)/shard_map/ppermute | solution.py:364
  105.4 1.2 collective-permute-start.20
  106.6 1.5 %collective-permute-start.21 = (bf16[4,8,16,640]{3,2,1,0:T(8,128)(2,1)S(1)}, bf16[4,8,16,640]{3,2,1,0:T(8,128)(2,1)S(1)}, u32[]{:S(2)}, u32[]{:S(2)}) collective-permute-start(bf16[4,8,16,640]{3,2,1,0:T(8,128)(2,1)S(1)} %pad_maximum_fusion.mine), channel_id=1, source_target_pairs={{0,48},{16,0},{32,16},{48,32},{1,49},{17,1},{33,17},{49,33},{2,50}... | collective-permute-start | bytes 1966088 | tf_op jit(solution)/shard_map/ppermute | solution.py:364
  108.1 4.5 %collective-permute-start.23 = (bf16[4,8,16,640]{3,2,1,0:T(8,128)(2,1)S(1)}, bf16[4,8,16,640]{3,2,1,0:T(8,128)(2,1)S(1)}, u32[]{:S(2)}, u32[]{:S(2)}) collective-permute-start(bf16[4,8,16,640]{3,2,1,0:T(8,128)(2,1)S(1)} %pad_maximum_fusion.mine), channel_id=1, source_target_pairs={{0,8},{8,0},{1,9},{9,1},{2,10},{10,2},{3,11},{11,3},{4,12},{12,4},... | collective-permute-start | bytes 1966088 | tf_op jit(solution)/shard_map/ppermute | solution.py:364
  112.6 0.9 pad_maximum_fusion.3.r2
  113.5 5.2 %scaled_rows.1 = (bf16[4,1536,1024]{2,1,0:T(8,128)(2,1)S(1)}, bf16[4,640,256]{2,1,0:T(8,128)(2,1)S(1)}, f32[4,16,256]{2,1,0:T(8,128)S(1)}) custom-call(s32[5]{0:T(128)S(1)} %copy-done, f32[6]{0:T(128)S(1)} %copy-done.1, bf16[2,4,4,2,16,256]{5,4,3,2,1,0:T(8,128)(2,1)} %copy-done.2, bf16[2,4,4,2,16,256]{5,4,3,2,1,0:T(8,128)(2,1)} %copy-done.4, ...), custom_call_target="tpu_custom_call" | custom-call | flops 1000000000 | bytes 20971520 | tf_op jit(solution)/shard_map/scaled_rows/pallas_call | solution.py:303
  118.9 4.9 %collective-permute-start.22 = (bf16[4,8,16,640]{3,2,1,0:T(8,128)(2,1)S(1)}, bf16[4,8,16,640]{3,2,1,0:T(8,128)(2,1)S(1)}, u32[]{:S(2)}, u32[]{:S(2)}) collective-permute-start(bf16[4,8,16,640]{3,2,1,0:T(8,128)(2,1)S(1)} %collective-permute-done.20.mine), channel_id=1, source_target_pairs={{0,8},{8,0},{1,9},{9,1},{2,10},{10,2},{3,11},{11,3},{4,12},{12,4},... | collective-permute-start | bytes 1966088 | tf_op jit(solution)/shard_map/ppermute | solution.py:364
  124.0 2.8 %collective-permute-start.24 = (bf16[2,8,16,640]{3,2,1,0:T(8,128)(2,1)S(1)}, bf16[2,8,16,640]{3,2,1,0:T(8,128)(2,1)S(1)}, u32[]{:S(2)}, u32[]{:S(2)}) collective-permute-start(bf16[2,8,16,640]{3,2,1,0:T(8,128)(2,1)S(1)} %slice.30), channel_id=1, source_target_pairs={{0,48},{16,0},{32,16},{48,32},{1,49},{17,1},{33,17},{49,33},{2,50}... | collective-permute-start | bytes 983048 | tf_op jit(solution)/shard_map/ppermute | solution.py:364
  126.8 5.4 %response_product.4.refs_0_ = f32[6,256,1024]{2,1,0:T(8,128)S(1)} custom-call(bf16[4,8,16,640]{3,2,1,0:T(8,128)(2,1)S(1)} %pad_maximum_fusion.mine, bf16[4,8,16,640]{3,2,1,0:T(8,128)(2,1)S(1)} %collective-permute-done.23.theirs, bf16[4,1536,1024]{2,1,0:T(8,128)(2,1)S(1)} %get-tuple-element.58.scaled, bf16[4,640,256]{2,1,0:T(8,128)(2,1)S(1)} %get-tuple-element.59.hot, ...), custom_call_target="tpu_custom_call" | custom-call | flops 4600000000 | bytes 10485760 | tf_op jit(solution)/shard_map/response_product/pallas_call | solution.py:348
  132.2 5.9 %response_product.5.refs_0_ = f32[6,256,1024]{2,1,0:T(8,128)S(1)} custom-call(bf16[4,8,16,640]{3,2,1,0:T(8,128)(2,1)S(1)} %collective-permute-done.20.mine, bf16[4,8,16,640]{3,2,1,0:T(8,128)(2,1)S(1)} %collective-permute-done.22.theirs, bf16[4,1536,1024]{2,1,0:T(8,128)(2,1)S(1)} %get-tuple-element.58.scaled, ...), custom_call_target="tpu_custom_call", output_to_operand_aliasing={{}: (5, {})} | custom-call | flops 4600000000 | bytes 10485760 | tf_op jit(solution)/shard_map/response_product/pallas_call | solution.py:348
  138.2 1.0 collective-permute-start.26
  139.3 5.9 %response_product.6.refs_0_ = f32[6,256,1024]{2,1,0:T(8,128)S(1)} custom-call(bf16[4,8,16,640]{3,2,1,0:T(8,128)(2,1)S(1)} %collective-permute-done.21.mine, bf16[4,8,16,640]{3,2,1,0:T(8,128)(2,1)S(1)} %collective-permute-done.27.theirs, bf16[4,1536,1024]{2,1,0:T(8,128)(2,1)S(1)} %get-tuple-element.58.scaled, ...), custom_call_target="tpu_custom_call", output_to_operand_aliasing={{}: (5, {})} | custom-call | flops 4600000000 | bytes 10485760 | tf_op jit(solution)/shard_map/response_product/pallas_call | solution.py:348
  145.2 7.2 %response_product.7 = f32[6,256,1024]{2,1,0:T(8,128)} custom-call(bf16[4,8,16,640]{3,2,1,0:T(8,128)(2,1)S(1)} %constant_dynamic-update-slice_fusion.mine, bf16[4,8,16,640]{3,2,1,0:T(8,128)(2,1)S(1)} %collective-permute-done.26.theirs, bf16[4,1536,1024]{2,1,0:T(8,128)(2,1)S(1)} %get-tuple-element.58.scaled, bf16[4,640,256]{2,1,0:T(8,128)(2,1)S(1)} %get-tuple-element.59.hot, ...), custom_call_target="tpu_custom_call" | custom-call | flops 4600000000 | bytes 10485760 | tf_op jit(solution)/shard_map/response_product/pallas_call | solution.py:348
  (60 shorter events, 2.0 us)
Async XLA Ops:
  0.0 14.2 %collective-permute-start = (f32[256,128]{1,0:T(8,128)}, f32[256,128]{1,0:T(8,128)S(1)}, u32[]{:S(2)}, u32[]{:S(2)}) collective-permute-start(f32[256,128]{1,0:T(8,128)} %bitcast.45), channel_id=1, source_target_pairs={{0,1},{1,2},{2,3},{3,0},{4,5},{5,6},{6,7},{7,4},{8,9},{9,10},{10,1... | collective-permute-start | bytes 393224 | tf_op jit(solution)/shard_map/ppermute | solution.py:364
  2.0 12.1 %collective-permute-start.1 = (f32[256,128]{1,0:T(8,128)}, f32[256,128]{1,0:T(8,128)S(1)}, u32[]{:S(2)}, u32[]{:S(2)}) collective-permute-start(f32[256,128]{1,0:T(8,128)} %bitcast.46), channel_id=1, source_target_pairs={{0,2},{1,3},{2,0},{3,1},{4,6},{5,7},{6,4},{7,5},{8,10},{9,11},{10,... | collective-permute-start | bytes 393224 | tf_op jit(solution)/shard_map/ppermute | solution.py:364
  4.5 9.7 %collective-permute-start.2 = (f32[256,128]{1,0:T(8,128)}, f32[256,128]{1,0:T(8,128)S(1)}, u32[]{:S(2)}, u32[]{:S(2)}) collective-permute-start(f32[256,128]{1,0:T(8,128)} %bitcast.47), channel_id=1, source_target_pairs={{0,3},{1,0},{2,1},{3,2},{4,7},{5,4},{6,5},{7,6},{8,11},{9,8},{10,9... | collective-permute-start | bytes 393224 | tf_op jit(solution)/shard_map/ppermute | solution.py:364
  14.2 37.2 %copy-start.7 = (f32[256,128]{1,0:T(8,128)}, f32[256,128]{1,0:T(8,128)S(1)}, u32[]{:S(2)}) copy-start(f32[256,128]{1,0:T(8,128)S(1)} %collective-permute-done.refs_3_) | copy-start | bytes 393220
  14.2 37.2 %copy-start.8 = (f32[256,128]{1,0:T(8,128)}, f32[256,128]{1,0:T(8,128)S(1)}, u32[]{:S(2)}) copy-start(f32[256,128]{1,0:T(8,128)S(1)} %collective-permute-done.1.refs_4_) | copy-start | bytes 393220
  14.2 37.2 %copy-start.9 = (f32[256,128]{1,0:T(8,128)}, f32[256,128]{1,0:T(8,128)S(1)}, u32[]{:S(2)}) copy-start(f32[256,128]{1,0:T(8,128)S(1)} %collective-permute-done.2.refs_5_) | copy-start | bytes 393220
  14.2 11.5 %collective-permute-start.3 = (f32[8,8,128]{2,1,0:T(8,128)S(1)}, f32[8,8,128]{2,1,0:T(8,128)S(1)}, u32[]{:S(2)}, u32[]{:S(2)}) collective-permute-start(f32[8,8,128]{2,1,0:T(8,128)S(1)} %all_to_all.10), channel_id=1, source_target_pairs={{0,64},{64,128},{128,192},{192,0},{1,65},{65,129},{129,193},{193,1... | collective-permute-start | bytes 98312 | tf_op jit(solution)/shard_map/ppermute | solution.py:364
  17.3 8.4 %collective-permute-start.4 = (f32[8,8,128]{2,1,0:T(8,128)S(1)}, f32[8,8,128]{2,1,0:T(8,128)S(1)}, u32[]{:S(2)}, u32[]{:S(2)}) collective-permute-start(f32[8,8,128]{2,1,0:T(8,128)S(1)} %all_to_all.10), channel_id=1, source_target_pairs={{0,128},{64,192},{128,0},{192,64},{1,129},{65,193},{129,1},{193,65... | collective-permute-start | bytes 98312 | tf_op jit(solution)/shard_map/ppermute | solution.py:364
  22.0 4.1 %collective-permute-start.5 = (f32[8,8,128]{2,1,0:T(8,128)S(1)}, f32[8,8,128]{2,1,0:T(8,128)S(1)}, u32[]{:S(2)}, u32[]{:S(2)}) collective-permute-start(f32[8,8,128]{2,1,0:T(8,128)S(1)} %all_to_all.10), channel_id=1, source_target_pairs={{0,192},{64,0},{128,64},{192,128},{1,193},{65,1},{129,65},{193,129... | collective-permute-start | bytes 98312 | tf_op jit(solution)/shard_map/ppermute | solution.py:364
  26.2 5.2 %collective-permute-start.6 = (f32[4,8,8,128]{3,2,1,0:T(8,128)S(1)}, f32[4,8,8,128]{3,2,1,0:T(8,128)S(1)}, u32[]{:S(2)}, u32[]{:S(2)}) collective-permute-start(f32[4,8,8,128]{3,2,1,0:T(8,128)S(1)} %pad_maximum_fusion.5), channel_id=1, source_target_pairs={{0,16},{16,32},{32,48},{48,0},{1,17},{17,33},{33,49},{49,1},{2,18}... | collective-permute-start | bytes 393224 | tf_op jit(solution)/shard_map/ppermute | solution.py:364
  27.5 6.4 %collective-permute-start.7 = (f32[4,8,8,128]{3,2,1,0:T(8,128)S(1)}, f32[4,8,8,128]{3,2,1,0:T(8,128)S(1)}, u32[]{:S(2)}, u32[]{:S(2)}) collective-permute-start(f32[4,8,8,128]{3,2,1,0:T(8,128)S(1)} %pad_maximum_fusion.5), channel_id=1, source_target_pairs={{0,32},{16,48},{32,0},{48,16},{1,33},{17,49},{33,1},{49,17},{2,34}... | collective-permute-start | bytes 393224 | tf_op jit(solution)/shard_map/ppermute | solution.py:364
  30.2 3.8 %collective-permute-start.8 = (f32[4,8,8,128]{3,2,1,0:T(8,128)S(1)}, f32[4,8,8,128]{3,2,1,0:T(8,128)S(1)}, u32[]{:S(2)}, u32[]{:S(2)}) collective-permute-start(f32[4,8,8,128]{3,2,1,0:T(8,128)S(1)} %pad_maximum_fusion.5), channel_id=1, source_target_pairs={{0,48},{16,0},{32,16},{48,32},{1,49},{17,1},{33,17},{49,33},{2,50}... | collective-permute-start | bytes 393224 | tf_op jit(solution)/shard_map/ppermute | solution.py:364
  34.0 7.7 %copy-start.3 = (f32[4,4,8,8,128]{4,3,2,1,0:T(8,128)}, f32[4,4,8,8,128]{4,3,2,1,0:T(8,128)S(1)}, u32[]{:S(2)}) copy-start(f32[4,4,8,8,128]{4,3,2,1,0:T(8,128)S(1)} %pad_maximum_fusion.1.refs_0_.refs_1_) | copy-start | bytes 1572868
  34.0 7.7 %collective-permute-start.9 = (f32[4,4,8,8,128]{4,3,2,1,0:T(8,128)S(1)}, f32[4,4,8,8,128]{4,3,2,1,0:T(8,128)S(1)}, u32[]{:S(2)}, u32[]{:S(2)}) collective-permute-start(f32[4,4,8,8,128]{4,3,2,1,0:T(8,128)S(1)} %pad_maximum_fusion.1.refs_0_.refs_1_), channel_id=1, source_target_pairs={{0,8},{8,0},{1,9},{9,1},{2,10},{10,2},{3,11},{11,3},{4,12},{12,4},... | collective-permute-start | bytes 1572872 | tf_op jit(solution)/shard_map/ppermute | solution.py:364
  41.7 0.8 copy-start.6
  51.4 20.7 %all-to-all-start.1 = ((bf16[32,16,256]{2,1,0:T(8,128)(2,1)}), bf16[32,16,256]{2,1,0:T(8,128)(2,1)S(1)}, u32[]{:S(2)}, u32[]{:S(2)}) async-start(bf16[32,16,256]{2,1,0:T(8,128)(2,1)} %get-tuple-element.38), calls=%async_computation.1 | async-start | bytes 524288 | tf_op jit(solution)/shard_map/all_to_all | solution.py:392
  59.0 54.5 %copy-start = (s32[5]{0:T(128)S(1)}, s32[5]{0:T(128)}, u32[]{:S(2)}) copy-start(s32[5]{0:T(128)} %stack.77.pos) | copy-start | bytes 64
  59.0 54.5 %copy-start.1 = (f32[6]{0:T(128)S(1)}, f32[6]{0:T(128)}, u32[]{:S(2)}) copy-start(f32[6]{0:T(128)} %omega.1) | copy-start | bytes 76
  69.9 3.6 %collective-permute-start.11 = (bf16[4,16,640]{2,1,0:T(8,128)(2,1)S(1)}, bf16[4,16,640]{2,1,0:T(8,128)(2,1)S(1)}, u32[]{:S(2)}, u32[]{:S(2)}) collective-permute-start(bf16[4,16,640]{2,1,0:T(8,128)(2,1)S(1)} %slice_bitcast_fusion), channel_id=1, source_target_pairs={{0,4},{4,0},{1,5},{5,1},{2,6},{6,2},{3,7},{7,3},{8,12},{12,8},{9,1... | collective-permute-start | bytes 245768 | tf_op jit(solution)/shard_map/ppermute | solution.py:364
  72.1 8.1 %collective-permute-start.10 = (bf16[32,16,256]{2,1,0:T(8,128)(2,1)S(1)}, bf16[32,16,256]{2,1,0:T(8,128)(2,1)S(1)}, u32[]{:S(2)}, u32[]{:S(2)}) collective-permute-start(bf16[32,16,256]{2,1,0:T(8,128)(2,1)S(1)} %all-to-all-done.1), channel_id=1, source_target_pairs={{0,4},{4,0},{1,5},{5,1},{2,6},{6,2},{3,7},{7,3},{8,12},{12,8},{9,1... | collective-permute-start | bytes 786440 | tf_op jit(solution)/shard_map/ppermute | solution.py:364
  80.2 33.3 %copy-start.2 = (bf16[2,4,4,2,16,256]{5,4,3,2,1,0:T(8,128)(2,1)}, bf16[2,4,4,2,16,256]{5,4,3,2,1,0:T(8,128)(2,1)S(1)}, u32[]{:S(2)}) copy-start(bf16[2,4,4,2,16,256]{5,4,3,2,1,0:T(8,128)(2,1)S(1)} %pad_maximum_fusion.2.r0) | copy-start | bytes 1572868
  80.2 15.2 %collective-permute-start.12 = (bf16[2,4,4,2,16,256]{5,4,3,2,1,0:T(8,128)(2,1)S(1)}, bf16[2,4,4,2,16,256]{5,4,3,2,1,0:T(8,128)(2,1)S(1)}, u32[]{:S(2)}, u32[]{:S(2)}) collective-permute-start(bf16[2,4,4,2,16,256]{5,4,3,2,1,0:T(8,128)(2,1)S(1)} %pad_maximum_fusion.2.r0), channel_id=1, source_target_pairs={{0,1},{1,2},{2,3},{3,0},{4,5},{5,6},{6,7},{7,4},{8,9},{9,10},{10,1... | collective-permute-start | bytes 1572872 | tf_op jit(solution)/shard_map/ppermute | solution.py:364
  80.6 14.8 %collective-permute-start.13 = (bf16[2,4,4,2,16,256]{5,4,3,2,1,0:T(8,128)(2,1)S(1)}, bf16[2,4,4,2,16,256]{5,4,3,2,1,0:T(8,128)(2,1)S(1)}, u32[]{:S(2)}, u32[]{:S(2)}) collective-permute-start(bf16[2,4,4,2,16,256]{5,4,3,2,1,0:T(8,128)(2,1)S(1)} %pad_maximum_fusion.2.r0), channel_id=1, source_target_pairs={{0,3},{1,0},{2,1},{3,2},{4,7},{5,4},{6,5},{7,6},{8,11},{9,8},{10,9... | collective-permute-start | bytes 1572872 | tf_op jit(solution)/shard_map/ppermute | solution.py:364
  83.0 11.0 %collective-permute-start.14 = (bf16[8,16,640]{2,1,0:T(8,128)(2,1)S(1)}, bf16[8,16,640]{2,1,0:T(8,128)(2,1)S(1)}, u32[]{:S(2)}, u32[]{:S(2)}) collective-permute-start(bf16[8,16,640]{2,1,0:T(8,128)(2,1)S(1)} %pad_maximum_fusion.4), channel_id=1, source_target_pairs={{0,64},{64,128},{128,192},{192,0},{1,65},{65,129},{129,193},{193,1... | collective-permute-start | bytes 491528 | tf_op jit(solution)/shard_map/ppermute | solution.py:364
  84.5 10.9 %collective-permute-start.15 = (bf16[8,16,640]{2,1,0:T(8,128)(2,1)S(1)}, bf16[8,16,640]{2,1,0:T(8,128)(2,1)S(1)}, u32[]{:S(2)}, u32[]{:S(2)}) collective-permute-start(bf16[8,16,640]{2,1,0:T(8,128)(2,1)S(1)} %pad_maximum_fusion.4), channel_id=1, source_target_pairs={{0,192},{64,0},{128,64},{192,128},{1,193},{65,1},{129,65},{193,129... | collective-permute-start | bytes 491528 | tf_op jit(solution)/shard_map/ppermute | solution.py:364
  95.4 18.1 %copy-start.4 = (bf16[2,4,4,2,16,256]{5,4,3,2,1,0:T(8,128)(2,1)}, bf16[2,4,4,2,16,256]{5,4,3,2,1,0:T(8,128)(2,1)S(1)}, u32[]{:S(2)}) copy-start(bf16[2,4,4,2,16,256]{5,4,3,2,1,0:T(8,128)(2,1)S(1)} %collective-permute-done.12.r1) | copy-start | bytes 1572868
  95.4 18.1 %copy-start.5 = (bf16[2,4,4,2,16,256]{5,4,3,2,1,0:T(8,128)(2,1)}, bf16[2,4,4,2,16,256]{5,4,3,2,1,0:T(8,128)(2,1)S(1)}, u32[]{:S(2)}) copy-start(bf16[2,4,4,2,16,256]{5,4,3,2,1,0:T(8,128)(2,1)S(1)} %collective-permute-done.13.r3) | copy-start | bytes 1572868
  95.4 9.8 %collective-permute-start.16 = (bf16[1,4,4,2,16,256]{5,4,3,2,1,0:T(8,128)(2,1)S(1)}, bf16[1,4,4,2,16,256]{5,4,3,2,1,0:T(8,128)(2,1)S(1)}, u32[]{:S(2)}, u32[]{:S(2)}) collective-permute-start(bf16[1,4,4,2,16,256]{5,4,3,2,1,0:T(8,128)(2,1)S(1)} %slice.26), channel_id=1, source_target_pairs={{0,3},{1,0},{2,1},{3,2},{4,7},{5,4},{6,5},{7,6},{8,11},{9,8},{10,9... | collective-permute-start | bytes 786440 | tf_op jit(solution)/shard_map/ppermute | solution.py:364
  96.8 8.4 %collective-permute-start.17 = (bf16[1,4,4,2,16,256]{5,4,3,2,1,0:T(8,128)(2,1)S(1)}, bf16[1,4,4,2,16,256]{5,4,3,2,1,0:T(8,128)(2,1)S(1)}, u32[]{:S(2)}, u32[]{:S(2)}) collective-permute-start(bf16[1,4,4,2,16,256]{5,4,3,2,1,0:T(8,128)(2,1)S(1)} %slice.27), channel_id=1, source_target_pairs={{0,1},{1,2},{2,3},{3,0},{4,5},{5,6},{6,7},{7,4},{8,9},{9,10},{10,1... | collective-permute-start | bytes 786440 | tf_op jit(solution)/shard_map/ppermute | solution.py:364
  97.1 4.7 %collective-permute-start.18 = (bf16[4,16,640]{2,1,0:T(8,128)(2,1)S(1)}, bf16[4,16,640]{2,1,0:T(8,128)(2,1)S(1)}, u32[]{:S(2)}, u32[]{:S(2)}) collective-permute-start(bf16[4,16,640]{2,1,0:T(8,128)(2,1)S(1)} %slice.28), channel_id=1, source_target_pairs={{0,192},{64,0},{128,64},{192,128},{1,193},{65,1},{129,65},{193,129... | collective-permute-start | bytes 245768 | tf_op jit(solution)/shard_map/ppermute | solution.py:364
  99.6 5.6 %collective-permute-start.19 = (bf16[4,16,640]{2,1,0:T(8,128)(2,1)S(1)}, bf16[4,16,640]{2,1,0:T(8,128)(2,1)S(1)}, u32[]{:S(2)}, u32[]{:S(2)}) collective-permute-start(bf16[4,16,640]{2,1,0:T(8,128)(2,1)S(1)} %slice.29), channel_id=1, source_target_pairs={{0,64},{64,128},{128,192},{192,0},{1,65},{65,129},{129,193},{193,1... | collective-permute-start | bytes 245768 | tf_op jit(solution)/shard_map/ppermute | solution.py:364
  105.4 13.6 %collective-permute-start.20 = (bf16[4,8,16,640]{3,2,1,0:T(8,128)(2,1)S(1)}, bf16[4,8,16,640]{3,2,1,0:T(8,128)(2,1)S(1)}, u32[]{:S(2)}, u32[]{:S(2)}) collective-permute-start(bf16[4,8,16,640]{3,2,1,0:T(8,128)(2,1)S(1)} %pad_maximum_fusion.mine), channel_id=1, source_target_pairs={{0,16},{16,32},{32,48},{48,0},{1,17},{17,33},{33,49},{49,1},{2,18}... | collective-permute-start | bytes 1966088 | tf_op jit(solution)/shard_map/ppermute | solution.py:364
  106.6 12.3 %collective-permute-start.21 = (bf16[4,8,16,640]{3,2,1,0:T(8,128)(2,1)S(1)}, bf16[4,8,16,640]{3,2,1,0:T(8,128)(2,1)S(1)}, u32[]{:S(2)}, u32[]{:S(2)}) collective-permute-start(bf16[4,8,16,640]{3,2,1,0:T(8,128)(2,1)S(1)} %pad_maximum_fusion.mine), channel_id=1, source_target_pairs={{0,48},{16,0},{32,16},{48,32},{1,49},{17,1},{33,17},{49,33},{2,50}... | collective-permute-start | bytes 1966088 | tf_op jit(solution)/shard_map/ppermute | solution.py:364
  108.1 18.6 %collective-permute-start.23 = (bf16[4,8,16,640]{3,2,1,0:T(8,128)(2,1)S(1)}, bf16[4,8,16,640]{3,2,1,0:T(8,128)(2,1)S(1)}, u32[]{:S(2)}, u32[]{:S(2)}) collective-permute-start(bf16[4,8,16,640]{3,2,1,0:T(8,128)(2,1)S(1)} %pad_maximum_fusion.mine), channel_id=1, source_target_pairs={{0,8},{8,0},{1,9},{9,1},{2,10},{10,2},{3,11},{11,3},{4,12},{12,4},... | collective-permute-start | bytes 1966088 | tf_op jit(solution)/shard_map/ppermute | solution.py:364
  118.9 13.3 %collective-permute-start.22 = (bf16[4,8,16,640]{3,2,1,0:T(8,128)(2,1)S(1)}, bf16[4,8,16,640]{3,2,1,0:T(8,128)(2,1)S(1)}, u32[]{:S(2)}, u32[]{:S(2)}) collective-permute-start(bf16[4,8,16,640]{3,2,1,0:T(8,128)(2,1)S(1)} %collective-permute-done.20.mine), channel_id=1, source_target_pairs={{0,8},{8,0},{1,9},{9,1},{2,10},{10,2},{3,11},{11,3},{4,12},{12,4},... | collective-permute-start | bytes 1966088 | tf_op jit(solution)/shard_map/ppermute | solution.py:364
  123.9 15.4 %collective-permute-start.27 = (bf16[4,8,16,640]{3,2,1,0:T(8,128)(2,1)S(1)}, bf16[4,8,16,640]{3,2,1,0:T(8,128)(2,1)S(1)}, u32[]{:S(2)}, u32[]{:S(2)}) collective-permute-start(bf16[4,8,16,640]{3,2,1,0:T(8,128)(2,1)S(1)} %collective-permute-done.21.mine), channel_id=1, source_target_pairs={{0,8},{8,0},{1,9},{9,1},{2,10},{10,2},{3,11},{11,3},{4,12},{12,4},... | collective-permute-start | bytes 1966088 | tf_op jit(solution)/shard_map/ppermute | solution.py:364
  124.0 14.1 %collective-permute-start.24 = (bf16[2,8,16,640]{3,2,1,0:T(8,128)(2,1)S(1)}, bf16[2,8,16,640]{3,2,1,0:T(8,128)(2,1)S(1)}, u32[]{:S(2)}, u32[]{:S(2)}) collective-permute-start(bf16[2,8,16,640]{3,2,1,0:T(8,128)(2,1)S(1)} %slice.30), channel_id=1, source_target_pairs={{0,48},{16,0},{32,16},{48,32},{1,49},{17,1},{33,17},{49,33},{2,50}... | collective-permute-start | bytes 983048 | tf_op jit(solution)/shard_map/ppermute | solution.py:364
  126.8 11.4 %collective-permute-start.25 = (bf16[2,8,16,640]{3,2,1,0:T(8,128)(2,1)S(1)}, bf16[2,8,16,640]{3,2,1,0:T(8,128)(2,1)S(1)}, u32[]{:S(2)}, u32[]{:S(2)}) collective-permute-start(bf16[2,8,16,640]{3,2,1,0:T(8,128)(2,1)S(1)} %slice.31), channel_id=1, source_target_pairs={{0,16},{16,32},{32,48},{48,0},{1,17},{17,33},{33,49},{49,1},{2,18}... | collective-permute-start | bytes 983048 | tf_op jit(solution)/shard_map/ppermute | solution.py:364
  138.2 7.0 %collective-permute-start.26 = (bf16[4,8,16,640]{3,2,1,0:T(8,128)(2,1)S(1)}, bf16[4,8,16,640]{3,2,1,0:T(8,128)(2,1)S(1)}, u32[]{:S(2)}, u32[]{:S(2)}) collective-permute-start(bf16[4,8,16,640]{3,2,1,0:T(8,128)(2,1)S(1)} %constant_dynamic-update-slice_fusion.mine), channel_id=1, source_target_pairs={{0,8},{8,0},{1,9},{9,1},{2,10},{10,2},{3,11},{11,3},{4,12},{12,4},... | collective-permute-start | bytes 1966088 | tf_op jit(solution)/shard_map/ppermute | solution.py:364

commit v3 on v2

--- a/solution.py
+++ b/solution.py
@@ -126,8 +126,8 @@
     count = len(bands)
 
     def product(q, carry):
-        szh = (zh - q // 4) & 3
-        sy = (y - q % 4) & 3
+        szh = zh ^ (q // 4)
+        sy = y ^ (q % 4)
         start = pl.multiple_of(q * 16, 16)
         rows_of = [band[pl.ds(start, 16), :] for band in bands]
         for n in range(8):
@@ -368,6 +368,12 @@
     return [value] + [shifted(value, axis, s) for s in range(1, lax.axis_size(axis))]
 
 
+def doubled(value, axis):
+    pair = jnp.stack([value, lax.ppermute(value, axis, [(i, i ^ 1) for i in range(4)])])
+    far = lax.ppermute(pair, axis, [(i, i ^ 3) for i in range(4)])
+    return jnp.stack([pair[0], pair[1], far[1], far[0]])
+
+
 def neighbours(value, axis):
     return shifted(value, axis, 1), shifted(value, axis, 3)
 
@@ -382,10 +388,10 @@
     bands = around(conduction.reshape(256, 128), "x")
     own = lax.all_to_all(jnp.broadcast_to(valence, (8, *valence.shape)), NARROW, 0, 0, tiled=True)
     own, bands = lax.optimization_barrier((own, bands))
-    own = jnp.stack(around(own, "zh"))
+    own = doubled(own, "zh")
     gap = jnp.broadcast_to((eps_cond[:, None] - eps_val)[:, None, :], (256, 2, 8)).reshape(4, 4, 2, 1, 128)
     own, gap = lax.optimization_barrier((own, gap))
-    own = jnp.stack(around(own, "y"))
+    own = doubled(own, "y")
     other = shifted(own, "co", 1)
 
     rows, spectrum = row_pairs(pos, own, other, bands[0], gmap)

time: 153 us -> 157 us (1.026)
  waiting for transfers between devices: 27.8 us -> 33.6 us
    ppermute x28 -> x22, starting transfers between devices: 53.9 us -> 38.7 us  [shifted(): lax.ppermute(value, axis, [(i, (i + shift) % size) for i in range(size)])]
    ppermute x0 -> x4, starting transfers between devices: none -> 12 us  [the longest x2 7.49 us: doubled(): far = lax.ppermute(pair, axis, [(i, i ^ 3) for i in range(4)])]
    ppermute x0 -> x4, waiting for transfers between devices: none -> 8.68 us  [the longest x2 4.4 us: doubled(): far = lax.ppermute(pair, axis, [(i, i ^ 3) for i in range(4)])]
    ppermute x28 -> x22, waiting for transfers between devices: 25.7 us -> 22.8 us  [shifted(): lax.ppermute(value, axis, [(i, (i + shift) % size) for i in range(size)])]
    all_to_all x1, starting transfers between devices: 7.58 us -> 9.36 us  [body(): rows = lax.all_to_all(rows, WIDE, 0, 0, tiled=True)]
  transfers between devices with their start and end apart: 29 -> 27, of which waited for: 13 -> 13; matrix products, arithmetic and copies ran while one was open for 4% -> 4% of each run, Pallas kernels for 21% -> 21%
where the time goes in v3:
time: 157 us
  starting transfers between devices  60.1 us (38%)
  Pallas kernels  48.2 us (31%)
  waiting for transfers between devices  33.6 us (21%)
  blocking collectives  7.84 us (5%)
  local copies, waits for them, and re-layouts  3.74 us (2%)
  other arithmetic  2.85 us (2%)
    ppermute x22, starting transfers between devices, shifted(): lax.ppermute(value, axis, [(i, (i + shift) % size) for i in range(size)])  38.7 us
    pallas_call x4, Pallas kernels, product_step(): pl.pallas_call(kernel, grid=(4 if last else 1,), in_specs=[resident()] *...  24.1 us
    ppermute x22, waiting for transfers between devices, shifted(): lax.ppermute(value, axis, [(i, (i + shift) % size) for i in range(size)])  22.8 us
    pallas_call x2, Pallas kernels, transform_call(): pl.pallas_call(kernel, grid_spec=pltpu.PrefetchScalarGridSpec(num_scalar_...  18.8 us
    all_to_all x1, starting transfers between devices, body(): rows = lax.all_to_all(rows, WIDE, 0, 0, tiled=True)  9.36 us
    all_to_all x1, blocking collectives, body(): lax.all_to_all(jnp.broadcast_to(valence, (8, *valence.shape)), NARROW, 0,...  7.84 us
    ppermute x2, starting transfers between devices, doubled(): far = lax.ppermute(pair, axis, [(i, i ^ 3) for i in range(4)])  7.49 us
    pallas_call x1, Pallas kernels, prepare(): pl.pallas_call(prepare_kernel, grid_spec=pltpu.PrefetchScalarGridSpec(num...  5.23 us
  transfers between devices with their start and end apart: 27, of which 13 were waited for; matrix products, arithmetic and copies ran while one was open for 4% of the time, Pallas kernels for 21%

profile of v3, /device:TPU:1, one launch (start us, length us, event | category | flops | bytes accessed | tf_op | source)
XLA Modules:
  0.0 156.6 jit_solution(13633630402764221473)
XLA Ops:
  0.0 2.0 %collective-permute-start = (f32[256,128]{1,0:T(8,128)}, f32[256,128]{1,0:T(8,128)S(1)}, u32[]{:S(2)}, u32[]{:S(2)}) collective-permute-start(f32[256,128]{1,0:T(8,128)} %bitcast.41), channel_id=1, source_target_pairs={{0,1},{1,2},{2,3},{3,0},{4,5},{5,6},{6,7},{7,4},{8,9},{9,10},{10,1... | collective-permute-start | bytes 393224 | tf_op jit(solution)/shard_map/ppermute | solution.py:364
  2.0 2.5 %collective-permute-start.1 = (f32[256,128]{1,0:T(8,128)}, f32[256,128]{1,0:T(8,128)S(1)}, u32[]{:S(2)}, u32[]{:S(2)}) collective-permute-start(f32[256,128]{1,0:T(8,128)} %bitcast.42), channel_id=1, source_target_pairs={{0,2},{1,3},{2,0},{3,1},{4,6},{5,7},{6,4},{7,5},{8,10},{9,11},{10,... | collective-permute-start | bytes 393224 | tf_op jit(solution)/shard_map/ppermute | solution.py:364
  4.5 1.2 collective-permute-start.2
  5.6 0.7 broadcast_in_dim.4
  6.3 7.8 %all_to_all.10 = f32[8,8,128]{2,1,0:T(8,128)S(1)} all-to-all(f32[8,8,128]{2,1,0:T(8,128)S(1)} %broadcast_in_dim.4), channel_id=1, replica_groups=mesh['zh'=4,'y'=4,'co'=2,'zl'=2,'x'=4] {'zl','x'}, dimensions={0} | all-to-all | bytes 65536 | tf_op jit(solution)/shard_map/all_to_all | solution.py:389
  14.2 3.1 %collective-permute-start.3 = (f32[8,8,128]{2,1,0:T(8,128)S(1)}, f32[8,8,128]{2,1,0:T(8,128)S(1)}, u32[]{:S(2)}, u32[]{:S(2)}) collective-permute-start(f32[8,8,128]{2,1,0:T(8,128)S(1)} %all_to_all.10), channel_id=1, source_target_pairs={{0,64},{64,0},{128,192},{192,128},{1,65},{65,1},{129,193},{193,129... | collective-permute-start | bytes 98312 | tf_op jit(solution)/shard_map/ppermute | solution.py:372
  17.3 1.7 %collective-permute-done.3 = f32[8,8,128]{2,1,0:T(8,128)S(1)} collective-permute-done((f32[8,8,128]{2,1,0:T(8,128)S(1)}, f32[8,8,128]{2,1,0:T(8,128)S(1)}, u32[]{:S(2)}, u32[]{:S(2)}) %collective-permute-start.3) | collective-permute-done | bytes 32800 | tf_op jit(solution)/shard_map/ppermute | solution.py:372
  19.0 4.7 %collective-permute-start.4 = (f32[2,8,8,128]{3,2,1,0:T(8,128)S(1)}, f32[2,8,8,128]{3,2,1,0:T(8,128)S(1)}, u32[]{:S(2)}, u32[]{:S(2)}) collective-permute-start(f32[2,8,8,128]{3,2,1,0:T(8,128)S(1)} %pad_maximum_fusion.7), channel_id=1, source_target_pairs={{0,192},{64,128},{128,64},{192,0},{1,193},{65,129},{129,65},{193,1... | collective-permute-start | bytes 196616 | tf_op jit(solution)/shard_map/ppermute | solution.py:373
  23.6 0.8 broadcast_subtract_fusion
  24.9 0.6 collective-permute-done.4
  25.6 1.4 collective-permute-start.5
  26.9 2.6 %collective-permute-done.5 = f32[4,8,8,128]{3,2,1,0:T(8,128)S(1)} collective-permute-done((f32[4,8,8,128]{3,2,1,0:T(8,128)S(1)}, f32[4,8,8,128]{3,2,1,0:T(8,128)S(1)}, u32[]{:S(2)}, u32[]{:S(2)}) %collective-permute-start.5) | collective-permute-done | bytes 131104 | tf_op jit(solution)/shard_map/ppermute | solution.py:372
  29.6 2.8 %collective-permute-start.6 = (f32[2,4,8,8,128]{4,3,2,1,0:T(8,128)S(1)}, f32[2,4,8,8,128]{4,3,2,1,0:T(8,128)S(1)}, u32[]{:S(2)}, u32[]{:S(2)}) collective-permute-start(f32[2,4,8,8,128]{4,3,2,1,0:T(8,128)S(1)} %pad_maximum_fusion.4), channel_id=1, source_target_pairs={{0,48},{16,32},{32,16},{48,0},{1,49},{17,33},{33,17},{49,1},{2,50}... | collective-permute-start | bytes 786440 | tf_op jit(solution)/shard_map/ppermute | solution.py:373
  32.4 3.8 %collective-permute-done.6 = f32[2,4,8,8,128]{4,3,2,1,0:T(8,128)S(1)} collective-permute-done((f32[2,4,8,8,128]{4,3,2,1,0:T(8,128)S(1)}, f32[2,4,8,8,128]{4,3,2,1,0:T(8,128)S(1)}, u32[]{:S(2)}, u32[]{:S(2)}) %collective-permute-start.6) | collective-permute-done | bytes 262176 | tf_op jit(solution)/shard_map/ppermute | solution.py:373
  36.3 6.9 %collective-permute-start.7 = (f32[4,4,8,8,128]{4,3,2,1,0:T(8,128)S(1)}, f32[4,4,8,8,128]{4,3,2,1,0:T(8,128)S(1)}, u32[]{:S(2)}, u32[]{:S(2)}) collective-permute-start(f32[4,4,8,8,128]{4,3,2,1,0:T(8,128)S(1)} %pad_maximum_fusion.1.refs_0_.refs_1_), channel_id=1, source_target_pairs={{0,8},{8,0},{1,9},{9,1},{2,10},{10,2},{3,11},{11,3},{4,12},{12,4},... | collective-permute-start | bytes 1572872 | tf_op jit(solution)/shard_map/ppermute | solution.py:364
  43.2 0.7 stack.71.pos
  43.8 0.9 collective-permute-done.7.refs_1_.refs_2_
  44.7 0.8 copy-done.6
  45.5 8.8 %row_pairs.1 = (bf16[32,16,256]{2,1,0:T(8,128)(2,1)}, bf16[416,256]{1,0:T(8,128)(2,1)}) custom-call(s32[5]{0:T(128)} %stack.71.pos, f32[4,4,8,8,128]{4,3,2,1,0:T(8,128)} %copy-done.3, f32[4,4,8,8,128]{4,3,2,1,0:T(8,128)} %copy-done.6, f32[256,128]{1,0:T(8,128)} %bitcast.44, bf16[1024,512]{1,0:T(8,128)(2,1)} %constant.38.clone.refs_3_.refs_6_, ...), custom_call_target="tpu_custom_call" | custom-call | flops 4000000000 | bytes 6291456 | tf_op jit(solution)/shard_map/row_pairs/pallas_call | solution.py:229
  54.4 9.4 %all-to-all-start.1 = ((bf16[32,16,256]{2,1,0:T(8,128)(2,1)}), bf16[32,16,256]{2,1,0:T(8,128)(2,1)S(1)}, u32[]{:S(2)}, u32[]{:S(2)}) async-start(bf16[32,16,256]{2,1,0:T(8,128)(2,1)} %get-tuple-element.38), calls=%async_computation.1 | async-start | bytes 524288 | tf_op jit(solution)/shard_map/all_to_all | solution.py:398
  63.8 9.9 %column_pairs.1 = bf16[2,4,16,640]{3,2,1,0:T(8,128)(2,1)} custom-call(s32[5]{0:T(128)} %stack.71.pos, bf16[416,256]{1,0:T(8,128)(2,1)} %get-tuple-element.39.refs_0_, f32[4,4,8,8,128]{4,3,2,1,0:T(8,128)} %copy-done.3, f32[4,4,8,8,128]{4,3,2,1,0:T(8,128)} %copy-done.6, f32[256,128]{1,0:T(8,128)} %copy-done.7, f32[256,128]{1,0:T(8,128)} %copy-done.8, ...), custom_call_target="tpu_custom_call" | custom-call | flops 8000000000 | bytes 6291456 | tf_op jit(solution)/shard_map/column_pairs/pallas_call | solution.py:229
  73.7 0.9 slice_bitcast_fusion
  74.7 2.2 %all-to-all-done.1 = bf16[32,16,256]{2,1,0:T(8,128)(2,1)S(1)} async-done(((bf16[32,16,256]{2,1,0:T(8,128)(2,1)}), bf16[32,16,256]{2,1,0:T(8,128)(2,1)S(1)}, u32[]{:S(2)}, u32[]{:S(2)}) %all-to-all-start.1) | async-done | bytes 262176 | tf_op jit(solution)/shard_map/all_to_all | solution.py:398
  76.8 1.6 %collective-permute-done.9 = bf16[4,16,640]{2,1,0:T(8,128)(2,1)S(1)} collective-permute-done((bf16[4,16,640]{2,1,0:T(8,128)(2,1)S(1)}, bf16[4,16,640]{2,1,0:T(8,128)(2,1)S(1)}, u32[]{:S(2)}, u32[]{:S(2)}) %collective-permute-start.9) | collective-permute-done | bytes 81952 | tf_op jit(solution)/shard_map/ppermute | solution.py:364
  78.4 0.9 broadcast_select_fusion.1
  79.4 5.6 %collective-permute-done.8 = bf16[32,16,256]{2,1,0:T(8,128)(2,1)S(1)} collective-permute-done((bf16[32,16,256]{2,1,0:T(8,128)(2,1)S(1)}, bf16[32,16,256]{2,1,0:T(8,128)(2,1)S(1)}, u32[]{:S(2)}, u32[]{:S(2)}) %collective-permute-start.8) | collective-permute-done | bytes 262176 | tf_op jit(solution)/shard_map/ppermute | solution.py:364
  85.3 2.4 %collective-permute-start.11 = (bf16[2,4,4,2,16,256]{5,4,3,2,1,0:T(8,128)(2,1)S(1)}, bf16[2,4,4,2,16,256]{5,4,3,2,1,0:T(8,128)(2,1)S(1)}, u32[]{:S(2)}, u32[]{:S(2)}) collective-permute-start(bf16[2,4,4,2,16,256]{5,4,3,2,1,0:T(8,128)(2,1)S(1)} %pad_maximum_fusion.2.r0), channel_id=1, source_target_pairs={{0,3},{1,0},{2,1},{3,2},{4,7},{5,4},{6,5},{7,6},{8,11},{9,8},{10,9... | collective-permute-start | bytes 1572872 | tf_op jit(solution)/shard_map/ppermute | solution.py:364
  87.8 1.5 collective-permute-start.12
  89.3 2.1 %collective-permute-start.13 = (bf16[8,16,640]{2,1,0:T(8,128)(2,1)S(1)}, bf16[8,16,640]{2,1,0:T(8,128)(2,1)S(1)}, u32[]{:S(2)}, u32[]{:S(2)}) collective-permute-start(bf16[8,16,640]{2,1,0:T(8,128)(2,1)S(1)} %pad_maximum_fusion.5), channel_id=1, source_target_pairs={{0,192},{64,0},{128,64},{192,128},{1,193},{65,1},{129,65},{193,129... | collective-permute-start | bytes 491528 | tf_op jit(solution)/shard_map/ppermute | solution.py:364
  91.3 7.6 %collective-permute-done.12 = bf16[8,16,640]{2,1,0:T(8,128)(2,1)S(1)} collective-permute-done((bf16[8,16,640]{2,1,0:T(8,128)(2,1)S(1)}, bf16[8,16,640]{2,1,0:T(8,128)(2,1)S(1)}, u32[]{:S(2)}, u32[]{:S(2)}) %collective-permute-start.12) | collective-permute-done | bytes 163872 | tf_op jit(solution)/shard_map/ppermute | solution.py:364
  99.0 0.9 collective-permute-done.13
  100.0 1.6 %collective-permute-start.14 = (bf16[1,4,4,2,16,256]{5,4,3,2,1,0:T(8,128)(2,1)S(1)}, bf16[1,4,4,2,16,256]{5,4,3,2,1,0:T(8,128)(2,1)S(1)}, u32[]{:S(2)}, u32[]{:S(2)}) collective-permute-start(bf16[1,4,4,2,16,256]{5,4,3,2,1,0:T(8,128)(2,1)S(1)} %slice.42), channel_id=1, source_target_pairs={{0,3},{1,0},{2,1},{3,2},{4,7},{5,4},{6,5},{7,6},{8,11},{9,8},{10,9... | collective-permute-start | bytes 786440 | tf_op jit(solution)/shard_map/ppermute | solution.py:364
  101.7 2.8 %collective-permute-start.16 = (bf16[4,16,640]{2,1,0:T(8,128)(2,1)S(1)}, bf16[4,16,640]{2,1,0:T(8,128)(2,1)S(1)}, u32[]{:S(2)}, u32[]{:S(2)}) collective-permute-start(bf16[4,16,640]{2,1,0:T(8,128)(2,1)S(1)} %slice.44), channel_id=1, source_target_pairs={{0,192},{64,0},{128,64},{192,128},{1,193},{65,1},{129,65},{193,129... | collective-permute-start | bytes 245768 | tf_op jit(solution)/shard_map/ppermute | solution.py:364
  104.6 2.0 %collective-permute-done.16 = bf16[4,16,640]{2,1,0:T(8,128)(2,1)S(1)} collective-permute-done((bf16[4,16,640]{2,1,0:T(8,128)(2,1)S(1)}, bf16[4,16,640]{2,1,0:T(8,128)(2,1)S(1)}, u32[]{:S(2)}, u32[]{:S(2)}) %collective-permute-start.16) | collective-permute-done | bytes 81952 | tf_op jit(solution)/shard_map/ppermute | solution.py:364
  106.6 3.4 %collective-permute-done.17 = bf16[4,16,640]{2,1,0:T(8,128)(2,1)S(1)} collective-permute-done((bf16[4,16,640]{2,1,0:T(8,128)(2,1)S(1)}, bf16[4,16,640]{2,1,0:T(8,128)(2,1)S(1)}, u32[]{:S(2)}, u32[]{:S(2)}) %collective-permute-start.17) | collective-permute-done | bytes 81952 | tf_op jit(solution)/shard_map/ppermute | solution.py:364
  110.2 0.8 collective-permute-start.18
  111.0 1.9 %collective-permute-start.19 = (bf16[4,8,16,640]{3,2,1,0:T(8,128)(2,1)S(1)}, bf16[4,8,16,640]{3,2,1,0:T(8,128)(2,1)S(1)}, u32[]{:S(2)}, u32[]{:S(2)}) collective-permute-start(bf16[4,8,16,640]{3,2,1,0:T(8,128)(2,1)S(1)} %pad_maximum_fusion.mine), channel_id=1, source_target_pairs={{0,48},{16,0},{32,16},{48,32},{1,49},{17,1},{33,17},{49,33},{2,50}... | collective-permute-start | bytes 1966088 | tf_op jit(solution)/shard_map/ppermute | solution.py:364
  112.9 4.2 %collective-permute-start.21 = (bf16[4,8,16,640]{3,2,1,0:T(8,128)(2,1)S(1)}, bf16[4,8,16,640]{3,2,1,0:T(8,128)(2,1)S(1)}, u32[]{:S(2)}, u32[]{:S(2)}) collective-permute-start(bf16[4,8,16,640]{3,2,1,0:T(8,128)(2,1)S(1)} %pad_maximum_fusion.mine), channel_id=1, source_target_pairs={{0,8},{8,0},{1,9},{9,1},{2,10},{10,2},{3,11},{11,3},{4,12},{12,4},... | collective-permute-start | bytes 1966088 | tf_op jit(solution)/shard_map/ppermute | solution.py:364
  117.1 0.9 pad_maximum_fusion.3.r2
  118.0 5.2 %scaled_rows.1 = (bf16[4,1536,1024]{2,1,0:T(8,128)(2,1)S(1)}, bf16[4,640,256]{2,1,0:T(8,128)(2,1)S(1)}, f32[4,16,256]{2,1,0:T(8,128)S(1)}) custom-call(s32[5]{0:T(128)S(1)} %copy-done, f32[6]{0:T(128)S(1)} %copy-done.1, bf16[2,4,4,2,16,256]{5,4,3,2,1,0:T(8,128)(2,1)} %copy-done.2, bf16[2,4,4,2,16,256]{5,4,3,2,1,0:T(8,128)(2,1)} %copy-done.4, ...), custom_call_target="tpu_custom_call" | custom-call | flops 1000000000 | bytes 20971520 | tf_op jit(solution)/shard_map/scaled_rows/pallas_call | solution.py:303
  123.3 0.8 collective-permute-done.18.mine
  124.0 4.6 %collective-permute-start.20 = (bf16[4,8,16,640]{3,2,1,0:T(8,128)(2,1)S(1)}, bf16[4,8,16,640]{3,2,1,0:T(8,128)(2,1)S(1)}, u32[]{:S(2)}, u32[]{:S(2)}) collective-permute-start(bf16[4,8,16,640]{3,2,1,0:T(8,128)(2,1)S(1)} %collective-permute-done.18.mine), channel_id=1, source_target_pairs={{0,8},{8,0},{1,9},{9,1},{2,10},{10,2},{3,11},{11,3},{4,12},{12,4},... | collective-permute-start | bytes 1966088 | tf_op jit(solution)/shard_map/ppermute | solution.py:364
  128.8 2.8 %collective-permute-start.22 = (bf16[2,8,16,640]{3,2,1,0:T(8,128)(2,1)S(1)}, bf16[2,8,16,640]{3,2,1,0:T(8,128)(2,1)S(1)}, u32[]{:S(2)}, u32[]{:S(2)}) collective-permute-start(bf16[2,8,16,640]{3,2,1,0:T(8,128)(2,1)S(1)} %slice.46), channel_id=1, source_target_pairs={{0,48},{16,0},{32,16},{48,32},{1,49},{17,1},{33,17},{49,33},{2,50}... | collective-permute-start | bytes 983048 | tf_op jit(solution)/shard_map/ppermute | solution.py:364
  131.5 5.3 %response_product.4.refs_0_ = f32[6,256,1024]{2,1,0:T(8,128)S(1)} custom-call(bf16[4,8,16,640]{3,2,1,0:T(8,128)(2,1)S(1)} %pad_maximum_fusion.mine, bf16[4,8,16,640]{3,2,1,0:T(8,128)(2,1)S(1)} %collective-permute-done.21.theirs, bf16[4,1536,1024]{2,1,0:T(8,128)(2,1)S(1)} %get-tuple-element.58.scaled, bf16[4,640,256]{2,1,0:T(8,128)(2,1)S(1)} %get-tuple-element.59.hot, ...), custom_call_target="tpu_custom_call" | custom-call | flops 4600000000 | bytes 10485760 | tf_op jit(solution)/shard_map/response_product/pallas_call | solution.py:348
  136.9 5.8 %response_product.5.refs_0_ = f32[6,256,1024]{2,1,0:T(8,128)S(1)} custom-call(bf16[4,8,16,640]{3,2,1,0:T(8,128)(2,1)S(1)} %collective-permute-done.18.mine, bf16[4,8,16,640]{3,2,1,0:T(8,128)(2,1)S(1)} %collective-permute-done.20.theirs, bf16[4,1536,1024]{2,1,0:T(8,128)(2,1)S(1)} %get-tuple-element.58.scaled, ...), custom_call_target="tpu_custom_call", output_to_operand_aliasing={{}: (5, {})} | custom-call | flops 4600000000 | bytes 10485760 | tf_op jit(solution)/shard_map/response_product/pallas_call | solution.py:348
  142.8 0.8 collective-permute-start.24
  143.6 5.8 %response_product.6.refs_0_ = f32[6,256,1024]{2,1,0:T(8,128)S(1)} custom-call(bf16[4,8,16,640]{3,2,1,0:T(8,128)(2,1)S(1)} %collective-permute-done.19.mine, bf16[4,8,16,640]{3,2,1,0:T(8,128)(2,1)S(1)} %collective-permute-done.25.theirs, bf16[4,1536,1024]{2,1,0:T(8,128)(2,1)S(1)} %get-tuple-element.58.scaled, ...), custom_call_target="tpu_custom_call", output_to_operand_aliasing={{}: (5, {})} | custom-call | flops 4600000000 | bytes 10485760 | tf_op jit(solution)/shard_map/response_product/pallas_call | solution.py:348
  149.4 7.2 %response_product.7 = f32[6,256,1024]{2,1,0:T(8,128)} custom-call(bf16[4,8,16,640]{3,2,1,0:T(8,128)(2,1)S(1)} %constant_dynamic-update-slice_fusion.mine, bf16[4,8,16,640]{3,2,1,0:T(8,128)(2,1)S(1)} %collective-permute-done.24.theirs, bf16[4,1536,1024]{2,1,0:T(8,128)(2,1)S(1)} %get-tuple-element.58.scaled, bf16[4,640,256]{2,1,0:T(8,128)(2,1)S(1)} %get-tuple-element.59.hot, ...), custom_call_target="tpu_custom_call" | custom-call | flops 4600000000 | bytes 10485760 | tf_op jit(solution)/shard_map/response_product/pallas_call | solution.py:348
  (60 shorter events, 1.7 us)
Async XLA Ops:
  0.0 14.2 %collective-permute-start = (f32[256,128]{1,0:T(8,128)}, f32[256,128]{1,0:T(8,128)S(1)}, u32[]{:S(2)}, u32[]{:S(2)}) collective-permute-start(f32[256,128]{1,0:T(8,128)} %bitcast.41), channel_id=1, source_target_pairs={{0,1},{1,2},{2,3},{3,0},{4,5},{5,6},{6,7},{7,4},{8,9},{9,10},{10,1... | collective-permute-start | bytes 393224 | tf_op jit(solution)/shard_map/ppermute | solution.py:364
  2.0 12.1 %collective-permute-start.1 = (f32[256,128]{1,0:T(8,128)}, f32[256,128]{1,0:T(8,128)S(1)}, u32[]{:S(2)}, u32[]{:S(2)}) collective-permute-start(f32[256,128]{1,0:T(8,128)} %bitcast.42), channel_id=1, source_target_pairs={{0,2},{1,3},{2,0},{3,1},{4,6},{5,7},{6,4},{7,5},{8,10},{9,11},{10,... | collective-permute-start | bytes 393224 | tf_op jit(solution)/shard_map/ppermute | solution.py:364
  4.5 9.7 %collective-permute-start.2 = (f32[256,128]{1,0:T(8,128)}, f32[256,128]{1,0:T(8,128)S(1)}, u32[]{:S(2)}, u32[]{:S(2)}) collective-permute-start(f32[256,128]{1,0:T(8,128)} %bitcast.43), channel_id=1, source_target_pairs={{0,3},{1,0},{2,1},{3,2},{4,7},{5,4},{6,5},{7,6},{8,11},{9,8},{10,9... | collective-permute-start | bytes 393224 | tf_op jit(solution)/shard_map/ppermute | solution.py:364
  14.2 40.2 %copy-start.7 = (f32[256,128]{1,0:T(8,128)}, f32[256,128]{1,0:T(8,128)S(1)}, u32[]{:S(2)}) copy-start(f32[256,128]{1,0:T(8,128)S(1)} %collective-permute-done.refs_3_) | copy-start | bytes 393220
  14.2 40.2 %copy-start.8 = (f32[256,128]{1,0:T(8,128)}, f32[256,128]{1,0:T(8,128)S(1)}, u32[]{:S(2)}) copy-start(f32[256,128]{1,0:T(8,128)S(1)} %collective-permute-done.1.refs_4_) | copy-start | bytes 393220
  14.2 40.2 %copy-start.9 = (f32[256,128]{1,0:T(8,128)}, f32[256,128]{1,0:T(8,128)S(1)}, u32[]{:S(2)}) copy-start(f32[256,128]{1,0:T(8,128)S(1)} %collective-permute-done.2.refs_5_) | copy-start | bytes 393220
  14.2 4.7 %collective-permute-start.3 = (f32[8,8,128]{2,1,0:T(8,128)S(1)}, f32[8,8,128]{2,1,0:T(8,128)S(1)}, u32[]{:S(2)}, u32[]{:S(2)}) collective-permute-start(f32[8,8,128]{2,1,0:T(8,128)S(1)} %all_to_all.10), channel_id=1, source_target_pairs={{0,64},{64,0},{128,192},{192,128},{1,65},{65,1},{129,193},{193,129... | collective-permute-start | bytes 98312 | tf_op jit(solution)/shard_map/ppermute | solution.py:372
  19.0 6.6 %collective-permute-start.4 = (f32[2,8,8,128]{3,2,1,0:T(8,128)S(1)}, f32[2,8,8,128]{3,2,1,0:T(8,128)S(1)}, u32[]{:S(2)}, u32[]{:S(2)}) collective-permute-start(f32[2,8,8,128]{3,2,1,0:T(8,128)S(1)} %pad_maximum_fusion.7), channel_id=1, source_target_pairs={{0,192},{64,128},{128,64},{192,0},{1,193},{65,129},{129,65},{193,1... | collective-permute-start | bytes 196616 | tf_op jit(solution)/shard_map/ppermute | solution.py:373
  25.6 4.0 %collective-permute-start.5 = (f32[4,8,8,128]{3,2,1,0:T(8,128)S(1)}, f32[4,8,8,128]{3,2,1,0:T(8,128)S(1)}, u32[]{:S(2)}, u32[]{:S(2)}) collective-permute-start(f32[4,8,8,128]{3,2,1,0:T(8,128)S(1)} %pad_maximum_fusion.6), channel_id=1, source_target_pairs={{0,16},{16,0},{32,48},{48,32},{1,17},{17,1},{33,49},{49,33},{2,18}... | collective-permute-start | bytes 393224 | tf_op jit(solution)/shard_map/ppermute | solution.py:372
  29.6 6.6 %collective-permute-start.6 = (f32[2,4,8,8,128]{4,3,2,1,0:T(8,128)S(1)}, f32[2,4,8,8,128]{4,3,2,1,0:T(8,128)S(1)}, u32[]{:S(2)}, u32[]{:S(2)}) collective-permute-start(f32[2,4,8,8,128]{4,3,2,1,0:T(8,128)S(1)} %pad_maximum_fusion.4), channel_id=1, source_target_pairs={{0,48},{16,32},{32,16},{48,0},{1,49},{17,33},{33,17},{49,1},{2,50}... | collective-permute-start | bytes 786440 | tf_op jit(solution)/shard_map/ppermute | solution.py:373
  36.2 8.5 %copy-start.3 = (f32[4,4,8,8,128]{4,3,2,1,0:T(8,128)}, f32[4,4,8,8,128]{4,3,2,1,0:T(8,128)S(1)}, u32[]{:S(2)}) copy-start(f32[4,4,8,8,128]{4,3,2,1,0:T(8,128)S(1)} %pad_maximum_fusion.1.refs_0_.refs_1_) | copy-start | bytes 1572868
  36.3 8.5 %collective-permute-start.7 = (f32[4,4,8,8,128]{4,3,2,1,0:T(8,128)S(1)}, f32[4,4,8,8,128]{4,3,2,1,0:T(8,128)S(1)}, u32[]{:S(2)}, u32[]{:S(2)}) collective-permute-start(f32[4,4,8,8,128]{4,3,2,1,0:T(8,128)S(1)} %pad_maximum_fusion.1.refs_0_.refs_1_), channel_id=1, source_target_pairs={{0,8},{8,0},{1,9},{9,1},{2,10},{10,2},{3,11},{11,3},{4,12},{12,4},... | collective-permute-start | bytes 1572872 | tf_op jit(solution)/shard_map/ppermute | solution.py:364
  44.7 0.8 copy-start.6
  54.4 22.5 %all-to-all-start.1 = ((bf16[32,16,256]{2,1,0:T(8,128)(2,1)}), bf16[32,16,256]{2,1,0:T(8,128)(2,1)S(1)}, u32[]{:S(2)}, u32[]{:S(2)}) async-start(bf16[32,16,256]{2,1,0:T(8,128)(2,1)} %get-tuple-element.38), calls=%async_computation.1 | async-start | bytes 524288 | tf_op jit(solution)/shard_map/all_to_all | solution.py:398
  63.7 54.3 %copy-start = (s32[5]{0:T(128)S(1)}, s32[5]{0:T(128)}, u32[]{:S(2)}) copy-start(s32[5]{0:T(128)} %stack.71.pos) | copy-start | bytes 64
  63.8 54.3 %copy-start.1 = (f32[6]{0:T(128)S(1)}, f32[6]{0:T(128)}, u32[]{:S(2)}) copy-start(f32[6]{0:T(128)} %omega.1) | copy-start | bytes 76
  74.6 3.8 %collective-permute-start.9 = (bf16[4,16,640]{2,1,0:T(8,128)(2,1)S(1)}, bf16[4,16,640]{2,1,0:T(8,128)(2,1)S(1)}, u32[]{:S(2)}, u32[]{:S(2)}) collective-permute-start(bf16[4,16,640]{2,1,0:T(8,128)(2,1)S(1)} %slice_bitcast_fusion), channel_id=1, source_target_pairs={{0,4},{4,0},{1,5},{5,1},{2,6},{6,2},{3,7},{7,3},{8,12},{12,8},{9,1... | collective-permute-start | bytes 245768 | tf_op jit(solution)/shard_map/ppermute | solution.py:364
  76.8 8.1 %collective-permute-start.8 = (bf16[32,16,256]{2,1,0:T(8,128)(2,1)S(1)}, bf16[32,16,256]{2,1,0:T(8,128)(2,1)S(1)}, u32[]{:S(2)}, u32[]{:S(2)}) collective-permute-start(bf16[32,16,256]{2,1,0:T(8,128)(2,1)S(1)} %all-to-all-done.1), channel_id=1, source_target_pairs={{0,4},{4,0},{1,5},{5,1},{2,6},{6,2},{3,7},{7,3},{8,12},{12,8},{9,1... | collective-permute-start | bytes 786440 | tf_op jit(solution)/shard_map/ppermute | solution.py:364
  85.0 33.0 %copy-start.2 = (bf16[2,4,4,2,16,256]{5,4,3,2,1,0:T(8,128)(2,1)}, bf16[2,4,4,2,16,256]{5,4,3,2,1,0:T(8,128)(2,1)S(1)}, u32[]{:S(2)}) copy-start(bf16[2,4,4,2,16,256]{5,4,3,2,1,0:T(8,128)(2,1)S(1)} %pad_maximum_fusion.2.r0) | copy-start | bytes 1572868
  85.0 14.9 %collective-permute-start.10 = (bf16[2,4,4,2,16,256]{5,4,3,2,1,0:T(8,128)(2,1)S(1)}, bf16[2,4,4,2,16,256]{5,4,3,2,1,0:T(8,128)(2,1)S(1)}, u32[]{:S(2)}, u32[]{:S(2)}) collective-permute-start(bf16[2,4,4,2,16,256]{5,4,3,2,1,0:T(8,128)(2,1)S(1)} %pad_maximum_fusion.2.r0), channel_id=1, source_target_pairs={{0,1},{1,2},{2,3},{3,0},{4,5},{5,6},{6,7},{7,4},{8,9},{9,10},{10,1... | collective-permute-start | bytes 1572872 | tf_op jit(solution)/shard_map/ppermute | solution.py:364
  85.3 14.6 %collective-permute-start.11 = (bf16[2,4,4,2,16,256]{5,4,3,2,1,0:T(8,128)(2,1)S(1)}, bf16[2,4,4,2,16,256]{5,4,3,2,1,0:T(8,128)(2,1)S(1)}, u32[]{:S(2)}, u32[]{:S(2)}) collective-permute-start(bf16[2,4,4,2,16,256]{5,4,3,2,1,0:T(8,128)(2,1)S(1)} %pad_maximum_fusion.2.r0), channel_id=1, source_target_pairs={{0,3},{1,0},{2,1},{3,2},{4,7},{5,4},{6,5},{7,6},{8,11},{9,8},{10,9... | collective-permute-start | bytes 1572872 | tf_op jit(solution)/shard_map/ppermute | solution.py:364
  87.8 11.2 %collective-permute-start.12 = (bf16[8,16,640]{2,1,0:T(8,128)(2,1)S(1)}, bf16[8,16,640]{2,1,0:T(8,128)(2,1)S(1)}, u32[]{:S(2)}, u32[]{:S(2)}) collective-permute-start(bf16[8,16,640]{2,1,0:T(8,128)(2,1)S(1)} %pad_maximum_fusion.5), channel_id=1, source_target_pairs={{0,64},{64,128},{128,192},{192,0},{1,65},{65,129},{129,193},{193,1... | collective-permute-start | bytes 491528 | tf_op jit(solution)/shard_map/ppermute | solution.py:364
  89.3 10.7 %collective-permute-start.13 = (bf16[8,16,640]{2,1,0:T(8,128)(2,1)S(1)}, bf16[8,16,640]{2,1,0:T(8,128)(2,1)S(1)}, u32[]{:S(2)}, u32[]{:S(2)}) collective-permute-start(bf16[8,16,640]{2,1,0:T(8,128)(2,1)S(1)} %pad_maximum_fusion.5), channel_id=1, source_target_pairs={{0,192},{64,0},{128,64},{192,128},{1,193},{65,1},{129,65},{193,129... | collective-permute-start | bytes 491528 | tf_op jit(solution)/shard_map/ppermute | solution.py:364
  99.9 18.1 %copy-start.4 = (bf16[2,4,4,2,16,256]{5,4,3,2,1,0:T(8,128)(2,1)}, bf16[2,4,4,2,16,256]{5,4,3,2,1,0:T(8,128)(2,1)S(1)}, u32[]{:S(2)}) copy-start(bf16[2,4,4,2,16,256]{5,4,3,2,1,0:T(8,128)(2,1)S(1)} %collective-permute-done.10.r1) | copy-start | bytes 1572868
  99.9 18.1 %copy-start.5 = (bf16[2,4,4,2,16,256]{5,4,3,2,1,0:T(8,128)(2,1)}, bf16[2,4,4,2,16,256]{5,4,3,2,1,0:T(8,128)(2,1)S(1)}, u32[]{:S(2)}) copy-start(bf16[2,4,4,2,16,256]{5,4,3,2,1,0:T(8,128)(2,1)S(1)} %collective-permute-done.11.r3) | copy-start | bytes 1572868
  100.0 10.1 %collective-permute-start.14 = (bf16[1,4,4,2,16,256]{5,4,3,2,1,0:T(8,128)(2,1)S(1)}, bf16[1,4,4,2,16,256]{5,4,3,2,1,0:T(8,128)(2,1)S(1)}, u32[]{:S(2)}, u32[]{:S(2)}) collective-permute-start(bf16[1,4,4,2,16,256]{5,4,3,2,1,0:T(8,128)(2,1)S(1)} %slice.42), channel_id=1, source_target_pairs={{0,3},{1,0},{2,1},{3,2},{4,7},{5,4},{6,5},{7,6},{8,11},{9,8},{10,9... | collective-permute-start | bytes 786440 | tf_op jit(solution)/shard_map/ppermute | solution.py:364
  101.6 8.4 %collective-permute-start.15 = (bf16[1,4,4,2,16,256]{5,4,3,2,1,0:T(8,128)(2,1)S(1)}, bf16[1,4,4,2,16,256]{5,4,3,2,1,0:T(8,128)(2,1)S(1)}, u32[]{:S(2)}, u32[]{:S(2)}) collective-permute-start(bf16[1,4,4,2,16,256]{5,4,3,2,1,0:T(8,128)(2,1)S(1)} %slice.43), channel_id=1, source_target_pairs={{0,1},{1,2},{2,3},{3,0},{4,5},{5,6},{6,7},{7,4},{8,9},{9,10},{10,1... | collective-permute-start | bytes 786440 | tf_op jit(solution)/shard_map/ppermute | solution.py:364
  101.7 4.9 %collective-permute-start.16 = (bf16[4,16,640]{2,1,0:T(8,128)(2,1)S(1)}, bf16[4,16,640]{2,1,0:T(8,128)(2,1)S(1)}, u32[]{:S(2)}, u32[]{:S(2)}) collective-permute-start(bf16[4,16,640]{2,1,0:T(8,128)(2,1)S(1)} %slice.44), channel_id=1, source_target_pairs={{0,192},{64,0},{128,64},{192,128},{1,193},{65,1},{129,65},{193,129... | collective-permute-start | bytes 245768 | tf_op jit(solution)/shard_map/ppermute | solution.py:364
  104.5 5.5 %collective-permute-start.17 = (bf16[4,16,640]{2,1,0:T(8,128)(2,1)S(1)}, bf16[4,16,640]{2,1,0:T(8,128)(2,1)S(1)}, u32[]{:S(2)}, u32[]{:S(2)}) collective-permute-start(bf16[4,16,640]{2,1,0:T(8,128)(2,1)S(1)} %slice.45), channel_id=1, source_target_pairs={{0,64},{64,128},{128,192},{192,0},{1,65},{65,129},{129,193},{193,1... | collective-permute-start | bytes 245768 | tf_op jit(solution)/shard_map/ppermute | solution.py:364
  110.2 13.9 %collective-permute-start.18 = (bf16[4,8,16,640]{3,2,1,0:T(8,128)(2,1)S(1)}, bf16[4,8,16,640]{3,2,1,0:T(8,128)(2,1)S(1)}, u32[]{:S(2)}, u32[]{:S(2)}) collective-permute-start(bf16[4,8,16,640]{3,2,1,0:T(8,128)(2,1)S(1)} %pad_maximum_fusion.mine), channel_id=1, source_target_pairs={{0,16},{16,32},{32,48},{48,0},{1,17},{17,33},{33,49},{49,1},{2,18}... | collective-permute-start | bytes 1966088 | tf_op jit(solution)/shard_map/ppermute | solution.py:364
  111.0 13.0 %collective-permute-start.19 = (bf16[4,8,16,640]{3,2,1,0:T(8,128)(2,1)S(1)}, bf16[4,8,16,640]{3,2,1,0:T(8,128)(2,1)S(1)}, u32[]{:S(2)}, u32[]{:S(2)}) collective-permute-start(bf16[4,8,16,640]{3,2,1,0:T(8,128)(2,1)S(1)} %pad_maximum_fusion.mine), channel_id=1, source_target_pairs={{0,48},{16,0},{32,16},{48,32},{1,49},{17,1},{33,17},{49,33},{2,50}... | collective-permute-start | bytes 1966088 | tf_op jit(solution)/shard_map/ppermute | solution.py:364
  112.9 18.6 %collective-permute-start.21 = (bf16[4,8,16,640]{3,2,1,0:T(8,128)(2,1)S(1)}, bf16[4,8,16,640]{3,2,1,0:T(8,128)(2,1)S(1)}, u32[]{:S(2)}, u32[]{:S(2)}) collective-permute-start(bf16[4,8,16,640]{3,2,1,0:T(8,128)(2,1)S(1)} %pad_maximum_fusion.mine), channel_id=1, source_target_pairs={{0,8},{8,0},{1,9},{9,1},{2,10},{10,2},{3,11},{11,3},{4,12},{12,4},... | collective-permute-start | bytes 1966088 | tf_op jit(solution)/shard_map/ppermute | solution.py:364
  124.0 12.9 %collective-permute-start.20 = (bf16[4,8,16,640]{3,2,1,0:T(8,128)(2,1)S(1)}, bf16[4,8,16,640]{3,2,1,0:T(8,128)(2,1)S(1)}, u32[]{:S(2)}, u32[]{:S(2)}) collective-permute-start(bf16[4,8,16,640]{3,2,1,0:T(8,128)(2,1)S(1)} %collective-permute-done.18.mine), channel_id=1, source_target_pairs={{0,8},{8,0},{1,9},{9,1},{2,10},{10,2},{3,11},{11,3},{4,12},{12,4},... | collective-permute-start | bytes 1966088 | tf_op jit(solution)/shard_map/ppermute | solution.py:364
  128.7 14.9 %collective-permute-start.25 = (bf16[4,8,16,640]{3,2,1,0:T(8,128)(2,1)S(1)}, bf16[4,8,16,640]{3,2,1,0:T(8,128)(2,1)S(1)}, u32[]{:S(2)}, u32[]{:S(2)}) collective-permute-start(bf16[4,8,16,640]{3,2,1,0:T(8,128)(2,1)S(1)} %collective-permute-done.19.mine), channel_id=1, source_target_pairs={{0,8},{8,0},{1,9},{9,1},{2,10},{10,2},{3,11},{11,3},{4,12},{12,4},... | collective-permute-start | bytes 1966088 | tf_op jit(solution)/shard_map/ppermute | solution.py:364
  128.8 13.9 %collective-permute-start.22 = (bf16[2,8,16,640]{3,2,1,0:T(8,128)(2,1)S(1)}, bf16[2,8,16,640]{3,2,1,0:T(8,128)(2,1)S(1)}, u32[]{:S(2)}, u32[]{:S(2)}) collective-permute-start(bf16[2,8,16,640]{3,2,1,0:T(8,128)(2,1)S(1)} %slice.46), channel_id=1, source_target_pairs={{0,48},{16,0},{32,16},{48,32},{1,49},{17,1},{33,17},{49,33},{2,50}... | collective-permute-start | bytes 983048 | tf_op jit(solution)/shard_map/ppermute | solution.py:364
  131.5 11.2 %collective-permute-start.23 = (bf16[2,8,16,640]{3,2,1,0:T(8,128)(2,1)S(1)}, bf16[2,8,16,640]{3,2,1,0:T(8,128)(2,1)S(1)}, u32[]{:S(2)}, u32[]{:S(2)}) collective-permute-start(bf16[2,8,16,640]{3,2,1,0:T(8,128)(2,1)S(1)} %slice.47), channel_id=1, source_target_pairs={{0,16},{16,32},{32,48},{48,0},{1,17},{17,33},{33,49},{49,1},{2,18}... | collective-permute-start | bytes 983048 | tf_op jit(solution)/shard_map/ppermute | solution.py:364
  142.8 6.6 %collective-permute-start.24 = (bf16[4,8,16,640]{3,2,1,0:T(8,128)(2,1)S(1)}, bf16[4,8,16,640]{3,2,1,0:T(8,128)(2,1)S(1)}, u32[]{:S(2)}, u32[]{:S(2)}) collective-permute-start(bf16[4,8,16,640]{3,2,1,0:T(8,128)(2,1)S(1)} %constant_dynamic-update-slice_fusion.mine), channel_id=1, source_target_pairs={{0,8},{8,0},{1,9},{9,1},{2,10},{10,2},{3,11},{11,3},{4,12},{12,4},... | collective-permute-start | bytes 1966088 | tf_op jit(solution)/shard_map/ppermute | solution.py:364

commit v4 on v2

--- a/solution.py
+++ b/solution.py
@@ -404,9 +404,11 @@
     cols = jnp.stack([cols, near_zh[0], jnp.concatenate(far_zh), near_zh[1]])
     near_y = neighbours(cols, "y")
     scaled, hot, sign = prepare(pos, omega, rows, gap, gmap, jnp.asarray(tables()[-1]))
+    hot, own_cols = lax.optimization_barrier((hot, cols))
+    theirs = shifted(own_cols, "co", 1)
     scaled, hot, sign, near_y = lax.optimization_barrier((scaled, hot, sign, near_y))
     far = opposite(*near_y, "y")
-    total = product_step(0, cols, shifted(cols, "co", 1), scaled, hot, sign, None, False)
+    total = product_step(0, cols, theirs, scaled, hot, sign, None, False)
     total = product_step(1, near_y[0], shifted(near_y[0], "co", 1), scaled, hot, sign, total, False)
     total, far = lax.optimization_barrier((total, far))
     for sy, mine in ((3, near_y[1]), (2, jnp.concatenate(far))):

time: 153 us -> 153 us (level)
  no operation moved by 1% of the time
where the time goes in v4:
time: 153 us; the launch traced here: 152 us
  starting transfers between devices  61.5 us (40%)
  Pallas kernels  48.5 us (32%)
  waiting for transfers between devices  27.7 us (18%)
  blocking collectives  7.84 us (5%)
  local copies, waits for them, and re-layouts  3.72 us (2%)
  other arithmetic  2.83 us (2%)
    ppermute x28, starting transfers between devices, shifted(): lax.ppermute(value, axis, [(i, (i + shift) % size) for i in range(size)])  54 us
    ppermute x28, waiting for transfers between devices, shifted(): lax.ppermute(value, axis, [(i, (i + shift) % size) for i in range(size)])  25.6 us
    pallas_call x4, Pallas kernels, product_step(): pl.pallas_call(kernel, grid=(4 if last else 1,), in_specs=[resident()] *...  24.4 us
    pallas_call x2, Pallas kernels, transform_call(): pl.pallas_call(kernel, grid_spec=pltpu.PrefetchScalarGridSpec(num_scalar_...  18.8 us
    all_to_all x1, blocking collectives, body(): lax.all_to_all(jnp.broadcast_to(valence, (8, *valence.shape)), NARROW, 0,...  7.84 us
    all_to_all x1, starting transfers between devices, body(): rows = lax.all_to_all(rows, WIDE, 0, 0, tiled=True)  7.58 us
    pallas_call x1, Pallas kernels, prepare(): pl.pallas_call(prepare_kernel, grid_spec=pltpu.PrefetchScalarGridSpec(num...  5.24 us
  transfers between devices with their start and end apart: 29, of which 13 were waited for; matrix products, arithmetic and copies ran while one was open for 4% of the time, Pallas kernels for 21%

profile of v4, /device:TPU:1, one launch (start us, length us, event | category | flops | bytes accessed | tf_op | source)
XLA Modules:
  0.0 152.4 jit_solution(4552254774836506548)
XLA Ops:
  0.0 2.0 %collective-permute-start = (f32[256,128]{1,0:T(8,128)}, f32[256,128]{1,0:T(8,128)S(1)}, u32[]{:S(2)}, u32[]{:S(2)}) collective-permute-start(f32[256,128]{1,0:T(8,128)} %bitcast.45), channel_id=1, source_target_pairs={{0,1},{1,2},{2,3},{3,0},{4,5},{5,6},{6,7},{7,4},{8,9},{9,10},{10,1... | collective-permute-start | bytes 393224 | tf_op jit(solution)/shard_map/ppermute | solution.py:364
  2.0 2.5 %collective-permute-start.1 = (f32[256,128]{1,0:T(8,128)}, f32[256,128]{1,0:T(8,128)S(1)}, u32[]{:S(2)}, u32[]{:S(2)}) collective-permute-start(f32[256,128]{1,0:T(8,128)} %bitcast.46), channel_id=1, source_target_pairs={{0,2},{1,3},{2,0},{3,1},{4,6},{5,7},{6,4},{7,5},{8,10},{9,11},{10,... | collective-permute-start | bytes 393224 | tf_op jit(solution)/shard_map/ppermute | solution.py:364
  4.5 1.2 collective-permute-start.2
  5.6 0.7 broadcast_in_dim.4
  6.3 7.8 %all_to_all.10 = f32[8,8,128]{2,1,0:T(8,128)S(1)} all-to-all(f32[8,8,128]{2,1,0:T(8,128)S(1)} %broadcast_in_dim.4), channel_id=1, replica_groups=mesh['zh'=4,'y'=4,'co'=2,'zl'=2,'x'=4] {'zl','x'}, dimensions={0} | all-to-all | bytes 65536 | tf_op jit(solution)/shard_map/all_to_all | solution.py:383
  14.2 3.1 %collective-permute-start.3 = (f32[8,8,128]{2,1,0:T(8,128)S(1)}, f32[8,8,128]{2,1,0:T(8,128)S(1)}, u32[]{:S(2)}, u32[]{:S(2)}) collective-permute-start(f32[8,8,128]{2,1,0:T(8,128)S(1)} %all_to_all.10), channel_id=1, source_target_pairs={{0,64},{64,128},{128,192},{192,0},{1,65},{65,129},{129,193},{193,1... | collective-permute-start | bytes 98312 | tf_op jit(solution)/shard_map/ppermute | solution.py:364
  17.3 4.7 %collective-permute-start.4 = (f32[8,8,128]{2,1,0:T(8,128)S(1)}, f32[8,8,128]{2,1,0:T(8,128)S(1)}, u32[]{:S(2)}, u32[]{:S(2)}) collective-permute-start(f32[8,8,128]{2,1,0:T(8,128)S(1)} %all_to_all.10), channel_id=1, source_target_pairs={{0,128},{64,192},{128,0},{192,64},{1,129},{65,193},{129,1},{193,65... | collective-permute-start | bytes 98312 | tf_op jit(solution)/shard_map/ppermute | solution.py:364
  22.0 2.4 %collective-permute-start.5 = (f32[8,8,128]{2,1,0:T(8,128)S(1)}, f32[8,8,128]{2,1,0:T(8,128)S(1)}, u32[]{:S(2)}, u32[]{:S(2)}) collective-permute-start(f32[8,8,128]{2,1,0:T(8,128)S(1)} %all_to_all.10), channel_id=1, source_target_pairs={{0,192},{64,0},{128,64},{192,128},{1,193},{65,1},{129,65},{193,129... | collective-permute-start | bytes 98312 | tf_op jit(solution)/shard_map/ppermute | solution.py:364
  24.4 0.8 broadcast_subtract_fusion
  25.3 0.4 reshape.39
  25.7 0.4 collective-permute-done.5
  26.2 1.4 collective-permute-start.6
  27.5 2.6 %collective-permute-start.7 = (f32[4,8,8,128]{3,2,1,0:T(8,128)S(1)}, f32[4,8,8,128]{3,2,1,0:T(8,128)S(1)}, u32[]{:S(2)}, u32[]{:S(2)}) collective-permute-start(f32[4,8,8,128]{3,2,1,0:T(8,128)S(1)} %pad_maximum_fusion.5), channel_id=1, source_target_pairs={{0,32},{16,48},{32,0},{48,16},{1,33},{17,49},{33,1},{49,17},{2,34}... | collective-permute-start | bytes 393224 | tf_op jit(solution)/shard_map/ppermute | solution.py:364
  30.2 1.1 collective-permute-start.8
  31.3 2.6 %collective-permute-done.7 = f32[4,8,8,128]{3,2,1,0:T(8,128)S(1)} collective-permute-done((f32[4,8,8,128]{3,2,1,0:T(8,128)S(1)}, f32[4,8,8,128]{3,2,1,0:T(8,128)S(1)}, u32[]{:S(2)}, u32[]{:S(2)}) %collective-permute-start.7) | collective-permute-done | bytes 131104 | tf_op jit(solution)/shard_map/ppermute | solution.py:364
  34.0 6.2 %collective-permute-start.9 = (f32[4,4,8,8,128]{4,3,2,1,0:T(8,128)S(1)}, f32[4,4,8,8,128]{4,3,2,1,0:T(8,128)S(1)}, u32[]{:S(2)}, u32[]{:S(2)}) collective-permute-start(f32[4,4,8,8,128]{4,3,2,1,0:T(8,128)S(1)} %pad_maximum_fusion.1.refs_0_.refs_1_), channel_id=1, source_target_pairs={{0,8},{8,0},{1,9},{9,1},{2,10},{10,2},{3,11},{11,3},{4,12},{12,4},... | collective-permute-start | bytes 1572872 | tf_op jit(solution)/shard_map/ppermute | solution.py:364
  40.2 0.7 stack.77.pos
  40.9 0.9 collective-permute-done.9.refs_1_.refs_2_
  41.7 0.8 copy-done.6
  42.5 8.8 %row_pairs.1 = (bf16[32,16,256]{2,1,0:T(8,128)(2,1)}, bf16[416,256]{1,0:T(8,128)(2,1)}) custom-call(s32[5]{0:T(128)} %stack.77.pos, f32[4,4,8,8,128]{4,3,2,1,0:T(8,128)} %copy-done.3, f32[4,4,8,8,128]{4,3,2,1,0:T(8,128)} %copy-done.6, f32[256,128]{1,0:T(8,128)} %bitcast.48, bf16[1024,512]{1,0:T(8,128)(2,1)} %constant.38.clone.refs_3_.refs_6_, ...), custom_call_target="tpu_custom_call" | custom-call | flops 4000000000 | bytes 6291456 | tf_op jit(solution)/shard_map/row_pairs/pallas_call | solution.py:229
  51.4 7.6 %all-to-all-start.1 = ((bf16[32,16,256]{2,1,0:T(8,128)(2,1)}), bf16[32,16,256]{2,1,0:T(8,128)(2,1)S(1)}, u32[]{:S(2)}, u32[]{:S(2)}) async-start(bf16[32,16,256]{2,1,0:T(8,128)(2,1)} %get-tuple-element.40), calls=%async_computation.1 | async-start | bytes 524288 | tf_op jit(solution)/shard_map/all_to_all | solution.py:392
  59.0 9.9 %column_pairs.1 = bf16[2,4,16,640]{3,2,1,0:T(8,128)(2,1)} custom-call(s32[5]{0:T(128)} %stack.77.pos, bf16[416,256]{1,0:T(8,128)(2,1)} %get-tuple-element.41.refs_0_, f32[4,4,8,8,128]{4,3,2,1,0:T(8,128)} %copy-done.3, f32[4,4,8,8,128]{4,3,2,1,0:T(8,128)} %copy-done.6, f32[256,128]{1,0:T(8,128)} %copy-done.7, f32[256,128]{1,0:T(8,128)} %copy-done.8, ...), custom_call_target="tpu_custom_call" | custom-call | flops 8000000000 | bytes 6291456 | tf_op jit(solution)/shard_map/column_pairs/pallas_call | solution.py:229
  69.0 0.9 slice_bitcast_fusion
  70.0 2.1 %all-to-all-done.1 = bf16[32,16,256]{2,1,0:T(8,128)(2,1)S(1)} async-done(((bf16[32,16,256]{2,1,0:T(8,128)(2,1)}), bf16[32,16,256]{2,1,0:T(8,128)(2,1)S(1)}, u32[]{:S(2)}, u32[]{:S(2)}) %all-to-all-start.1) | async-done | bytes 262176 | tf_op jit(solution)/shard_map/all_to_all | solution.py:392
  72.1 1.4 collective-permute-done.11
  73.5 0.9 broadcast_select_fusion.1
  74.4 5.7 %collective-permute-done.10 = bf16[32,16,256]{2,1,0:T(8,128)(2,1)S(1)} collective-permute-done((bf16[32,16,256]{2,1,0:T(8,128)(2,1)S(1)}, bf16[32,16,256]{2,1,0:T(8,128)(2,1)S(1)}, u32[]{:S(2)}, u32[]{:S(2)}) %collective-permute-start.10) | collective-permute-done | bytes 262176 | tf_op jit(solution)/shard_map/ppermute | solution.py:364
  80.6 2.4 %collective-permute-start.13 = (bf16[2,4,4,2,16,256]{5,4,3,2,1,0:T(8,128)(2,1)S(1)}, bf16[2,4,4,2,16,256]{5,4,3,2,1,0:T(8,128)(2,1)S(1)}, u32[]{:S(2)}, u32[]{:S(2)}) collective-permute-start(bf16[2,4,4,2,16,256]{5,4,3,2,1,0:T(8,128)(2,1)S(1)} %pad_maximum_fusion.2.r0), channel_id=1, source_target_pairs={{0,3},{1,0},{2,1},{3,2},{4,7},{5,4},{6,5},{7,6},{8,11},{9,8},{10,9... | collective-permute-start | bytes 1572872 | tf_op jit(solution)/shard_map/ppermute | solution.py:364
  83.0 1.6 %collective-permute-start.14 = (bf16[8,16,640]{2,1,0:T(8,128)(2,1)S(1)}, bf16[8,16,640]{2,1,0:T(8,128)(2,1)S(1)}, u32[]{:S(2)}, u32[]{:S(2)}) collective-permute-start(bf16[8,16,640]{2,1,0:T(8,128)(2,1)S(1)} %pad_maximum_fusion.4), channel_id=1, source_target_pairs={{0,64},{64,128},{128,192},{192,0},{1,65},{65,129},{129,193},{193,1... | collective-permute-start | bytes 491528 | tf_op jit(solution)/shard_map/ppermute | solution.py:364
  84.5 2.0 %collective-permute-start.15 = (bf16[8,16,640]{2,1,0:T(8,128)(2,1)S(1)}, bf16[8,16,640]{2,1,0:T(8,128)(2,1)S(1)}, u32[]{:S(2)}, u32[]{:S(2)}) collective-permute-start(bf16[8,16,640]{2,1,0:T(8,128)(2,1)S(1)} %pad_maximum_fusion.4), channel_id=1, source_target_pairs={{0,192},{64,0},{128,64},{192,128},{1,193},{65,1},{129,65},{193,129... | collective-permute-start | bytes 491528 | tf_op jit(solution)/shard_map/ppermute | solution.py:364
  86.6 7.5 %collective-permute-done.14 = bf16[8,16,640]{2,1,0:T(8,128)(2,1)S(1)} collective-permute-done((bf16[8,16,640]{2,1,0:T(8,128)(2,1)S(1)}, bf16[8,16,640]{2,1,0:T(8,128)(2,1)S(1)}, u32[]{:S(2)}, u32[]{:S(2)}) %collective-permute-start.14) | collective-permute-done | bytes 163872 | tf_op jit(solution)/shard_map/ppermute | solution.py:364
  94.0 1.4 collective-permute-done.15
  95.4 1.3 collective-permute-start.16
  97.1 2.5 %collective-permute-start.18 = (bf16[4,16,640]{2,1,0:T(8,128)(2,1)S(1)}, bf16[4,16,640]{2,1,0:T(8,128)(2,1)S(1)}, u32[]{:S(2)}, u32[]{:S(2)}) collective-permute-start(bf16[4,16,640]{2,1,0:T(8,128)(2,1)S(1)} %slice.28), channel_id=1, source_target_pairs={{0,192},{64,0},{128,64},{192,128},{1,193},{65,1},{129,65},{193,129... | collective-permute-start | bytes 245768 | tf_op jit(solution)/shard_map/ppermute | solution.py:364
  99.7 2.1 %collective-permute-done.18 = bf16[4,16,640]{2,1,0:T(8,128)(2,1)S(1)} collective-permute-done((bf16[4,16,640]{2,1,0:T(8,128)(2,1)S(1)}, bf16[4,16,640]{2,1,0:T(8,128)(2,1)S(1)}, u32[]{:S(2)}, u32[]{:S(2)}) %collective-permute-start.18) | collective-permute-done | bytes 81952 | tf_op jit(solution)/shard_map/ppermute | solution.py:364
  101.8 3.4 %collective-permute-done.19 = bf16[4,16,640]{2,1,0:T(8,128)(2,1)S(1)} collective-permute-done((bf16[4,16,640]{2,1,0:T(8,128)(2,1)S(1)}, bf16[4,16,640]{2,1,0:T(8,128)(2,1)S(1)}, u32[]{:S(2)}, u32[]{:S(2)}) %collective-permute-start.19) | collective-permute-done | bytes 81952 | tf_op jit(solution)/shard_map/ppermute | solution.py:364
  105.4 1.2 collective-permute-start.20
  106.6 1.5 %collective-permute-start.21 = (bf16[4,8,16,640]{3,2,1,0:T(8,128)(2,1)S(1)}, bf16[4,8,16,640]{3,2,1,0:T(8,128)(2,1)S(1)}, u32[]{:S(2)}, u32[]{:S(2)}) collective-permute-start(bf16[4,8,16,640]{3,2,1,0:T(8,128)(2,1)S(1)} %pad_maximum_fusion.mine), channel_id=1, source_target_pairs={{0,48},{16,0},{32,16},{48,32},{1,49},{17,1},{33,17},{49,33},{2,50}... | collective-permute-start | bytes 1966088 | tf_op jit(solution)/shard_map/ppermute | solution.py:364
  108.1 0.9 pad_maximum_fusion.3.r2
  109.0 5.2 %scaled_rows.1 = (bf16[4,1536,1024]{2,1,0:T(8,128)(2,1)S(1)}, bf16[4,640,256]{2,1,0:T(8,128)(2,1)S(1)}, f32[4,16,256]{2,1,0:T(8,128)S(1)}) custom-call(s32[5]{0:T(128)S(1)} %copy-done, f32[6]{0:T(128)S(1)} %copy-done.1, bf16[2,4,4,2,16,256]{5,4,3,2,1,0:T(8,128)(2,1)} %copy-done.2, bf16[2,4,4,2,16,256]{5,4,3,2,1,0:T(8,128)(2,1)} %copy-done.4, ...), custom_call_target="tpu_custom_call" | custom-call | flops 1000000000 | bytes 20971520 | tf_op jit(solution)/shard_map/scaled_rows/pallas_call | solution.py:303
  114.3 4.5 %collective-permute-start.23 = (bf16[4,8,16,640]{3,2,1,0:T(8,128)(2,1)S(1)}, bf16[4,8,16,640]{3,2,1,0:T(8,128)(2,1)S(1)}, u32[]{:S(2)}, u32[]{:S(2)}) collective-permute-start(bf16[4,8,16,640]{3,2,1,0:T(8,128)(2,1)S(1)} %pad_maximum_fusion.mine), channel_id=1, source_target_pairs={{0,8},{8,0},{1,9},{9,1},{2,10},{10,2},{3,11},{11,3},{4,12},{12,4},... | collective-permute-start | bytes 1966088 | tf_op jit(solution)/shard_map/ppermute | solution.py:364
  118.9 4.9 %collective-permute-start.22 = (bf16[4,8,16,640]{3,2,1,0:T(8,128)(2,1)S(1)}, bf16[4,8,16,640]{3,2,1,0:T(8,128)(2,1)S(1)}, u32[]{:S(2)}, u32[]{:S(2)}) collective-permute-start(bf16[4,8,16,640]{3,2,1,0:T(8,128)(2,1)S(1)} %collective-permute-done.20.mine), channel_id=1, source_target_pairs={{0,8},{8,0},{1,9},{9,1},{2,10},{10,2},{3,11},{11,3},{4,12},{12,4},... | collective-permute-start | bytes 1966088 | tf_op jit(solution)/shard_map/ppermute | solution.py:364
  124.0 2.8 %collective-permute-start.24 = (bf16[2,8,16,640]{3,2,1,0:T(8,128)(2,1)S(1)}, bf16[2,8,16,640]{3,2,1,0:T(8,128)(2,1)S(1)}, u32[]{:S(2)}, u32[]{:S(2)}) collective-permute-start(bf16[2,8,16,640]{3,2,1,0:T(8,128)(2,1)S(1)} %slice.30), channel_id=1, source_target_pairs={{0,48},{16,0},{32,16},{48,32},{1,49},{17,1},{33,17},{49,33},{2,50}... | collective-permute-start | bytes 983048 | tf_op jit(solution)/shard_map/ppermute | solution.py:364
  126.8 5.4 %response_product.4.refs_0_ = f32[6,256,1024]{2,1,0:T(8,128)S(1)} custom-call(bf16[4,8,16,640]{3,2,1,0:T(8,128)(2,1)S(1)} %pad_maximum_fusion.mine, bf16[4,8,16,640]{3,2,1,0:T(8,128)(2,1)S(1)} %collective-permute-done.23.theirs, bf16[4,1536,1024]{2,1,0:T(8,128)(2,1)S(1)} %get-tuple-element.61.scaled, bf16[4,640,256]{2,1,0:T(8,128)(2,1)S(1)} %get-tuple-element.62.hot, ...), custom_call_target="tpu_custom_call" | custom-call | flops 4600000000 | bytes 10485760 | tf_op jit(solution)/shard_map/response_product/pallas_call | solution.py:348
  132.2 5.9 %response_product.5.refs_0_ = f32[6,256,1024]{2,1,0:T(8,128)S(1)} custom-call(bf16[4,8,16,640]{3,2,1,0:T(8,128)(2,1)S(1)} %collective-permute-done.20.mine, bf16[4,8,16,640]{3,2,1,0:T(8,128)(2,1)S(1)} %collective-permute-done.22.theirs, bf16[4,1536,1024]{2,1,0:T(8,128)(2,1)S(1)} %get-tuple-element.61.scaled, ...), custom_call_target="tpu_custom_call", output_to_operand_aliasing={{}: (5, {})} | custom-call | flops 4600000000 | bytes 10485760 | tf_op jit(solution)/shard_map/response_product/pallas_call | solution.py:348
  138.2 1.0 collective-permute-start.26
  139.3 5.9 %response_product.6.refs_0_ = f32[6,256,1024]{2,1,0:T(8,128)S(1)} custom-call(bf16[4,8,16,640]{3,2,1,0:T(8,128)(2,1)S(1)} %collective-permute-done.21.mine, bf16[4,8,16,640]{3,2,1,0:T(8,128)(2,1)S(1)} %collective-permute-done.27.theirs, bf16[4,1536,1024]{2,1,0:T(8,128)(2,1)S(1)} %get-tuple-element.61.scaled, ...), custom_call_target="tpu_custom_call", output_to_operand_aliasing={{}: (5, {})} | custom-call | flops 4600000000 | bytes 10485760 | tf_op jit(solution)/shard_map/response_product/pallas_call | solution.py:348
  145.2 7.2 %response_product.7 = f32[6,256,1024]{2,1,0:T(8,128)} custom-call(bf16[4,8,16,640]{3,2,1,0:T(8,128)(2,1)S(1)} %constant_dynamic-update-slice_fusion.mine, bf16[4,8,16,640]{3,2,1,0:T(8,128)(2,1)S(1)} %collective-permute-done.26.theirs, bf16[4,1536,1024]{2,1,0:T(8,128)(2,1)S(1)} %get-tuple-element.61.scaled, bf16[4,640,256]{2,1,0:T(8,128)(2,1)S(1)} %get-tuple-element.62.hot, ...), custom_call_target="tpu_custom_call" | custom-call | flops 4600000000 | bytes 10485760 | tf_op jit(solution)/shard_map/response_product/pallas_call | solution.py:348
  (60 shorter events, 1.9 us)
Async XLA Ops:
  0.0 14.2 %collective-permute-start = (f32[256,128]{1,0:T(8,128)}, f32[256,128]{1,0:T(8,128)S(1)}, u32[]{:S(2)}, u32[]{:S(2)}) collective-permute-start(f32[256,128]{1,0:T(8,128)} %bitcast.45), channel_id=1, source_target_pairs={{0,1},{1,2},{2,3},{3,0},{4,5},{5,6},{6,7},{7,4},{8,9},{9,10},{10,1... | collective-permute-start | bytes 393224 | tf_op jit(solution)/shard_map/ppermute | solution.py:364
  2.0 12.1 %collective-permute-start.1 = (f32[256,128]{1,0:T(8,128)}, f32[256,128]{1,0:T(8,128)S(1)}, u32[]{:S(2)}, u32[]{:S(2)}) collective-permute-start(f32[256,128]{1,0:T(8,128)} %bitcast.46), channel_id=1, source_target_pairs={{0,2},{1,3},{2,0},{3,1},{4,6},{5,7},{6,4},{7,5},{8,10},{9,11},{10,... | collective-permute-start | bytes 393224 | tf_op jit(solution)/shard_map/ppermute | solution.py:364
  4.5 9.7 %collective-permute-start.2 = (f32[256,128]{1,0:T(8,128)}, f32[256,128]{1,0:T(8,128)S(1)}, u32[]{:S(2)}, u32[]{:S(2)}) collective-permute-start(f32[256,128]{1,0:T(8,128)} %bitcast.47), channel_id=1, source_target_pairs={{0,3},{1,0},{2,1},{3,2},{4,7},{5,4},{6,5},{7,6},{8,11},{9,8},{10,9... | collective-permute-start | bytes 393224 | tf_op jit(solution)/shard_map/ppermute | solution.py:364
  14.2 37.2 %copy-start.7 = (f32[256,128]{1,0:T(8,128)}, f32[256,128]{1,0:T(8,128)S(1)}, u32[]{:S(2)}) copy-start(f32[256,128]{1,0:T(8,128)S(1)} %collective-permute-done.refs_3_) | copy-start | bytes 393220
  14.2 37.2 %copy-start.8 = (f32[256,128]{1,0:T(8,128)}, f32[256,128]{1,0:T(8,128)S(1)}, u32[]{:S(2)}) copy-start(f32[256,128]{1,0:T(8,128)S(1)} %collective-permute-done.1.refs_4_) | copy-start | bytes 393220
  14.2 37.2 %copy-start.9 = (f32[256,128]{1,0:T(8,128)}, f32[256,128]{1,0:T(8,128)S(1)}, u32[]{:S(2)}) copy-start(f32[256,128]{1,0:T(8,128)S(1)} %collective-permute-done.2.refs_5_) | copy-start | bytes 393220
  14.2 11.5 %collective-permute-start.3 = (f32[8,8,128]{2,1,0:T(8,128)S(1)}, f32[8,8,128]{2,1,0:T(8,128)S(1)}, u32[]{:S(2)}, u32[]{:S(2)}) collective-permute-start(f32[8,8,128]{2,1,0:T(8,128)S(1)} %all_to_all.10), channel_id=1, source_target_pairs={{0,64},{64,128},{128,192},{192,0},{1,65},{65,129},{129,193},{193,1... | collective-permute-start | bytes 98312 | tf_op jit(solution)/shard_map/ppermute | solution.py:364
  17.3 8.4 %collective-permute-start.4 = (f32[8,8,128]{2,1,0:T(8,128)S(1)}, f32[8,8,128]{2,1,0:T(8,128)S(1)}, u32[]{:S(2)}, u32[]{:S(2)}) collective-permute-start(f32[8,8,128]{2,1,0:T(8,128)S(1)} %all_to_all.10), channel_id=1, source_target_pairs={{0,128},{64,192},{128,0},{192,64},{1,129},{65,193},{129,1},{193,65... | collective-permute-start | bytes 98312 | tf_op jit(solution)/shard_map/ppermute | solution.py:364
  22.0 4.1 %collective-permute-start.5 = (f32[8,8,128]{2,1,0:T(8,128)S(1)}, f32[8,8,128]{2,1,0:T(8,128)S(1)}, u32[]{:S(2)}, u32[]{:S(2)}) collective-permute-start(f32[8,8,128]{2,1,0:T(8,128)S(1)} %all_to_all.10), channel_id=1, source_target_pairs={{0,192},{64,0},{128,64},{192,128},{1,193},{65,1},{129,65},{193,129... | collective-permute-start | bytes 98312 | tf_op jit(solution)/shard_map/ppermute | solution.py:364
  26.2 5.2 %collective-permute-start.6 = (f32[4,8,8,128]{3,2,1,0:T(8,128)S(1)}, f32[4,8,8,128]{3,2,1,0:T(8,128)S(1)}, u32[]{:S(2)}, u32[]{:S(2)}) collective-permute-start(f32[4,8,8,128]{3,2,1,0:T(8,128)S(1)} %pad_maximum_fusion.5), channel_id=1, source_target_pairs={{0,16},{16,32},{32,48},{48,0},{1,17},{17,33},{33,49},{49,1},{2,18}... | collective-permute-start | bytes 393224 | tf_op jit(solution)/shard_map/ppermute | solution.py:364
  27.5 6.4 %collective-permute-start.7 = (f32[4,8,8,128]{3,2,1,0:T(8,128)S(1)}, f32[4,8,8,128]{3,2,1,0:T(8,128)S(1)}, u32[]{:S(2)}, u32[]{:S(2)}) collective-permute-start(f32[4,8,8,128]{3,2,1,0:T(8,128)S(1)} %pad_maximum_fusion.5), channel_id=1, source_target_pairs={{0,32},{16,48},{32,0},{48,16},{1,33},{17,49},{33,1},{49,17},{2,34}... | collective-permute-start | bytes 393224 | tf_op jit(solution)/shard_map/ppermute | solution.py:364
  30.2 3.8 %collective-permute-start.8 = (f32[4,8,8,128]{3,2,1,0:T(8,128)S(1)}, f32[4,8,8,128]{3,2,1,0:T(8,128)S(1)}, u32[]{:S(2)}, u32[]{:S(2)}) collective-permute-start(f32[4,8,8,128]{3,2,1,0:T(8,128)S(1)} %pad_maximum_fusion.5), channel_id=1, source_target_pairs={{0,48},{16,0},{32,16},{48,32},{1,49},{17,1},{33,17},{49,33},{2,50}... | collective-permute-start | bytes 393224 | tf_op jit(solution)/shard_map/ppermute | solution.py:364
  34.0 7.7 %copy-start.3 = (f32[4,4,8,8,128]{4,3,2,1,0:T(8,128)}, f32[4,4,8,8,128]{4,3,2,1,0:T(8,128)S(1)}, u32[]{:S(2)}) copy-start(f32[4,4,8,8,128]{4,3,2,1,0:T(8,128)S(1)} %pad_maximum_fusion.1.refs_0_.refs_1_) | copy-start | bytes 1572868
  34.0 7.7 %collective-permute-start.9 = (f32[4,4,8,8,128]{4,3,2,1,0:T(8,128)S(1)}, f32[4,4,8,8,128]{4,3,2,1,0:T(8,128)S(1)}, u32[]{:S(2)}, u32[]{:S(2)}) collective-permute-start(f32[4,4,8,8,128]{4,3,2,1,0:T(8,128)S(1)} %pad_maximum_fusion.1.refs_0_.refs_1_), channel_id=1, source_target_pairs={{0,8},{8,0},{1,9},{9,1},{2,10},{10,2},{3,11},{11,3},{4,12},{12,4},... | collective-permute-start | bytes 1572872 | tf_op jit(solution)/shard_map/ppermute | solution.py:364
  41.7 0.8 copy-start.6
  51.4 20.7 %all-to-all-start.1 = ((bf16[32,16,256]{2,1,0:T(8,128)(2,1)}), bf16[32,16,256]{2,1,0:T(8,128)(2,1)S(1)}, u32[]{:S(2)}, u32[]{:S(2)}) async-start(bf16[32,16,256]{2,1,0:T(8,128)(2,1)} %get-tuple-element.40), calls=%async_computation.1 | async-start | bytes 524288 | tf_op jit(solution)/shard_map/all_to_all | solution.py:392
  59.0 50.0 %copy-start = (s32[5]{0:T(128)S(1)}, s32[5]{0:T(128)}, u32[]{:S(2)}) copy-start(s32[5]{0:T(128)} %stack.77.pos) | copy-start | bytes 64
  59.0 50.0 %copy-start.1 = (f32[6]{0:T(128)S(1)}, f32[6]{0:T(128)}, u32[]{:S(2)}) copy-start(f32[6]{0:T(128)} %omega.1) | copy-start | bytes 76
  69.9 3.6 %collective-permute-start.11 = (bf16[4,16,640]{2,1,0:T(8,128)(2,1)S(1)}, bf16[4,16,640]{2,1,0:T(8,128)(2,1)S(1)}, u32[]{:S(2)}, u32[]{:S(2)}) collective-permute-start(bf16[4,16,640]{2,1,0:T(8,128)(2,1)S(1)} %slice_bitcast_fusion), channel_id=1, source_target_pairs={{0,4},{4,0},{1,5},{5,1},{2,6},{6,2},{3,7},{7,3},{8,12},{12,8},{9,1... | collective-permute-start | bytes 245768 | tf_op jit(solution)/shard_map/ppermute | solution.py:364
  72.1 8.1 %collective-permute-start.10 = (bf16[32,16,256]{2,1,0:T(8,128)(2,1)S(1)}, bf16[32,16,256]{2,1,0:T(8,128)(2,1)S(1)}, u32[]{:S(2)}, u32[]{:S(2)}) collective-permute-start(bf16[32,16,256]{2,1,0:T(8,128)(2,1)S(1)} %all-to-all-done.1), channel_id=1, source_target_pairs={{0,4},{4,0},{1,5},{5,1},{2,6},{6,2},{3,7},{7,3},{8,12},{12,8},{9,1... | collective-permute-start | bytes 786440 | tf_op jit(solution)/shard_map/ppermute | solution.py:364
  80.2 28.8 %copy-start.2 = (bf16[2,4,4,2,16,256]{5,4,3,2,1,0:T(8,128)(2,1)}, bf16[2,4,4,2,16,256]{5,4,3,2,1,0:T(8,128)(2,1)S(1)}, u32[]{:S(2)}) copy-start(bf16[2,4,4,2,16,256]{5,4,3,2,1,0:T(8,128)(2,1)S(1)} %pad_maximum_fusion.2.r0) | copy-start | bytes 1572868
  80.2 15.2 %collective-permute-start.12 = (bf16[2,4,4,2,16,256]{5,4,3,2,1,0:T(8,128)(2,1)S(1)}, bf16[2,4,4,2,16,256]{5,4,3,2,1,0:T(8,128)(2,1)S(1)}, u32[]{:S(2)}, u32[]{:S(2)}) collective-permute-start(bf16[2,4,4,2,16,256]{5,4,3,2,1,0:T(8,128)(2,1)S(1)} %pad_maximum_fusion.2.r0), channel_id=1, source_target_pairs={{0,1},{1,2},{2,3},{3,0},{4,5},{5,6},{6,7},{7,4},{8,9},{9,10},{10,1... | collective-permute-start | bytes 1572872 | tf_op jit(solution)/shard_map/ppermute | solution.py:364
  80.6 14.8 %collective-permute-start.13 = (bf16[2,4,4,2,16,256]{5,4,3,2,1,0:T(8,128)(2,1)S(1)}, bf16[2,4,4,2,16,256]{5,4,3,2,1,0:T(8,128)(2,1)S(1)}, u32[]{:S(2)}, u32[]{:S(2)}) collective-permute-start(bf16[2,4,4,2,16,256]{5,4,3,2,1,0:T(8,128)(2,1)S(1)} %pad_maximum_fusion.2.r0), channel_id=1, source_target_pairs={{0,3},{1,0},{2,1},{3,2},{4,7},{5,4},{6,5},{7,6},{8,11},{9,8},{10,9... | collective-permute-start | bytes 1572872 | tf_op jit(solution)/shard_map/ppermute | solution.py:364
  83.0 11.0 %collective-permute-start.14 = (bf16[8,16,640]{2,1,0:T(8,128)(2,1)S(1)}, bf16[8,16,640]{2,1,0:T(8,128)(2,1)S(1)}, u32[]{:S(2)}, u32[]{:S(2)}) collective-permute-start(bf16[8,16,640]{2,1,0:T(8,128)(2,1)S(1)} %pad_maximum_fusion.4), channel_id=1, source_target_pairs={{0,64},{64,128},{128,192},{192,0},{1,65},{65,129},{129,193},{193,1... | collective-permute-start | bytes 491528 | tf_op jit(solution)/shard_map/ppermute | solution.py:364
  84.5 10.9 %collective-permute-start.15 = (bf16[8,16,640]{2,1,0:T(8,128)(2,1)S(1)}, bf16[8,16,640]{2,1,0:T(8,128)(2,1)S(1)}, u32[]{:S(2)}, u32[]{:S(2)}) collective-permute-start(bf16[8,16,640]{2,1,0:T(8,128)(2,1)S(1)} %pad_maximum_fusion.4), channel_id=1, source_target_pairs={{0,192},{64,0},{128,64},{192,128},{1,193},{65,1},{129,65},{193,129... | collective-permute-start | bytes 491528 | tf_op jit(solution)/shard_map/ppermute | solution.py:364
  95.4 13.6 %copy-start.4 = (bf16[2,4,4,2,16,256]{5,4,3,2,1,0:T(8,128)(2,1)}, bf16[2,4,4,2,16,256]{5,4,3,2,1,0:T(8,128)(2,1)S(1)}, u32[]{:S(2)}) copy-start(bf16[2,4,4,2,16,256]{5,4,3,2,1,0:T(8,128)(2,1)S(1)} %collective-permute-done.12.r1) | copy-start | bytes 1572868
  95.4 13.6 %copy-start.5 = (bf16[2,4,4,2,16,256]{5,4,3,2,1,0:T(8,128)(2,1)}, bf16[2,4,4,2,16,256]{5,4,3,2,1,0:T(8,128)(2,1)S(1)}, u32[]{:S(2)}) copy-start(bf16[2,4,4,2,16,256]{5,4,3,2,1,0:T(8,128)(2,1)S(1)} %collective-permute-done.13.r3) | copy-start | bytes 1572868
  95.4 9.8 %collective-permute-start.16 = (bf16[1,4,4,2,16,256]{5,4,3,2,1,0:T(8,128)(2,1)S(1)}, bf16[1,4,4,2,16,256]{5,4,3,2,1,0:T(8,128)(2,1)S(1)}, u32[]{:S(2)}, u32[]{:S(2)}) collective-permute-start(bf16[1,4,4,2,16,256]{5,4,3,2,1,0:T(8,128)(2,1)S(1)} %slice.26), channel_id=1, source_target_pairs={{0,3},{1,0},{2,1},{3,2},{4,7},{5,4},{6,5},{7,6},{8,11},{9,8},{10,9... | collective-permute-start | bytes 786440 | tf_op jit(solution)/shard_map/ppermute | solution.py:364
  96.8 8.4 %collective-permute-start.17 = (bf16[1,4,4,2,16,256]{5,4,3,2,1,0:T(8,128)(2,1)S(1)}, bf16[1,4,4,2,16,256]{5,4,3,2,1,0:T(8,128)(2,1)S(1)}, u32[]{:S(2)}, u32[]{:S(2)}) collective-permute-start(bf16[1,4,4,2,16,256]{5,4,3,2,1,0:T(8,128)(2,1)S(1)} %slice.27), channel_id=1, source_target_pairs={{0,1},{1,2},{2,3},{3,0},{4,5},{5,6},{6,7},{7,4},{8,9},{9,10},{10,1... | collective-permute-start | bytes 786440 | tf_op jit(solution)/shard_map/ppermute | solution.py:364
  97.1 4.7 %collective-permute-start.18 = (bf16[4,16,640]{2,1,0:T(8,128)(2,1)S(1)}, bf16[4,16,640]{2,1,0:T(8,128)(2,1)S(1)}, u32[]{:S(2)}, u32[]{:S(2)}) collective-permute-start(bf16[4,16,640]{2,1,0:T(8,128)(2,1)S(1)} %slice.28), channel_id=1, source_target_pairs={{0,192},{64,0},{128,64},{192,128},{1,193},{65,1},{129,65},{193,129... | collective-permute-start | bytes 245768 | tf_op jit(solution)/shard_map/ppermute | solution.py:364
  99.6 5.6 %collective-permute-start.19 = (bf16[4,16,640]{2,1,0:T(8,128)(2,1)S(1)}, bf16[4,16,640]{2,1,0:T(8,128)(2,1)S(1)}, u32[]{:S(2)}, u32[]{:S(2)}) collective-permute-start(bf16[4,16,640]{2,1,0:T(8,128)(2,1)S(1)} %slice.29), channel_id=1, source_target_pairs={{0,64},{64,128},{128,192},{192,0},{1,65},{65,129},{129,193},{193,1... | collective-permute-start | bytes 245768 | tf_op jit(solution)/shard_map/ppermute | solution.py:364
  105.4 13.6 %collective-permute-start.20 = (bf16[4,8,16,640]{3,2,1,0:T(8,128)(2,1)S(1)}, bf16[4,8,16,640]{3,2,1,0:T(8,128)(2,1)S(1)}, u32[]{:S(2)}, u32[]{:S(2)}) collective-permute-start(bf16[4,8,16,640]{3,2,1,0:T(8,128)(2,1)S(1)} %pad_maximum_fusion.mine), channel_id=1, source_target_pairs={{0,16},{16,32},{32,48},{48,0},{1,17},{17,33},{33,49},{49,1},{2,18}... | collective-permute-start | bytes 1966088 | tf_op jit(solution)/shard_map/ppermute | solution.py:364
  106.6 12.3 %collective-permute-start.21 = (bf16[4,8,16,640]{3,2,1,0:T(8,128)(2,1)S(1)}, bf16[4,8,16,640]{3,2,1,0:T(8,128)(2,1)S(1)}, u32[]{:S(2)}, u32[]{:S(2)}) collective-permute-start(bf16[4,8,16,640]{3,2,1,0:T(8,128)(2,1)S(1)} %pad_maximum_fusion.mine), channel_id=1, source_target_pairs={{0,48},{16,0},{32,16},{48,32},{1,49},{17,1},{33,17},{49,33},{2,50}... | collective-permute-start | bytes 1966088 | tf_op jit(solution)/shard_map/ppermute | solution.py:364
  114.3 12.5 %collective-permute-start.23 = (bf16[4,8,16,640]{3,2,1,0:T(8,128)(2,1)S(1)}, bf16[4,8,16,640]{3,2,1,0:T(8,128)(2,1)S(1)}, u32[]{:S(2)}, u32[]{:S(2)}) collective-permute-start(bf16[4,8,16,640]{3,2,1,0:T(8,128)(2,1)S(1)} %pad_maximum_fusion.mine), channel_id=1, source_target_pairs={{0,8},{8,0},{1,9},{9,1},{2,10},{10,2},{3,11},{11,3},{4,12},{12,4},... | collective-permute-start | bytes 1966088 | tf_op jit(solution)/shard_map/ppermute | solution.py:364
  118.9 13.3 %collective-permute-start.22 = (bf16[4,8,16,640]{3,2,1,0:T(8,128)(2,1)S(1)}, bf16[4,8,16,640]{3,2,1,0:T(8,128)(2,1)S(1)}, u32[]{:S(2)}, u32[]{:S(2)}) collective-permute-start(bf16[4,8,16,640]{3,2,1,0:T(8,128)(2,1)S(1)} %collective-permute-done.20.mine), channel_id=1, source_target_pairs={{0,8},{8,0},{1,9},{9,1},{2,10},{10,2},{3,11},{11,3},{4,12},{12,4},... | collective-permute-start | bytes 1966088 | tf_op jit(solution)/shard_map/ppermute | solution.py:364
  123.9 15.4 %collective-permute-start.27 = (bf16[4,8,16,640]{3,2,1,0:T(8,128)(2,1)S(1)}, bf16[4,8,16,640]{3,2,1,0:T(8,128)(2,1)S(1)}, u32[]{:S(2)}, u32[]{:S(2)}) collective-permute-start(bf16[4,8,16,640]{3,2,1,0:T(8,128)(2,1)S(1)} %collective-permute-done.21.mine), channel_id=1, source_target_pairs={{0,8},{8,0},{1,9},{9,1},{2,10},{10,2},{3,11},{11,3},{4,12},{12,4},... | collective-permute-start | bytes 1966088 | tf_op jit(solution)/shard_map/ppermute | solution.py:364
  124.0 14.1 %collective-permute-start.24 = (bf16[2,8,16,640]{3,2,1,0:T(8,128)(2,1)S(1)}, bf16[2,8,16,640]{3,2,1,0:T(8,128)(2,1)S(1)}, u32[]{:S(2)}, u32[]{:S(2)}) collective-permute-start(bf16[2,8,16,640]{3,2,1,0:T(8,128)(2,1)S(1)} %slice.30), channel_id=1, source_target_pairs={{0,48},{16,0},{32,16},{48,32},{1,49},{17,1},{33,17},{49,33},{2,50}... | collective-permute-start | bytes 983048 | tf_op jit(solution)/shard_map/ppermute | solution.py:364
  126.8 11.4 %collective-permute-start.25 = (bf16[2,8,16,640]{3,2,1,0:T(8,128)(2,1)S(1)}, bf16[2,8,16,640]{3,2,1,0:T(8,128)(2,1)S(1)}, u32[]{:S(2)}, u32[]{:S(2)}) collective-permute-start(bf16[2,8,16,640]{3,2,1,0:T(8,128)(2,1)S(1)} %slice.31), channel_id=1, source_target_pairs={{0,16},{16,32},{32,48},{48,0},{1,17},{17,33},{33,49},{49,1},{2,18}... | collective-permute-start | bytes 983048 | tf_op jit(solution)/shard_map/ppermute | solution.py:364
  138.2 7.0 %collective-permute-start.26 = (bf16[4,8,16,640]{3,2,1,0:T(8,128)(2,1)S(1)}, bf16[4,8,16,640]{3,2,1,0:T(8,128)(2,1)S(1)}, u32[]{:S(2)}, u32[]{:S(2)}) collective-permute-start(bf16[4,8,16,640]{3,2,1,0:T(8,128)(2,1)S(1)} %constant_dynamic-update-slice_fusion.mine), channel_id=1, source_target_pairs={{0,8},{8,0},{1,9},{9,1},{2,10},{10,2},{3,11},{11,3},{4,12},{12,4},... | collective-permute-start | bytes 1966088 | tf_op jit(solution)/shard_map/ppermute | solution.py:364

commit v5 on v2

--- a/solution.py
+++ b/solution.py
@@ -321,14 +321,15 @@
     )(pos, omega, *rows, gap, gmap, ident)
 
 
-def product_step(sy, mine, theirs, scaled, hot, sign, total, last):
+def product_step(sy, mine, theirs, scaled, hot, sign, total, last, which=None):
     def kernel(mine, theirs, scaled, hot, sign, *refs):
         out, cols = refs[-2:]
         add = None if total is None else refs[0]
 
         def quarter(n):
             for side, ref in enumerate((mine, theirs)):
-                full = dot(ref[...].reshape(512, CAN), hot[n]).reshape(32, 16, 256) * sign[n][None]
+                block = ref[which] if side == 1 and which is not None else ref[...]
+                full = dot(block.reshape(512, CAN), hot[n]).reshape(32, 16, 256) * sign[n][None]
                 cols[n, side * 512 : side * 512 + 512, :] = full.reshape(512, 256).astype(BF)
             part = dot(scaled[sy], cols[n]).reshape(6, 256, 256)
             at = pl.ds(pl.multiple_of(n * 256, 256), 256)
@@ -407,12 +408,12 @@
     scaled, hot, sign, near_y = lax.optimization_barrier((scaled, hot, sign, near_y))
     far = opposite(*near_y, "y")
     total = product_step(0, cols, shifted(cols, "co", 1), scaled, hot, sign, None, False)
-    total = product_step(1, near_y[0], shifted(near_y[0], "co", 1), scaled, hot, sign, total, False)
+    both = shifted(jnp.stack(near_y), "co", 1)
+    total = product_step(1, near_y[0], both, scaled, hot, sign, total, False, 0)
     total, far = lax.optimization_barrier((total, far))
-    for sy, mine in ((3, near_y[1]), (2, jnp.concatenate(far))):
-        theirs = shifted(mine, "co", 1)
-        total = product_step(sy, mine, theirs, scaled, hot, sign, total, sy == 2)
-    return total
+    total = product_step(3, near_y[1], both, scaled, hot, sign, total, False, 1)
+    far = jnp.concatenate(far)
+    return product_step(2, far, shifted(far, "co", 1), scaled, hot, sign, total, True)
 
 
 def solution(mesh):

time: 153 us -> 153 us (level)
  waiting for transfers between devices: 27.8 us -> 33.3 us
  starting transfers between devices: 61.4 us -> 56.7 us
    ppermute x28 -> x27, waiting for transfers between devices: 25.7 us -> 31.1 us  [shifted(): lax.ppermute(value, axis, [(i, (i + shift) % size) for i in range(size)])]
    ppermute x28 -> x27, starting transfers between devices: 53.9 us -> 49.1 us  [shifted(): lax.ppermute(value, axis, [(i, (i + shift) % size) for i in range(size)])]
  transfers between devices with their start and end apart: 29 -> 28, of which waited for: 13 -> 14; matrix products, arithmetic and copies ran while one was open for 4% -> 4% of each run, Pallas kernels for 21% -> 21%
where the time goes in v5:
time: 153 us
  starting transfers between devices  56.7 us (37%)
  Pallas kernels  48 us (31%)
  waiting for transfers between devices  33.3 us (22%)
  blocking collectives  7.84 us (5%)
  local copies, waits for them, and re-layouts  3.71 us (2%)
  other arithmetic  2.94 us (2%)
    ppermute x27, starting transfers between devices, shifted(): lax.ppermute(value, axis, [(i, (i + shift) % size) for i in range(size)])  49.1 us
    ppermute x27, waiting for transfers between devices, shifted(): lax.ppermute(value, axis, [(i, (i + shift) % size) for i in range(size)])  31.1 us
    pallas_call x4, Pallas kernels, product_step(): pl.pallas_call(kernel, grid=(4 if last else 1,), in_specs=[resident()] *...  24.1 us
    pallas_call x2, Pallas kernels, transform_call(): pl.pallas_call(kernel, grid_spec=pltpu.PrefetchScalarGridSpec(num_scalar_...  18.7 us
    all_to_all x1, blocking collectives, body(): lax.all_to_all(jnp.broadcast_to(valence, (8, *valence.shape)), NARROW, 0,...  7.84 us
    all_to_all x1, starting transfers between devices, body(): rows = lax.all_to_all(rows, WIDE, 0, 0, tiled=True)  7.59 us
    pallas_call x1, Pallas kernels, prepare(): pl.pallas_call(prepare_kernel, grid_spec=pltpu.PrefetchScalarGridSpec(num...  5.22 us
  transfers between devices with their start and end apart: 28, of which 14 were waited for; matrix products, arithmetic and copies ran while one was open for 4% of the time, Pallas kernels for 21%

profile of v5, /device:TPU:1, one launch (start us, length us, event | category | flops | bytes accessed | tf_op | source)
XLA Modules:
  0.0 152.8 jit_solution(11610394405951704225)
XLA Ops:
  0.0 2.0 %collective-permute-start = (f32[256,128]{1,0:T(8,128)}, f32[256,128]{1,0:T(8,128)S(1)}, u32[]{:S(2)}, u32[]{:S(2)}) collective-permute-start(f32[256,128]{1,0:T(8,128)} %bitcast.49), channel_id=1, source_target_pairs={{0,1},{1,2},{2,3},{3,0},{4,5},{5,6},{6,7},{7,4},{8,9},{9,10},{10,1... | collective-permute-start | bytes 393224 | tf_op jit(solution)/shard_map/ppermute | solution.py:365
  2.0 2.5 %collective-permute-start.1 = (f32[256,128]{1,0:T(8,128)}, f32[256,128]{1,0:T(8,128)S(1)}, u32[]{:S(2)}, u32[]{:S(2)}) collective-permute-start(f32[256,128]{1,0:T(8,128)} %bitcast.50), channel_id=1, source_target_pairs={{0,2},{1,3},{2,0},{3,1},{4,6},{5,7},{6,4},{7,5},{8,10},{9,11},{10,... | collective-permute-start | bytes 393224 | tf_op jit(solution)/shard_map/ppermute | solution.py:365
  4.5 1.2 collective-permute-start.2
  5.6 0.7 broadcast_in_dim.4
  6.3 7.8 %all_to_all.10 = f32[8,8,128]{2,1,0:T(8,128)S(1)} all-to-all(f32[8,8,128]{2,1,0:T(8,128)S(1)} %broadcast_in_dim.4), channel_id=1, replica_groups=mesh['zh'=4,'y'=4,'co'=2,'zl'=2,'x'=4] {'zl','x'}, dimensions={0} | all-to-all | bytes 65536 | tf_op jit(solution)/shard_map/all_to_all | solution.py:384
  14.2 3.1 %collective-permute-start.3 = (f32[8,8,128]{2,1,0:T(8,128)S(1)}, f32[8,8,128]{2,1,0:T(8,128)S(1)}, u32[]{:S(2)}, u32[]{:S(2)}) collective-permute-start(f32[8,8,128]{2,1,0:T(8,128)S(1)} %all_to_all.10), channel_id=1, source_target_pairs={{0,64},{64,128},{128,192},{192,0},{1,65},{65,129},{129,193},{193,1... | collective-permute-start | bytes 98312 | tf_op jit(solution)/shard_map/ppermute | solution.py:365
  17.3 4.7 %collective-permute-start.4 = (f32[8,8,128]{2,1,0:T(8,128)S(1)}, f32[8,8,128]{2,1,0:T(8,128)S(1)}, u32[]{:S(2)}, u32[]{:S(2)}) collective-permute-start(f32[8,8,128]{2,1,0:T(8,128)S(1)} %all_to_all.10), channel_id=1, source_target_pairs={{0,128},{64,192},{128,0},{192,64},{1,129},{65,193},{129,1},{193,65... | collective-permute-start | bytes 98312 | tf_op jit(solution)/shard_map/ppermute | solution.py:365
  22.0 2.4 %collective-permute-start.5 = (f32[8,8,128]{2,1,0:T(8,128)S(1)}, f32[8,8,128]{2,1,0:T(8,128)S(1)}, u32[]{:S(2)}, u32[]{:S(2)}) collective-permute-start(f32[8,8,128]{2,1,0:T(8,128)S(1)} %all_to_all.10), channel_id=1, source_target_pairs={{0,192},{64,0},{128,64},{192,128},{1,193},{65,1},{129,65},{193,129... | collective-permute-start | bytes 98312 | tf_op jit(solution)/shard_map/ppermute | solution.py:365
  24.4 0.8 broadcast_subtract_fusion
  25.7 0.4 collective-permute-done.5
  26.2 1.4 collective-permute-start.6
  27.5 2.6 %collective-permute-start.7 = (f32[4,8,8,128]{3,2,1,0:T(8,128)S(1)}, f32[4,8,8,128]{3,2,1,0:T(8,128)S(1)}, u32[]{:S(2)}, u32[]{:S(2)}) collective-permute-start(f32[4,8,8,128]{3,2,1,0:T(8,128)S(1)} %pad_maximum_fusion.6), channel_id=1, source_target_pairs={{0,32},{16,48},{32,0},{48,16},{1,33},{17,49},{33,1},{49,17},{2,34}... | collective-permute-start | bytes 393224 | tf_op jit(solution)/shard_map/ppermute | solution.py:365
  30.2 1.1 collective-permute-start.8
  31.3 2.6 %collective-permute-done.7 = f32[4,8,8,128]{3,2,1,0:T(8,128)S(1)} collective-permute-done((f32[4,8,8,128]{3,2,1,0:T(8,128)S(1)}, f32[4,8,8,128]{3,2,1,0:T(8,128)S(1)}, u32[]{:S(2)}, u32[]{:S(2)}) %collective-permute-start.7) | collective-permute-done | bytes 131104 | tf_op jit(solution)/shard_map/ppermute | solution.py:365
  34.0 6.2 %collective-permute-start.9 = (f32[4,4,8,8,128]{4,3,2,1,0:T(8,128)S(1)}, f32[4,4,8,8,128]{4,3,2,1,0:T(8,128)S(1)}, u32[]{:S(2)}, u32[]{:S(2)}) collective-permute-start(f32[4,4,8,8,128]{4,3,2,1,0:T(8,128)S(1)} %pad_maximum_fusion.2.refs_0_.refs_1_), channel_id=1, source_target_pairs={{0,8},{8,0},{1,9},{9,1},{2,10},{10,2},{3,11},{11,3},{4,12},{12,4},... | collective-permute-start | bytes 1572872 | tf_op jit(solution)/shard_map/ppermute | solution.py:365
  40.2 0.7 stack.86.pos
  40.9 0.9 collective-permute-done.9.refs_1_.refs_2_
  41.7 0.8 copy-done.6
  42.5 8.8 %row_pairs.1 = (bf16[32,16,256]{2,1,0:T(8,128)(2,1)}, bf16[416,256]{1,0:T(8,128)(2,1)}) custom-call(s32[5]{0:T(128)} %stack.86.pos, f32[4,4,8,8,128]{4,3,2,1,0:T(8,128)} %copy-done.3, f32[4,4,8,8,128]{4,3,2,1,0:T(8,128)} %copy-done.6, f32[256,128]{1,0:T(8,128)} %bitcast.52, bf16[1024,512]{1,0:T(8,128)(2,1)} %constant.38.clone.refs_3_.refs_6_, ...), custom_call_target="tpu_custom_call" | custom-call | flops 4000000000 | bytes 6291456 | tf_op jit(solution)/shard_map/row_pairs/pallas_call | solution.py:229
  51.4 7.6 %all-to-all-start.1 = ((bf16[32,16,256]{2,1,0:T(8,128)(2,1)}), bf16[32,16,256]{2,1,0:T(8,128)(2,1)S(1)}, u32[]{:S(2)}, u32[]{:S(2)}) async-start(bf16[32,16,256]{2,1,0:T(8,128)(2,1)} %get-tuple-element.38), calls=%async_computation.1 | async-start | bytes 524288 | tf_op jit(solution)/shard_map/all_to_all | solution.py:393
  59.0 9.8 %column_pairs.1 = bf16[2,4,16,640]{3,2,1,0:T(8,128)(2,1)} custom-call(s32[5]{0:T(128)} %stack.86.pos, bf16[416,256]{1,0:T(8,128)(2,1)} %get-tuple-element.39.refs_0_, f32[4,4,8,8,128]{4,3,2,1,0:T(8,128)} %copy-done.3, f32[4,4,8,8,128]{4,3,2,1,0:T(8,128)} %copy-done.6, f32[256,128]{1,0:T(8,128)} %copy-done.7, f32[256,128]{1,0:T(8,128)} %copy-done.8, ...), custom_call_target="tpu_custom_call" | custom-call | flops 8000000000 | bytes 6291456 | tf_op jit(solution)/shard_map/column_pairs/pallas_call | solution.py:229
  68.8 0.9 slice_bitcast_fusion
  69.9 2.2 %all-to-all-done.1 = bf16[32,16,256]{2,1,0:T(8,128)(2,1)S(1)} async-done(((bf16[32,16,256]{2,1,0:T(8,128)(2,1)}), bf16[32,16,256]{2,1,0:T(8,128)(2,1)S(1)}, u32[]{:S(2)}, u32[]{:S(2)}) %all-to-all-start.1) | async-done | bytes 262176 | tf_op jit(solution)/shard_map/all_to_all | solution.py:393
  72.1 1.2 collective-permute-done.11
  73.3 0.9 broadcast_select_fusion.1
  74.3 5.9 %collective-permute-done.10 = bf16[32,16,256]{2,1,0:T(8,128)(2,1)S(1)} collective-permute-done((bf16[32,16,256]{2,1,0:T(8,128)(2,1)S(1)}, bf16[32,16,256]{2,1,0:T(8,128)(2,1)S(1)}, u32[]{:S(2)}, u32[]{:S(2)}) %collective-permute-start.10) | collective-permute-done | bytes 262176 | tf_op jit(solution)/shard_map/ppermute | solution.py:365
  80.6 2.4 %collective-permute-start.13 = (bf16[2,4,4,2,16,256]{5,4,3,2,1,0:T(8,128)(2,1)S(1)}, bf16[2,4,4,2,16,256]{5,4,3,2,1,0:T(8,128)(2,1)S(1)}, u32[]{:S(2)}, u32[]{:S(2)}) collective-permute-start(bf16[2,4,4,2,16,256]{5,4,3,2,1,0:T(8,128)(2,1)S(1)} %pad_maximum_fusion.3.r0), channel_id=1, source_target_pairs={{0,3},{1,0},{2,1},{3,2},{4,7},{5,4},{6,5},{7,6},{8,11},{9,8},{10,9... | collective-permute-start | bytes 1572872 | tf_op jit(solution)/shard_map/ppermute | solution.py:365
  83.0 1.3 collective-permute-start.14
  84.2 2.3 %collective-permute-start.15 = (bf16[8,16,640]{2,1,0:T(8,128)(2,1)S(1)}, bf16[8,16,640]{2,1,0:T(8,128)(2,1)S(1)}, u32[]{:S(2)}, u32[]{:S(2)}) collective-permute-start(bf16[8,16,640]{2,1,0:T(8,128)(2,1)S(1)} %pad_maximum_fusion.5), channel_id=1, source_target_pairs={{0,192},{64,0},{128,64},{192,128},{1,193},{65,1},{129,65},{193,129... | collective-permute-start | bytes 491528 | tf_op jit(solution)/shard_map/ppermute | solution.py:365
  86.6 7.4 %collective-permute-done.14 = bf16[8,16,640]{2,1,0:T(8,128)(2,1)S(1)} collective-permute-done((bf16[8,16,640]{2,1,0:T(8,128)(2,1)S(1)}, bf16[8,16,640]{2,1,0:T(8,128)(2,1)S(1)}, u32[]{:S(2)}, u32[]{:S(2)}) %collective-permute-start.14) | collective-permute-done | bytes 163872 | tf_op jit(solution)/shard_map/ppermute | solution.py:365
  94.0 1.2 collective-permute-done.15
  95.3 1.5 collective-permute-start.16
  96.9 2.8 %collective-permute-start.18 = (bf16[4,16,640]{2,1,0:T(8,128)(2,1)S(1)}, bf16[4,16,640]{2,1,0:T(8,128)(2,1)S(1)}, u32[]{:S(2)}, u32[]{:S(2)}) collective-permute-start(bf16[4,16,640]{2,1,0:T(8,128)(2,1)S(1)} %slice.28), channel_id=1, source_target_pairs={{0,192},{64,0},{128,64},{192,128},{1,193},{65,1},{129,65},{193,129... | collective-permute-start | bytes 245768 | tf_op jit(solution)/shard_map/ppermute | solution.py:365
  99.9 2.1 %collective-permute-done.18 = bf16[4,16,640]{2,1,0:T(8,128)(2,1)S(1)} collective-permute-done((bf16[4,16,640]{2,1,0:T(8,128)(2,1)S(1)}, bf16[4,16,640]{2,1,0:T(8,128)(2,1)S(1)}, u32[]{:S(2)}, u32[]{:S(2)}) %collective-permute-start.18) | collective-permute-done | bytes 81952 | tf_op jit(solution)/shard_map/ppermute | solution.py:365
  102.0 3.4 %collective-permute-done.19 = bf16[4,16,640]{2,1,0:T(8,128)(2,1)S(1)} collective-permute-done((bf16[4,16,640]{2,1,0:T(8,128)(2,1)S(1)}, bf16[4,16,640]{2,1,0:T(8,128)(2,1)S(1)}, u32[]{:S(2)}, u32[]{:S(2)}) %collective-permute-start.19) | collective-permute-done | bytes 81952 | tf_op jit(solution)/shard_map/ppermute | solution.py:365
  105.6 1.0 collective-permute-start.20
  106.5 1.8 %collective-permute-start.21 = (bf16[4,8,16,640]{3,2,1,0:T(8,128)(2,1)S(1)}, bf16[4,8,16,640]{3,2,1,0:T(8,128)(2,1)S(1)}, u32[]{:S(2)}, u32[]{:S(2)}) collective-permute-start(bf16[4,8,16,640]{3,2,1,0:T(8,128)(2,1)S(1)} %pad_maximum_fusion.1.mine), channel_id=1, source_target_pairs={{0,48},{16,0},{32,16},{48,32},{1,49},{17,1},{33,17},{49,33},{2,50}... | collective-permute-start | bytes 1966088 | tf_op jit(solution)/shard_map/ppermute | solution.py:365
  108.3 0.9 pad_maximum_fusion.4.r2
  109.2 5.2 %scaled_rows.1 = (bf16[4,1536,1024]{2,1,0:T(8,128)(2,1)S(1)}, bf16[4,640,256]{2,1,0:T(8,128)(2,1)S(1)}, f32[4,16,256]{2,1,0:T(8,128)S(1)}) custom-call(s32[5]{0:T(128)S(1)} %copy-done, f32[6]{0:T(128)S(1)} %copy-done.1, bf16[2,4,4,2,16,256]{5,4,3,2,1,0:T(8,128)(2,1)} %copy-done.2, bf16[2,4,4,2,16,256]{5,4,3,2,1,0:T(8,128)(2,1)} %copy-done.4, ...), custom_call_target="tpu_custom_call" | custom-call | flops 1000000000 | bytes 20971520 | tf_op jit(solution)/shard_map/scaled_rows/pallas_call | solution.py:303
  114.4 5.0 %collective-permute-done.20.mine = bf16[4,8,16,640]{3,2,1,0:T(8,128)(2,1)S(1)} collective-permute-done((bf16[4,8,16,640]{3,2,1,0:T(8,128)(2,1)S(1)}, bf16[4,8,16,640]{3,2,1,0:T(8,128)(2,1)S(1)}, u32[]{:S(2)}, u32[]{:S(2)}) %collective-permute-start.20) | collective-permute-done | bytes 655392 | tf_op jit(solution)/shard_map/ppermute | solution.py:365
  119.6 4.7 %collective-permute-start.22 = (bf16[2,4,8,16,640]{4,3,2,1,0:T(8,128)(2,1)S(1)}, bf16[2,4,8,16,640]{4,3,2,1,0:T(8,128)(2,1)S(1)}, u32[]{:S(2)}, u32[]{:S(2)}) collective-permute-start(bf16[2,4,8,16,640]{4,3,2,1,0:T(8,128)(2,1)S(1)} %pad_maximum_fusion), channel_id=1, source_target_pairs={{0,8},{8,0},{1,9},{9,1},{2,10},{10,2},{3,11},{11,3},{4,12},{12,4},... | collective-permute-start | bytes 3932168 | tf_op jit(solution)/shard_map/ppermute | solution.py:365
  124.4 2.8 %collective-permute-start.24 = (bf16[2,8,16,640]{3,2,1,0:T(8,128)(2,1)S(1)}, bf16[2,8,16,640]{3,2,1,0:T(8,128)(2,1)S(1)}, u32[]{:S(2)}, u32[]{:S(2)}) collective-permute-start(bf16[2,8,16,640]{3,2,1,0:T(8,128)(2,1)S(1)} %slice.30), channel_id=1, source_target_pairs={{0,48},{16,0},{32,16},{48,32},{1,49},{17,1},{33,17},{49,33},{2,50}... | collective-permute-start | bytes 983048 | tf_op jit(solution)/shard_map/ppermute | solution.py:365
  127.2 0.7 collective-permute-done.23.theirs
  127.8 5.3 %response_product.4.refs_0_ = f32[6,256,1024]{2,1,0:T(8,128)S(1)} custom-call(bf16[4,8,16,640]{3,2,1,0:T(8,128)(2,1)S(1)} %pad_maximum_fusion.1.mine, bf16[4,8,16,640]{3,2,1,0:T(8,128)(2,1)S(1)} %collective-permute-done.23.theirs, bf16[4,1536,1024]{2,1,0:T(8,128)(2,1)S(1)} %get-tuple-element.59.scaled, bf16[4,640,256]{2,1,0:T(8,128)(2,1)S(1)} %get-tuple-element.60.hot, ...), custom_call_target="tpu_custom_call" | custom-call | flops 4600000000 | bytes 10485760 | tf_op jit(solution)/shard_map/response_product/pallas_call | solution.py:349
  133.2 5.8 %response_product.5.refs_0_ = f32[6,256,1024]{2,1,0:T(8,128)S(1)} custom-call(bf16[4,8,16,640]{3,2,1,0:T(8,128)(2,1)S(1)} %collective-permute-done.20.mine, bf16[2,4,8,16,640]{4,3,2,1,0:T(8,128)(2,1)S(1)} %collective-permute-done.22.theirs, bf16[4,1536,1024]{2,1,0:T(8,128)(2,1)S(1)} %get-tuple-element.59.scaled, ...), custom_call_target="tpu_custom_call", output_to_operand_aliasing={{}: (5, {})} | custom-call | flops 4600000000 | bytes 10485760 | tf_op jit(solution)/shard_map/response_product/pallas_call | solution.py:349
  139.1 0.7 collective-permute-start.26
  139.8 5.8 %response_product.6.refs_0_ = f32[6,256,1024]{2,1,0:T(8,128)S(1)} custom-call(bf16[4,8,16,640]{3,2,1,0:T(8,128)(2,1)S(1)} %collective-permute-done.21.mine, bf16[2,4,8,16,640]{4,3,2,1,0:T(8,128)(2,1)S(1)} %collective-permute-done.22.theirs, bf16[4,1536,1024]{2,1,0:T(8,128)(2,1)S(1)} %get-tuple-element.59.scaled, ...), custom_call_target="tpu_custom_call", output_to_operand_aliasing={{}: (5, {})} | custom-call | flops 4600000000 | bytes 10485760 | tf_op jit(solution)/shard_map/response_product/pallas_call | solution.py:349
  145.7 7.2 %response_product.7 = f32[6,256,1024]{2,1,0:T(8,128)} custom-call(bf16[4,8,16,640]{3,2,1,0:T(8,128)(2,1)S(1)} %constant_dynamic-update-slice_fusion.mine, bf16[4,8,16,640]{3,2,1,0:T(8,128)(2,1)S(1)} %collective-permute-done.26.theirs, bf16[4,1536,1024]{2,1,0:T(8,128)(2,1)S(1)} %get-tuple-element.59.scaled, bf16[4,640,256]{2,1,0:T(8,128)(2,1)S(1)} %get-tuple-element.60.hot, ...), custom_call_target="tpu_custom_call" | custom-call | flops 4600000000 | bytes 10485760 | tf_op jit(solution)/shard_map/response_product/pallas_call | solution.py:349
  (59 shorter events, 2.1 us)
Async XLA Ops:
  0.0 14.2 %collective-permute-start = (f32[256,128]{1,0:T(8,128)}, f32[256,128]{1,0:T(8,128)S(1)}, u32[]{:S(2)}, u32[]{:S(2)}) collective-permute-start(f32[256,128]{1,0:T(8,128)} %bitcast.49), channel_id=1, source_target_pairs={{0,1},{1,2},{2,3},{3,0},{4,5},{5,6},{6,7},{7,4},{8,9},{9,10},{10,1... | collective-permute-start | bytes 393224 | tf_op jit(solution)/shard_map/ppermute | solution.py:365
  2.0 12.1 %collective-permute-start.1 = (f32[256,128]{1,0:T(8,128)}, f32[256,128]{1,0:T(8,128)S(1)}, u32[]{:S(2)}, u32[]{:S(2)}) collective-permute-start(f32[256,128]{1,0:T(8,128)} %bitcast.50), channel_id=1, source_target_pairs={{0,2},{1,3},{2,0},{3,1},{4,6},{5,7},{6,4},{7,5},{8,10},{9,11},{10,... | collective-permute-start | bytes 393224 | tf_op jit(solution)/shard_map/ppermute | solution.py:365
  4.5 9.7 %collective-permute-start.2 = (f32[256,128]{1,0:T(8,128)}, f32[256,128]{1,0:T(8,128)S(1)}, u32[]{:S(2)}, u32[]{:S(2)}) collective-permute-start(f32[256,128]{1,0:T(8,128)} %bitcast.51), channel_id=1, source_target_pairs={{0,3},{1,0},{2,1},{3,2},{4,7},{5,4},{6,5},{7,6},{8,11},{9,8},{10,9... | collective-permute-start | bytes 393224 | tf_op jit(solution)/shard_map/ppermute | solution.py:365
  14.2 37.2 %copy-start.7 = (f32[256,128]{1,0:T(8,128)}, f32[256,128]{1,0:T(8,128)S(1)}, u32[]{:S(2)}) copy-start(f32[256,128]{1,0:T(8,128)S(1)} %collective-permute-done.refs_3_) | copy-start | bytes 393220
  14.2 37.2 %copy-start.8 = (f32[256,128]{1,0:T(8,128)}, f32[256,128]{1,0:T(8,128)S(1)}, u32[]{:S(2)}) copy-start(f32[256,128]{1,0:T(8,128)S(1)} %collective-permute-done.1.refs_4_) | copy-start | bytes 393220
  14.2 37.2 %copy-start.9 = (f32[256,128]{1,0:T(8,128)}, f32[256,128]{1,0:T(8,128)S(1)}, u32[]{:S(2)}) copy-start(f32[256,128]{1,0:T(8,128)S(1)} %collective-permute-done.2.refs_5_) | copy-start | bytes 393220
  14.2 11.5 %collective-permute-start.3 = (f32[8,8,128]{2,1,0:T(8,128)S(1)}, f32[8,8,128]{2,1,0:T(8,128)S(1)}, u32[]{:S(2)}, u32[]{:S(2)}) collective-permute-start(f32[8,8,128]{2,1,0:T(8,128)S(1)} %all_to_all.10), channel_id=1, source_target_pairs={{0,64},{64,128},{128,192},{192,0},{1,65},{65,129},{129,193},{193,1... | collective-permute-start | bytes 98312 | tf_op jit(solution)/shard_map/ppermute | solution.py:365
  17.3 8.4 %collective-permute-start.4 = (f32[8,8,128]{2,1,0:T(8,128)S(1)}, f32[8,8,128]{2,1,0:T(8,128)S(1)}, u32[]{:S(2)}, u32[]{:S(2)}) collective-permute-start(f32[8,8,128]{2,1,0:T(8,128)S(1)} %all_to_all.10), channel_id=1, source_target_pairs={{0,128},{64,192},{128,0},{192,64},{1,129},{65,193},{129,1},{193,65... | collective-permute-start | bytes 98312 | tf_op jit(solution)/shard_map/ppermute | solution.py:365
  22.0 4.1 %collective-permute-start.5 = (f32[8,8,128]{2,1,0:T(8,128)S(1)}, f32[8,8,128]{2,1,0:T(8,128)S(1)}, u32[]{:S(2)}, u32[]{:S(2)}) collective-permute-start(f32[8,8,128]{2,1,0:T(8,128)S(1)} %all_to_all.10), channel_id=1, source_target_pairs={{0,192},{64,0},{128,64},{192,128},{1,193},{65,1},{129,65},{193,129... | collective-permute-start | bytes 98312 | tf_op jit(solution)/shard_map/ppermute | solution.py:365
  26.2 5.2 %collective-permute-start.6 = (f32[4,8,8,128]{3,2,1,0:T(8,128)S(1)}, f32[4,8,8,128]{3,2,1,0:T(8,128)S(1)}, u32[]{:S(2)}, u32[]{:S(2)}) collective-permute-start(f32[4,8,8,128]{3,2,1,0:T(8,128)S(1)} %pad_maximum_fusion.6), channel_id=1, source_target_pairs={{0,16},{16,32},{32,48},{48,0},{1,17},{17,33},{33,49},{49,1},{2,18}... | collective-permute-start | bytes 393224 | tf_op jit(solution)/shard_map/ppermute | solution.py:365
  27.5 6.4 %collective-permute-start.7 = (f32[4,8,8,128]{3,2,1,0:T(8,128)S(1)}, f32[4,8,8,128]{3,2,1,0:T(8,128)S(1)}, u32[]{:S(2)}, u32[]{:S(2)}) collective-permute-start(f32[4,8,8,128]{3,2,1,0:T(8,128)S(1)} %pad_maximum_fusion.6), channel_id=1, source_target_pairs={{0,32},{16,48},{32,0},{48,16},{1,33},{17,49},{33,1},{49,17},{2,34}... | collective-permute-start | bytes 393224 | tf_op jit(solution)/shard_map/ppermute | solution.py:365
  30.2 3.8 %collective-permute-start.8 = (f32[4,8,8,128]{3,2,1,0:T(8,128)S(1)}, f32[4,8,8,128]{3,2,1,0:T(8,128)S(1)}, u32[]{:S(2)}, u32[]{:S(2)}) collective-permute-start(f32[4,8,8,128]{3,2,1,0:T(8,128)S(1)} %pad_maximum_fusion.6), channel_id=1, source_target_pairs={{0,48},{16,0},{32,16},{48,32},{1,49},{17,1},{33,17},{49,33},{2,50}... | collective-permute-start | bytes 393224 | tf_op jit(solution)/shard_map/ppermute | solution.py:365
  34.0 7.7 %copy-start.3 = (f32[4,4,8,8,128]{4,3,2,1,0:T(8,128)}, f32[4,4,8,8,128]{4,3,2,1,0:T(8,128)S(1)}, u32[]{:S(2)}) copy-start(f32[4,4,8,8,128]{4,3,2,1,0:T(8,128)S(1)} %pad_maximum_fusion.2.refs_0_.refs_1_) | copy-start | bytes 1572868
  34.0 7.7 %collective-permute-start.9 = (f32[4,4,8,8,128]{4,3,2,1,0:T(8,128)S(1)}, f32[4,4,8,8,128]{4,3,2,1,0:T(8,128)S(1)}, u32[]{:S(2)}, u32[]{:S(2)}) collective-permute-start(f32[4,4,8,8,128]{4,3,2,1,0:T(8,128)S(1)} %pad_maximum_fusion.2.refs_0_.refs_1_), channel_id=1, source_target_pairs={{0,8},{8,0},{1,9},{9,1},{2,10},{10,2},{3,11},{11,3},{4,12},{12,4},... | collective-permute-start | bytes 1572872 | tf_op jit(solution)/shard_map/ppermute | solution.py:365
  41.7 0.8 copy-start.6
  51.4 20.7 %all-to-all-start.1 = ((bf16[32,16,256]{2,1,0:T(8,128)(2,1)}), bf16[32,16,256]{2,1,0:T(8,128)(2,1)S(1)}, u32[]{:S(2)}, u32[]{:S(2)}) async-start(bf16[32,16,256]{2,1,0:T(8,128)(2,1)} %get-tuple-element.38), calls=%async_computation.1 | async-start | bytes 524288 | tf_op jit(solution)/shard_map/all_to_all | solution.py:393
  69.7 3.6 %collective-permute-start.11 = (bf16[4,16,640]{2,1,0:T(8,128)(2,1)S(1)}, bf16[4,16,640]{2,1,0:T(8,128)(2,1)S(1)}, u32[]{:S(2)}, u32[]{:S(2)}) collective-permute-start(bf16[4,16,640]{2,1,0:T(8,128)(2,1)S(1)} %slice_bitcast_fusion), channel_id=1, source_target_pairs={{0,4},{4,0},{1,5},{5,1},{2,6},{6,2},{3,7},{7,3},{8,12},{12,8},{9,1... | collective-permute-start | bytes 245768 | tf_op jit(solution)/shard_map/ppermute | solution.py:365
  72.1 8.1 %collective-permute-start.10 = (bf16[32,16,256]{2,1,0:T(8,128)(2,1)S(1)}, bf16[32,16,256]{2,1,0:T(8,128)(2,1)S(1)}, u32[]{:S(2)}, u32[]{:S(2)}) collective-permute-start(bf16[32,16,256]{2,1,0:T(8,128)(2,1)S(1)} %all-to-all-done.1), channel_id=1, source_target_pairs={{0,4},{4,0},{1,5},{5,1},{2,6},{6,2},{3,7},{7,3},{8,12},{12,8},{9,1... | collective-permute-start | bytes 786440 | tf_op jit(solution)/shard_map/ppermute | solution.py:365
  80.2 25.3 %copy-start.2 = (bf16[2,4,4,2,16,256]{5,4,3,2,1,0:T(8,128)(2,1)}, bf16[2,4,4,2,16,256]{5,4,3,2,1,0:T(8,128)(2,1)S(1)}, u32[]{:S(2)}) copy-start(bf16[2,4,4,2,16,256]{5,4,3,2,1,0:T(8,128)(2,1)S(1)} %pad_maximum_fusion.3.r0) | copy-start | bytes 1572868
  80.2 15.0 %collective-permute-start.12 = (bf16[2,4,4,2,16,256]{5,4,3,2,1,0:T(8,128)(2,1)S(1)}, bf16[2,4,4,2,16,256]{5,4,3,2,1,0:T(8,128)(2,1)S(1)}, u32[]{:S(2)}, u32[]{:S(2)}) collective-permute-start(bf16[2,4,4,2,16,256]{5,4,3,2,1,0:T(8,128)(2,1)S(1)} %pad_maximum_fusion.3.r0), channel_id=1, source_target_pairs={{0,1},{1,2},{2,3},{3,0},{4,5},{5,6},{6,7},{7,4},{8,9},{9,10},{10,1... | collective-permute-start | bytes 1572872 | tf_op jit(solution)/shard_map/ppermute | solution.py:365
  80.6 14.7 %collective-permute-start.13 = (bf16[2,4,4,2,16,256]{5,4,3,2,1,0:T(8,128)(2,1)S(1)}, bf16[2,4,4,2,16,256]{5,4,3,2,1,0:T(8,128)(2,1)S(1)}, u32[]{:S(2)}, u32[]{:S(2)}) collective-permute-start(bf16[2,4,4,2,16,256]{5,4,3,2,1,0:T(8,128)(2,1)S(1)} %pad_maximum_fusion.3.r0), channel_id=1, source_target_pairs={{0,3},{1,0},{2,1},{3,2},{4,7},{5,4},{6,5},{7,6},{8,11},{9,8},{10,9... | collective-permute-start | bytes 1572872 | tf_op jit(solution)/shard_map/ppermute | solution.py:365
  83.0 11.0 %collective-permute-start.14 = (bf16[8,16,640]{2,1,0:T(8,128)(2,1)S(1)}, bf16[8,16,640]{2,1,0:T(8,128)(2,1)S(1)}, u32[]{:S(2)}, u32[]{:S(2)}) collective-permute-start(bf16[8,16,640]{2,1,0:T(8,128)(2,1)S(1)} %pad_maximum_fusion.5), channel_id=1, source_target_pairs={{0,64},{64,128},{128,192},{192,0},{1,65},{65,129},{129,193},{193,1... | collective-permute-start | bytes 491528 | tf_op jit(solution)/shard_map/ppermute | solution.py:365
  84.2 11.0 %collective-permute-start.15 = (bf16[8,16,640]{2,1,0:T(8,128)(2,1)S(1)}, bf16[8,16,640]{2,1,0:T(8,128)(2,1)S(1)}, u32[]{:S(2)}, u32[]{:S(2)}) collective-permute-start(bf16[8,16,640]{2,1,0:T(8,128)(2,1)S(1)} %pad_maximum_fusion.5), channel_id=1, source_target_pairs={{0,192},{64,0},{128,64},{192,128},{1,193},{65,1},{129,65},{193,129... | collective-permute-start | bytes 491528 | tf_op jit(solution)/shard_map/ppermute | solution.py:365
  95.2 10.3 %copy-start.4 = (bf16[2,4,4,2,16,256]{5,4,3,2,1,0:T(8,128)(2,1)}, bf16[2,4,4,2,16,256]{5,4,3,2,1,0:T(8,128)(2,1)S(1)}, u32[]{:S(2)}) copy-start(bf16[2,4,4,2,16,256]{5,4,3,2,1,0:T(8,128)(2,1)S(1)} %collective-permute-done.12.r1) | copy-start | bytes 1572868
  95.3 10.3 %copy-start.5 = (bf16[2,4,4,2,16,256]{5,4,3,2,1,0:T(8,128)(2,1)}, bf16[2,4,4,2,16,256]{5,4,3,2,1,0:T(8,128)(2,1)S(1)}, u32[]{:S(2)}) copy-start(bf16[2,4,4,2,16,256]{5,4,3,2,1,0:T(8,128)(2,1)S(1)} %collective-permute-done.13.r3) | copy-start | bytes 1572868
  95.3 10.1 %collective-permute-start.16 = (bf16[1,4,4,2,16,256]{5,4,3,2,1,0:T(8,128)(2,1)S(1)}, bf16[1,4,4,2,16,256]{5,4,3,2,1,0:T(8,128)(2,1)S(1)}, u32[]{:S(2)}, u32[]{:S(2)}) collective-permute-start(bf16[1,4,4,2,16,256]{5,4,3,2,1,0:T(8,128)(2,1)S(1)} %slice.26), channel_id=1, source_target_pairs={{0,3},{1,0},{2,1},{3,2},{4,7},{5,4},{6,5},{7,6},{8,11},{9,8},{10,9... | collective-permute-start | bytes 786440 | tf_op jit(solution)/shard_map/ppermute | solution.py:365
  96.8 8.6 %collective-permute-start.17 = (bf16[1,4,4,2,16,256]{5,4,3,2,1,0:T(8,128)(2,1)S(1)}, bf16[1,4,4,2,16,256]{5,4,3,2,1,0:T(8,128)(2,1)S(1)}, u32[]{:S(2)}, u32[]{:S(2)}) collective-permute-start(bf16[1,4,4,2,16,256]{5,4,3,2,1,0:T(8,128)(2,1)S(1)} %slice.27), channel_id=1, source_target_pairs={{0,1},{1,2},{2,3},{3,0},{4,5},{5,6},{6,7},{7,4},{8,9},{9,10},{10,1... | collective-permute-start | bytes 786440 | tf_op jit(solution)/shard_map/ppermute | solution.py:365
  96.9 5.0 %collective-permute-start.18 = (bf16[4,16,640]{2,1,0:T(8,128)(2,1)S(1)}, bf16[4,16,640]{2,1,0:T(8,128)(2,1)S(1)}, u32[]{:S(2)}, u32[]{:S(2)}) collective-permute-start(bf16[4,16,640]{2,1,0:T(8,128)(2,1)S(1)} %slice.28), channel_id=1, source_target_pairs={{0,192},{64,0},{128,64},{192,128},{1,193},{65,1},{129,65},{193,129... | collective-permute-start | bytes 245768 | tf_op jit(solution)/shard_map/ppermute | solution.py:365
  99.8 9.4 %copy-start = (s32[5]{0:T(128)S(1)}, s32[5]{0:T(128)}, u32[]{:S(2)}) copy-start(s32[5]{0:T(128)} %stack.86.pos) | copy-start | bytes 64
  99.8 9.4 %copy-start.1 = (f32[6]{0:T(128)S(1)}, f32[6]{0:T(128)}, u32[]{:S(2)}) copy-start(f32[6]{0:T(128)} %omega.1) | copy-start | bytes 76
  99.8 5.6 %collective-permute-start.19 = (bf16[4,16,640]{2,1,0:T(8,128)(2,1)S(1)}, bf16[4,16,640]{2,1,0:T(8,128)(2,1)S(1)}, u32[]{:S(2)}, u32[]{:S(2)}) collective-permute-start(bf16[4,16,640]{2,1,0:T(8,128)(2,1)S(1)} %slice.29), channel_id=1, source_target_pairs={{0,64},{64,128},{128,192},{192,0},{1,65},{65,129},{129,193},{193,1... | collective-permute-start | bytes 245768 | tf_op jit(solution)/shard_map/ppermute | solution.py:365
  105.6 13.9 %collective-permute-start.20 = (bf16[4,8,16,640]{3,2,1,0:T(8,128)(2,1)S(1)}, bf16[4,8,16,640]{3,2,1,0:T(8,128)(2,1)S(1)}, u32[]{:S(2)}, u32[]{:S(2)}) collective-permute-start(bf16[4,8,16,640]{3,2,1,0:T(8,128)(2,1)S(1)} %pad_maximum_fusion.1.mine), channel_id=1, source_target_pairs={{0,16},{16,32},{32,48},{48,0},{1,17},{17,33},{33,49},{49,1},{2,18}... | collective-permute-start | bytes 1966088 | tf_op jit(solution)/shard_map/ppermute | solution.py:365
  106.5 12.9 %collective-permute-start.21 = (bf16[4,8,16,640]{3,2,1,0:T(8,128)(2,1)S(1)}, bf16[4,8,16,640]{3,2,1,0:T(8,128)(2,1)S(1)}, u32[]{:S(2)}, u32[]{:S(2)}) collective-permute-start(bf16[4,8,16,640]{3,2,1,0:T(8,128)(2,1)S(1)} %pad_maximum_fusion.1.mine), channel_id=1, source_target_pairs={{0,48},{16,0},{32,16},{48,32},{1,49},{17,1},{33,17},{49,33},{2,50}... | collective-permute-start | bytes 1966088 | tf_op jit(solution)/shard_map/ppermute | solution.py:365
  119.6 13.6 %collective-permute-start.22 = (bf16[2,4,8,16,640]{4,3,2,1,0:T(8,128)(2,1)S(1)}, bf16[2,4,8,16,640]{4,3,2,1,0:T(8,128)(2,1)S(1)}, u32[]{:S(2)}, u32[]{:S(2)}) collective-permute-start(bf16[2,4,8,16,640]{4,3,2,1,0:T(8,128)(2,1)S(1)} %pad_maximum_fusion), channel_id=1, source_target_pairs={{0,8},{8,0},{1,9},{9,1},{2,10},{10,2},{3,11},{11,3},{4,12},{12,4},... | collective-permute-start | bytes 3932168 | tf_op jit(solution)/shard_map/ppermute | solution.py:365
  124.2 3.6 %collective-permute-start.23 = (bf16[4,8,16,640]{3,2,1,0:T(8,128)(2,1)S(1)}, bf16[4,8,16,640]{3,2,1,0:T(8,128)(2,1)S(1)}, u32[]{:S(2)}, u32[]{:S(2)}) collective-permute-start(bf16[4,8,16,640]{3,2,1,0:T(8,128)(2,1)S(1)} %pad_maximum_fusion.1.mine), channel_id=1, source_target_pairs={{0,8},{8,0},{1,9},{9,1},{2,10},{10,2},{3,11},{11,3},{4,12},{12,4},... | collective-permute-start | bytes 1966088 | tf_op jit(solution)/shard_map/ppermute | solution.py:365
  124.4 14.6 %collective-permute-start.24 = (bf16[2,8,16,640]{3,2,1,0:T(8,128)(2,1)S(1)}, bf16[2,8,16,640]{3,2,1,0:T(8,128)(2,1)S(1)}, u32[]{:S(2)}, u32[]{:S(2)}) collective-permute-start(bf16[2,8,16,640]{3,2,1,0:T(8,128)(2,1)S(1)} %slice.30), channel_id=1, source_target_pairs={{0,48},{16,0},{32,16},{48,32},{1,49},{17,1},{33,17},{49,33},{2,50}... | collective-permute-start | bytes 983048 | tf_op jit(solution)/shard_map/ppermute | solution.py:365
  127.2 11.9 %collective-permute-start.25 = (bf16[2,8,16,640]{3,2,1,0:T(8,128)(2,1)S(1)}, bf16[2,8,16,640]{3,2,1,0:T(8,128)(2,1)S(1)}, u32[]{:S(2)}, u32[]{:S(2)}) collective-permute-start(bf16[2,8,16,640]{3,2,1,0:T(8,128)(2,1)S(1)} %slice.31), channel_id=1, source_target_pairs={{0,16},{16,32},{32,48},{48,0},{1,17},{17,33},{33,49},{49,1},{2,18}... | collective-permute-start | bytes 983048 | tf_op jit(solution)/shard_map/ppermute | solution.py:365
  139.1 6.5 %collective-permute-start.26 = (bf16[4,8,16,640]{3,2,1,0:T(8,128)(2,1)S(1)}, bf16[4,8,16,640]{3,2,1,0:T(8,128)(2,1)S(1)}, u32[]{:S(2)}, u32[]{:S(2)}) collective-permute-start(bf16[4,8,16,640]{3,2,1,0:T(8,128)(2,1)S(1)} %constant_dynamic-update-slice_fusion.mine), channel_id=1, source_target_pairs={{0,8},{8,0},{1,9},{9,1},{2,10},{10,2},{3,11},{11,3},{4,12},{12,4},... | collective-permute-start | bytes 1966088 | tf_op jit(solution)/shard_map/ppermute | solution.py:365
